TPU v7x, 256 devices: a whole 4x4x8 slice. The times are simulated.
256 devices in a mesh: row: 8 (over z_hi, y), col: 32 (over z_lo, x, core).
Axes of the slice: x: 4, y: 4, z: 8 (z_hi: 2, z_lo: 4; z = z_hi * 4 + z_lo), core: 2. Of those that a mesh axis runs over, the one named last changes fastest.
Arguments:
- inputs: bfloat16 [1024, 9216], P('col', 'row'), may hold values from -6 to 6
- out_grad: bfloat16 [1024, 9216], P('col', 'row'), may hold values from -6 to 6
- preact: bfloat16 [1024, 36864], P('row', 'col'), may hold values from -6 to 6
- first_weight: bfloat16 [9216, 36864], P('row', 'col'), may hold values from -0.0625 to 0.0625
- second_weight: bfloat16 [36864, 9216], P('col', 'row'), may hold values from -0.03125 to 0.03125
Outputs:
- grad_inputs: float32 [1024, 9216], P('col', 'row')
- grad_first: bfloat16 [9216, 36864], P('row', 'col')
- grad_second: bfloat16 [36864, 9216], P('col', 'row')
All inputs are finite; a program needn't handle non-finite values.
Results may differ from a plain program's by a relative error of at most 0.005.
Values may be sent and summed in bfloat16 or wider, within the bound.
No kernel may reach another device: no remote copies, remote signals or barrier semaphores. Data moves between devices by JAX's collectives and lax.ppermute only.
A program may use at most 64 MiB of HBM per device.

v0:
```python
import math

import jax
import jax.numpy as jnp
from jax import lax
from jax.experimental import pallas as pl
from jax.experimental.pallas import tpu as pltpu
from jax.sharding import Mesh
from jax.sharding import PartitionSpec as P


INV_ROOT_TWO = 0.7071067811865476
INV_ROOT_TWO_PI = 0.3989422804014327
BF16 = jnp.bfloat16
F32 = jnp.float32


def gelu_value(values):
    return 0.5 * values * (1.0 + lax.erf(values * INV_ROOT_TWO))


def gelu_slope(values):
    normal_cdf = 0.5 * (1.0 + lax.erf(values * INV_ROOT_TWO))
    density = jnp.exp(-0.5 * values * values) * INV_ROOT_TWO_PI
    return normal_cdf + values * density


def shift(value, axis, step):
    size = lax.axis_size(axis)
    return lax.ppermute(value, axis, [(i, (i + step) % size) for i in range(size)])


def swap(value, axis):
    return lax.ppermute(value, axis, [(0, 1), (1, 0)])


VMEM = pl.BlockSpec(memory_space=pltpu.VMEM)
SMEM = pl.BlockSpec(memory_space=pltpu.SMEM)


def cost(flops, moved):
    return pl.CostEstimate(flops=flops, bytes_accessed=moved, transcendentals=0)


def call(kernel, outs, operands, scratch=(), where=None, flops=0, hbm_out=False):
    moved = sum(2 * o.size for o in operands)
    operands = [pltpu.with_memory_space_constraint(o, pltpu.VMEM) for o in operands]
    specs = [VMEM] * len(operands)
    if where is not None:
        operands, specs = [where] + operands, [SMEM] + specs
    space = pl.BlockSpec(memory_space=pl.ANY) if hbm_out else VMEM
    make = jax.ShapeDtypeStruct if hbm_out else pltpu.VMEM
    return pl.pallas_call(
        kernel,
        out_shape=tuple(make(shape, dtype) for shape, dtype in outs),
        in_specs=specs,
        out_specs=(space,) * len(outs),
        scratch_shapes=scratch,
        cost_estimate=cost(flops, moved),
        compiler_params=pltpu.CompilerParams(vmem_limit_bytes=GRANT),
    )(*operands)


GRANT = 12 * 1024 * 1024


def times(left, right):
    return lax.dot_general(left, right, (((1,), (1,)), ((), ())), preferred_element_type=F32)


def col_place_kernel(where, *refs):
    out = refs[-1]
    zh, y, zl, x = (where[i] for i in range(4))
    for kz in range(4):
        for kx in range(4):
            az = lax.rem(zl + 4 - kz, 4)
            ax = lax.rem(x + 4 - kx, 4)
            far = lax.rem(lax.div(az, 2) + zh, 2)
            ay = lax.rem(az, 2) * 2 + lax.div(ax, 2)
            out[far, lax.rem(ay + 4 - y, 4), lax.rem(ax, 2)] = refs[kx][kz]


def col_place(where, pieces):
    rows, width = pieces[0].shape[1:]
    return call(
        col_place_kernel, [((2, 4, 2, rows, width), BF16)], pieces, where=where
    )[0]


def shifts(value, axis):
    return [value] + [shift(value, axis, k) for k in (1, 2, 3)]


def spread(value):
    own, one, two, three = shifts(value, "y")
    return [own, three, two, one]


def col_gather(where, own):
    line = jnp.stack(shifts(own, "zl"))
    half = col_place(where, shifts(line, "x"))
    return half, swap(half, "c")


def own_act_kernel(half, weight, part, first):
    @pl.loop(0, 2)
    def _(far):
        rows = half[far].reshape(-1, half.shape[-1])
        got = times(rows, weight[...]).reshape(part.shape[1:])
        part[far] = got.astype(BF16)
        first[far] = got[0]


def own_act(half, weight):
    width = weight.shape[0]
    rows = half.shape[2] * half.shape[3]
    return call(
        own_act_kernel,
        [((2, 4, rows, width), BF16), ((2, rows, width), F32)],
        [half, weight],
        flops=2 * half.size * width,
    )


def other_act_kernel(far, half, weight, part, first, keep, one, two, three):
    rows = part.shape[2]
    got = times(half[far].reshape(-1, half.shape[-1]), weight[...])
    keep[:rows] = first[far]
    keep[rows:] = got[:rows]
    for k, send in ((1, one), (2, two), (3, three)):
        send[:rows] = part[far, k]
        send[rows:] = got[k * rows : (k + 1) * rows].astype(BF16)


def other_act(far, half, weight, part, first):
    width = weight.shape[0]
    rows = 2 * part.shape[2]
    return call(
        lambda *refs: other_act_kernel(far, *refs),
        [((rows, width), F32)] + [((rows, width), BF16)] * 3,
        [half, weight, part, first],
        flops=half.size * width,
    )


def token_kernel(where, p0, p1, p2, p3, weight, away, keep, rows):
    y, x = where[1], where[3]
    block = rows.shape[3]
    for j, piece in enumerate((p0, p1, p2, p3)):
        ay = lax.rem(y + j, 4)
        for low in range(2):
            ax = lax.rem(ay, 2) * 2 + low
            kx = lax.rem(ax + 4 - x, 4)
            for core in range(2):
                start = (core * 2 + low) * block
                rows[core, kx, lax.div(ay, 2)] = piece[start : start + block]

    @pl.loop(0, 2)
    def _(core):
        got = times(rows[core].reshape(-1, rows.shape[-1]), weight[...])

        @pl.when(core == 0)
        def _():
            keep[...] = got.reshape(keep.shape)

        @pl.when(core == 1)
        def _():
            away[...] = got.astype(BF16).reshape(away.shape)


def token_products(where, pieces, weight):
    token_rows, width = pieces[0].shape
    shape = (4, 2, token_rows // 4, weight.shape[0])
    return call(
        token_kernel,
        [(shape, BF16), (shape, F32)],
        [*pieces, weight],
        scratch=[pltpu.VMEM((2, 4, 2, token_rows // 4, width), BF16)],
        where=where,
        flops=8 * token_rows * width * width,
    )


def line_send_kernel(near, near_got, far, far_got, keep, one, two, three):
    for plane, (own, got) in enumerate(((near, near_got), (far, far_got))):
        for k, out in enumerate((keep, one, two, three)):
            out[plane] = (own[k] + got[k].astype(F32)).astype(out.dtype)


def line_sends(near, near_got, far, far_got):
    shape = (2, *near.shape[1:])
    return call(
        line_send_kernel,
        [(shape, F32)] + [(shape, BF16)] * 3,
        [near, near_got, far, far_got],
    )


def line_kernel(where, kept, one, two, three, *outs_sums):
    zh, zl = where[0], where[2]
    outs, sums = outs_sums[:4], outs_sums[4]
    sums[...] = (
        kept[...] + one[...].astype(F32) + two[...].astype(F32) + three[...].astype(F32)
    )
    for k, out in enumerate(outs):
        az = lax.rem(zl + k, 4)
        plane = lax.rem(lax.div(az, 2) + zh, 2)
        out[...] = sums[plane, lax.rem(az, 2)].astype(out.dtype)


def line_sums(where, lines):
    block, width = lines[0].shape[2:]
    return call(
        line_kernel,
        [((block, width), F32)] + [((block, width), BF16)] * 3,
        lines,
        scratch=[pltpu.VMEM((2, 2, block, width), F32)],
        where=where,
    )


CHUNK = 384


def outer(lefts, rights, out, stage, sem, factor):
    dims = (((0,), (0,)), ((), ()))

    def send(i):
        start = pl.multiple_of(i * CHUNK, CHUNK)
        return pltpu.make_async_copy(stage.at[i], out.at[pl.ds(start, CHUNK)], sem.at[i])

    @pl.loop(0, out.shape[0] // CHUNK)
    def _(i):
        columns = pl.ds(pl.multiple_of(i * CHUNK, CHUNK), CHUNK)
        total = sum(
            lax.dot_general(left(columns), right(), dims, preferred_element_type=F32)
            for left, right in zip(lefts, rights)
        )
        stage[i] = (total * factor).astype(BF16)
        send(i).start()

    for i in range(out.shape[0] // CHUNK):
        send(i).wait()


def second_kernel(factor, *refs):
    pieces, (own, other, out, act, stage, sem) = refs[:4], refs[4:]
    rows = pieces[0].shape[1] // 2
    width = own.shape[-1]
    for j, piece in enumerate(pieces):

        @pl.loop(0, 4)
        def _(i):
            far, core = lax.div(i, 2), lax.rem(i, 2)
            values = piece[far, pl.ds(core * rows, rows)].astype(F32)
            start = (core * 8 + far * 4 + j) * rows
            act[pl.ds(start, rows)] = gelu_value(values).astype(BF16)

    half = 8 * rows
    lefts = [lambda cols, n=n: act[n * half : (n + 1) * half, cols] for n in range(2)]
    rights = [lambda h=h: h[...].reshape(-1, width) for h in (own, other)]
    outer(lefts, rights, out, stage, sem, factor)


def first_kernel(factor, *refs):
    pieces, (own, other, out, right, stage, sem) = refs[:8], refs[8:]
    rows = pieces[0].shape[0] // 2
    half = 8 * rows
    for i, piece in enumerate(pieces):

        @pl.loop(0, 2)
        def _(core):
            right[pl.ds((core * 8 + i) * rows, rows)] = piece[pl.ds(core * rows, rows)]

    lefts = [
        lambda cols, h=h: h[:, :, :, :, cols].reshape(-1, CHUNK) for h in (own, other)
    ]
    rights = [lambda n=n: right[n * half : (n + 1) * half] for n in range(2)]
    outer(lefts, rights, out, stage, sem, factor)


def token_outer(kernel, pieces, halves, factor, swapped):
    width = pieces[0].shape[-1]
    tokens = sum(p.size for p in pieces) // width
    left, right = width, halves[0].shape[-1]
    if swapped:
        left, right = right, left
    return call(
        lambda *refs: kernel(factor, *refs),
        [((left, right), BF16)],
        [*pieces, *halves],
        scratch=[
            pltpu.VMEM((tokens, width), BF16),
            pltpu.VMEM((left // CHUNK, CHUNK, right), BF16),
            pltpu.SemaphoreType.DMA((left // CHUNK,)),
        ],
        flops=2 * tokens * left * right,
        hbm_out=True,
    )[0]


def compute(inputs, out_grad, preact, first_weight, second_weight):
    where = jnp.stack(
        [lax.axis_index(a) for a in ("zh", "y", "zl", "x", "c")]
    ).astype(jnp.int32)
    c = where[4]
    token_rows, width = preact.shape
    block = token_rows // 4
    factor = 1.0 / math.sqrt(8 * token_rows)

    split = preact.reshape(2, 2, block, width)
    preact = jnp.stack(
        [
            jnp.where(c == 0, split[:, 0], split[:, 1]),
            jnp.where(c == 0, split[:, 1], split[:, 0]),
        ]
    ).reshape(token_rows, width)

    grad_half, grad_other = col_gather(where, out_grad)
    pre_far = swap(preact, "zh")
    pre = spread(jnp.stack([preact, pre_far]))

    part, first = own_act(grad_half, second_weight)

    def plane_sum(far):
        keep, *sends = other_act(far, grad_other, second_weight, part, first)
        got = [shift(s, "y", k) for k, s in zip((1, 2, 3), sends)]
        return keep + sum(g.astype(F32) for g in got)

    far_sum = plane_sum(1).astype(BF16)
    near_sum = plane_sum(0)
    from_far = swap(far_sum, "zh")
    grad_act = near_sum + from_far.astype(F32)
    grad_own = (grad_act * gelu_slope(preact.astype(F32))).astype(BF16)

    near = spread(grad_own)
    own_far = swap(grad_own, "zh")
    far = spread(own_far)

    def plane_inputs(pieces):
        away, keep = token_products(where, pieces, first_weight)
        return keep, swap(away, "c")

    keep, *sends = line_sends(*plane_inputs(near), *plane_inputs(far))
    lines = [keep] + [shift(s, "x", k) for k, s in zip((1, 2, 3), sends)]
    grad_inputs, *sends = line_sums(where, lines)
    got = [shift(s, "zl", k) for k, s in zip((1, 2, 3), sends)]
    grad_inputs = grad_inputs + sum(g.astype(F32) for g in got)

    halves = col_gather(where, inputs)
    grad_first = token_outer(first_kernel, near + far, halves, factor, True)
    grad_second = token_outer(
        second_kernel, pre, (grad_half, grad_other), factor, False
    )
    return (grad_inputs, grad_first, grad_second)


def solution(mesh):
    fine = Mesh(mesh.devices.reshape(2, 4, 4, 4, 2), ("zh", "y", "zl", "x", "c"))
    row, col = ("zh", "y"), ("zl", "x", "c")
    return jax.shard_map(
        compute,
        mesh=fine,
        in_specs=(P(col, row), P(col, row), P(row, col), P(row, col), P(col, row)),
        out_specs=(P(col, row), P(row, col), P(col, row)),
        check_vma=False,
    )
```

profile of v0, /device:TPU:26, one launch (start us, length us, event | category | flops | bytes accessed | tf_op | source)
XLA Modules:
  0.0 181.9 jit_solution(733896560819488240)
XLA Ops:
  0.6 4.7 %collective-permute-start.2 = (bf16[32,1152]{1,0:T(8,128)(2,1)}, bf16[32,1152]{1,0:T(8,128)(2,1)S(1)}, u32[]{:S(2)}, u32[]{:S(2)}) collective-permute-start(bf16[32,1152]{1,0:T(8,128)(2,1)} %param.6), channel_id=1, source_target_pairs={{0,24},{8,0},{16,8},{24,16},{1,25},{9,1},{17,9},{25,17},{2,26},{10... | collective-permute-start | bytes 221192 | tf_op jit(solution)/shard_map/ppermute | solution.py:30
  6.0 2.3 %collective-permute-done.2 = bf16[32,1152]{1,0:T(8,128)(2,1)S(1)} collective-permute-done((bf16[32,1152]{1,0:T(8,128)(2,1)}, bf16[32,1152]{1,0:T(8,128)(2,1)S(1)}, u32[]{:S(2)}, u32[]{:S(2)}) %collective-permute-start.2) | collective-permute-done | bytes 73760 | tf_op jit(solution)/shard_map/ppermute | solution.py:30
  8.3 4.2 %collective-permute-done.1 = bf16[32,1152]{1,0:T(8,128)(2,1)S(1)} collective-permute-done((bf16[32,1152]{1,0:T(8,128)(2,1)}, bf16[32,1152]{1,0:T(8,128)(2,1)S(1)}, u32[]{:S(2)}, u32[]{:S(2)}) %collective-permute-start.1) | collective-permute-done | bytes 73760 | tf_op jit(solution)/shard_map/ppermute | solution.py:30
  16.3 2.2 %collective-permute-start.5 = (bf16[4,32,1152]{2,1,0:T(8,128)(2,1)S(1)}, bf16[4,32,1152]{2,1,0:T(8,128)(2,1)}, u32[]{:S(2)}, u32[]{:S(2)}) collective-permute-start(bf16[4,32,1152]{2,1,0:T(8,128)(2,1)S(1)} %pad_maximum_fusion.1.refs_0_), channel_id=1, source_target_pairs={{0,6},{2,0},{4,2},{6,4},{1,7},{3,1},{5,3},{7,5},{8,14},{10,8},{12,... | collective-permute-start | bytes 884744 | tf_op jit(solution)/shard_map/ppermute | solution.py:30
  18.5 5.0 %collective-permute-done.3.refs_1_ = bf16[4,32,1152]{2,1,0:T(8,128)(2,1)S(1)} collective-permute-done((bf16[4,32,1152]{2,1,0:T(8,128)(2,1)S(1)}, bf16[4,32,1152]{2,1,0:T(8,128)(2,1)S(1)}, u32[]{:S(2)}, u32[]{:S(2)}) %collective-permute-start.3) | collective-permute-done | bytes 294944 | tf_op jit(solution)/shard_map/ppermute | solution.py:30
  23.6 3.0 %collective-permute-done.4.refs_2_ = bf16[4,32,1152]{2,1,0:T(8,128)(2,1)S(1)} collective-permute-done((bf16[4,32,1152]{2,1,0:T(8,128)(2,1)S(1)}, bf16[4,32,1152]{2,1,0:T(8,128)(2,1)S(1)}, u32[]{:S(2)}, u32[]{:S(2)}) %collective-permute-start.4) | collective-permute-done | bytes 294944 | tf_op jit(solution)/shard_map/ppermute | solution.py:30
  26.6 4.5 %collective-permute-done.5.refs_3_ = bf16[4,32,1152]{2,1,0:T(8,128)(2,1)} collective-permute-done((bf16[4,32,1152]{2,1,0:T(8,128)(2,1)S(1)}, bf16[4,32,1152]{2,1,0:T(8,128)(2,1)}, u32[]{:S(2)}, u32[]{:S(2)}) %collective-permute-start.5) | collective-permute-done | bytes 294944 | tf_op jit(solution)/shard_map/ppermute | solution.py:30
  34.5 3.3 %shard_map.77 = (bf16[2,4,64,1152]{3,2,1,0:T(8,128)(2,1)S(1)}, f32[2,64,1152]{2,1,0:T(8,128)S(1)}) custom-call(bf16[2,4,2,32,1152]{4,3,2,1,0:T(8,128)(2,1)} %shard_map.76.half.refs_4_, bf16[1152,1152]{1,0:T(8,128)(2,1)S(1)} %copy-done), custom_call_target="tpu_custom_call" | custom-call | flops 1358954496 | bytes 3833856 | tf_op jit(solution)/shard_map/pallas_call | solution.py:53
  37.9 2.4 %shard_map.79 = (f32[128,1152]{1,0:T(8,128)S(1)}, bf16[128,1152]{1,0:T(8,128)(2,1)S(1)}, bf16[128,1152]{1,0:T(8,128)(2,1)S(1)}, bf16[128,1152]{1,0:T(8,128)(2,1)S(1)}) custom-call(bf16[2,4,2,32,1152]{4,3,2,1,0:T(8,128)(2,1)} %collective-permute-done.6.refs_0_.refs_5_, bf16[1152,1152]{1,0:T(8,128)(2,1)S(1)} %copy-done, ...), custom_call_target="tpu_custom_call" | custom-call | flops 679477248 | bytes 5308416 | tf_op jit(solution)/shard_map/pallas_call | solution.py:53
  42.0 2.2 %collective-permute-start.10 = (bf16[128,1152]{1,0:T(8,128)(2,1)S(1)}, bf16[128,1152]{1,0:T(8,128)(2,1)S(1)}, u32[]{:S(2)}, u32[]{:S(2)}) collective-permute-start(bf16[128,1152]{1,0:T(8,128)(2,1)S(1)} %get-tuple-element.32), channel_id=1, source_target_pairs={{0,32},{32,64},{64,96},{96,0},{1,33},{33,65},{65,97},{97,1},{2,34}... | collective-permute-start | bytes 884744 | tf_op jit(solution)/shard_map/ppermute | solution.py:30
  44.2 2.4 %shard_map.78 = (f32[128,1152]{1,0:T(8,128)S(1)}, bf16[128,1152]{1,0:T(8,128)(2,1)S(1)}, bf16[128,1152]{1,0:T(8,128)(2,1)S(1)}, bf16[128,1152]{1,0:T(8,128)(2,1)S(1)}) custom-call(bf16[2,4,2,32,1152]{4,3,2,1,0:T(8,128)(2,1)} %collective-permute-done.6.refs_0_.refs_5_, bf16[1152,1152]{1,0:T(8,128)(2,1)S(1)} %copy-done, ...), custom_call_target="tpu_custom_call" | custom-call | flops 679477248 | bytes 5308416 | tf_op jit(solution)/shard_map/pallas_call | solution.py:53
  46.6 10.4 %collective-permute-done.12 = bf16[128,1152]{1,0:T(8,128)(2,1)S(1)} collective-permute-done((bf16[128,1152]{1,0:T(8,128)(2,1)S(1)}, bf16[128,1152]{1,0:T(8,128)(2,1)S(1)}, u32[]{:S(2)}, u32[]{:S(2)}) %collective-permute-start.12) | collective-permute-done | bytes 294944 | tf_op jit(solution)/shard_map/ppermute | solution.py:30
  59.9 2.3 %collective-permute-start.7 = (bf16[128,1152]{1,0:T(8,128)(2,1)S(1)}, bf16[128,1152]{1,0:T(8,128)(2,1)S(1)}, u32[]{:S(2)}, u32[]{:S(2)}) collective-permute-start(bf16[128,1152]{1,0:T(8,128)(2,1)S(1)} %get-tuple-element.28), channel_id=1, source_target_pairs={{0,32},{32,64},{64,96},{96,0},{1,33},{33,65},{65,97},{97,1},{2,34}... | collective-permute-start | bytes 884744 | tf_op jit(solution)/shard_map/ppermute | solution.py:30
  62.2 5.5 %collective-permute-start.13 = (bf16[128,1152]{1,0:T(8,128)(2,1)S(1)}, bf16[128,1152]{1,0:T(8,128)(2,1)S(1)}, u32[]{:S(2)}, u32[]{:S(2)}) collective-permute-start(bf16[128,1152]{1,0:T(8,128)(2,1)S(1)} %add_convert_fusion), channel_id=1, source_target_pairs={{0,128},{128,0},{1,129},{129,1},{2,130},{130,2},{3,131},{131,3},{4... | collective-permute-start | bytes 884744 | tf_op jit(solution)/shard_map/ppermute | solution.py:34
  70.3 3.7 %collective-permute-done.9 = bf16[128,1152]{1,0:T(8,128)(2,1)S(1)} collective-permute-done((bf16[128,1152]{1,0:T(8,128)(2,1)S(1)}, bf16[128,1152]{1,0:T(8,128)(2,1)S(1)}, u32[]{:S(2)}, u32[]{:S(2)}) %collective-permute-start.9) | collective-permute-done | bytes 294944 | tf_op jit(solution)/shard_map/ppermute | solution.py:30
  75.7 5.6 %collective-permute-start.18 = (bf16[128,1152]{1,0:T(8,128)(2,1)S(1)}, bf16[128,1152]{1,0:T(8,128)(2,1)S(1)}, u32[]{:S(2)}, u32[]{:S(2)}) collective-permute-start(bf16[128,1152]{1,0:T(8,128)(2,1)S(1)} %fusion.7.p0.refs_0_), channel_id=1, source_target_pairs={{0,128},{128,0},{1,129},{129,1},{2,130},{130,2},{3,131},{131,3},{4... | collective-permute-start | bytes 884744 | tf_op jit(solution)/shard_map/ppermute | solution.py:34
  81.3 3.5 %collective-permute-start.15 = (bf16[128,1152]{1,0:T(8,128)(2,1)S(1)}, bf16[128,1152]{1,0:T(8,128)(2,1)S(1)}, u32[]{:S(2)}, u32[]{:S(2)}) collective-permute-start(bf16[128,1152]{1,0:T(8,128)(2,1)S(1)} %fusion.7.p0.refs_0_), channel_id=1, source_target_pairs={{0,64},{32,96},{64,0},{96,32},{1,65},{33,97},{65,1},{97,33},{2,66}... | collective-permute-start | bytes 884744 | tf_op jit(solution)/shard_map/ppermute | solution.py:30
  85.6 3.6 %collective-permute-start.33 = (bf16[4,32,1152]{2,1,0:T(8,128)(2,1)S(1)}, bf16[4,32,1152]{2,1,0:T(8,128)(2,1)S(1)}, u32[]{:S(2)}, u32[]{:S(2)}) collective-permute-start(bf16[4,32,1152]{2,1,0:T(8,128)(2,1)S(1)} %pad_maximum_fusion.3.refs_0_), channel_id=1, source_target_pairs={{0,4},{2,6},{4,0},{6,2},{1,5},{3,7},{5,1},{7,3},{8,12},{10,14},{12... | collective-permute-start | bytes 884744 | tf_op jit(solution)/shard_map/ppermute | solution.py:30
  92.5 2.2 %collective-permute-start.20 = (bf16[128,1152]{1,0:T(8,128)(2,1)S(1)}, bf16[128,1152]{1,0:T(8,128)(2,1)S(1)}, u32[]{:S(2)}, u32[]{:S(2)}) collective-permute-start(bf16[128,1152]{1,0:T(8,128)(2,1)S(1)} %collective-permute-done.18.p0.refs_4_), channel_id=1, source_target_pairs={{0,64},{32,96},{64,0},{96,32},{1,65},{33,97},{65,1},{97,33},{2,66}... | collective-permute-start | bytes 884744 | tf_op jit(solution)/shard_map/ppermute | solution.py:30
  94.7 4.3 %collective-permute-done.16.p3.refs_3_ = bf16[128,1152]{1,0:T(8,128)(2,1)S(1)} collective-permute-done((bf16[128,1152]{1,0:T(8,128)(2,1)S(1)}, bf16[128,1152]{1,0:T(8,128)(2,1)S(1)}, u32[]{:S(2)}, u32[]{:S(2)}) %collective-permute-start.16) | collective-permute-done | bytes 294944 | tf_op jit(solution)/shard_map/ppermute | solution.py:30
  99.0 2.6 %collective-permute-start.21 = (bf16[128,1152]{1,0:T(8,128)(2,1)S(1)}, bf16[128,1152]{1,0:T(8,128)(2,1)S(1)}, u32[]{:S(2)}, u32[]{:S(2)}) collective-permute-start(bf16[128,1152]{1,0:T(8,128)(2,1)S(1)} %collective-permute-done.18.p0.refs_4_), channel_id=1, source_target_pairs={{0,32},{32,64},{64,96},{96,0},{1,33},{33,65},{65,97},{97,1},{2,34}... | collective-permute-start | bytes 884744 | tf_op jit(solution)/shard_map/ppermute | solution.py:30
  101.6 2.9 %shard_map.80 = (bf16[4,2,32,1152]{3,2,1,0:T(8,128)(2,1)S(1)}, f32[4,2,32,1152]{3,2,1,0:T(8,128)S(1)}) custom-call(s32[5]{0:T(128)S(1)} %stack.64.where, bf16[128,1152]{1,0:T(8,128)(2,1)S(1)} %fusion.7.p0.refs_0_, bf16[128,1152]{1,0:T(8,128)(2,1)S(1)} %collective-permute-done.14.p1.refs_1_, bf16[128,1152]{1,0:T(8,128)(2,1)S(1)} %collective-permute-done.15.p2.refs_2_, ...), custom_call_target="tpu_custom_call" | custom-call | flops 1358954496 | bytes 3833856 | tf_op jit(solution)/shard_map/pallas_call | solution.py:53
  107.1 2.8 %collective-permute-done.21.p3.refs_7_ = bf16[128,1152]{1,0:T(8,128)(2,1)S(1)} collective-permute-done((bf16[128,1152]{1,0:T(8,128)(2,1)S(1)}, bf16[128,1152]{1,0:T(8,128)(2,1)S(1)}, u32[]{:S(2)}, u32[]{:S(2)}) %collective-permute-start.21) | collective-permute-done | bytes 294944 | tf_op jit(solution)/shard_map/ppermute | solution.py:30
  109.9 2.9 %shard_map.81 = (bf16[4,2,32,1152]{3,2,1,0:T(8,128)(2,1)S(1)}, f32[4,2,32,1152]{3,2,1,0:T(8,128)S(1)}) custom-call(s32[5]{0:T(128)S(1)} %stack.64.where, bf16[128,1152]{1,0:T(8,128)(2,1)S(1)} %collective-permute-done.18.p0.refs_4_, bf16[128,1152]{1,0:T(8,128)(2,1)S(1)} %collective-permute-done.19.p1.refs_5_, ...), custom_call_target="tpu_custom_call" | custom-call | flops 1358954496 | bytes 3833856 | tf_op jit(solution)/shard_map/pallas_call | solution.py:53
  112.9 11.3 %collective-permute-done.36 = bf16[128,1152]{1,0:T(8,128)(2,1)S(1)} collective-permute-done((bf16[128,1152]{1,0:T(8,128)(2,1)S(1)}, bf16[128,1152]{1,0:T(8,128)(2,1)S(1)}, u32[]{:S(2)}, u32[]{:S(2)}) %collective-permute-start.36) | collective-permute-done | bytes 294944 | tf_op jit(solution)/shard_map/ppermute | solution.py:34
  124.5 3.1 %collective-permute-start.39 = (bf16[2,128,1152]{2,1,0:T(8,128)(2,1)S(1)}, bf16[2,128,1152]{2,1,0:T(8,128)(2,1)S(1)}, u32[]{:S(2)}, u32[]{:S(2)}) collective-permute-start(bf16[2,128,1152]{2,1,0:T(8,128)(2,1)S(1)} %pad_maximum_fusion.refs_0_), channel_id=1, source_target_pairs={{0,32},{32,64},{64,96},{96,0},{1,33},{33,65},{65,97},{97,1},{2,34}... | collective-permute-start | bytes 1769480 | tf_op jit(solution)/shard_map/ppermute | solution.py:30
  129.2 18.9 %collective-permute-done.37.refs_1_ = bf16[2,128,1152]{2,1,0:T(8,128)(2,1)S(1)} collective-permute-done((bf16[2,128,1152]{2,1,0:T(8,128)(2,1)S(1)}, bf16[2,128,1152]{2,1,0:T(8,128)(2,1)S(1)}, u32[]{:S(2)}, u32[]{:S(2)}) %collective-permute-start.37) | collective-permute-done | bytes 589856 | tf_op jit(solution)/shard_map/ppermute | solution.py:30
  149.1 2.4 %collective-permute-start.25 = (bf16[2,2,32,1152]{3,2,1,0:T(8,128)(2,1)S(1)}, bf16[2,2,32,1152]{3,2,1,0:T(8,128)(2,1)S(1)}, u32[]{:S(2)}, u32[]{:S(2)}) collective-permute-start(bf16[2,2,32,1152]{3,2,1,0:T(8,128)(2,1)S(1)} %get-tuple-element.42), channel_id=1, source_target_pairs={{0,6},{2,0},{4,2},{6,4},{1,7},{3,1},{5,3},{7,5},{8,14},{10,8},{12,... | collective-permute-start | bytes 884744 | tf_op jit(solution)/shard_map/ppermute | solution.py:30
  151.4 7.4 %shard_map.86 = bf16[1152,1152]{1,0:T(8,128)(2,1)} custom-call(bf16[2,128,1152]{2,1,0:T(8,128)(2,1)S(1)} %pad_maximum_fusion.refs_0_, bf16[2,128,1152]{2,1,0:T(8,128)(2,1)S(1)} %collective-permute-done.37.refs_1_, bf16[2,128,1152]{2,1,0:T(8,128)(2,1)S(1)} %collective-permute-done.38.refs_2_, bf16[2,128,1152]{2,1,0:T(8,128)(2,1)S(1)} %collective-permute-done.39.refs_3_, ...), custom_call_target="tpu_custom_call" | custom-call | flops 2717908992 | bytes 4718592 | tf_op jit(solution)/shard_map/pallas_call | solution.py:53
  158.9 2.4 %collective-permute-done.25.three = bf16[2,2,32,1152]{3,2,1,0:T(8,128)(2,1)S(1)} collective-permute-done((bf16[2,2,32,1152]{3,2,1,0:T(8,128)(2,1)S(1)}, bf16[2,2,32,1152]{3,2,1,0:T(8,128)(2,1)S(1)}, u32[]{:S(2)}, u32[]{:S(2)}) %collective-permute-start.25) | collective-permute-done | bytes 294944 | tf_op jit(solution)/shard_map/ppermute | solution.py:30
  163.2 11.2 %collective-permute-start.27 = (bf16[32,1152]{1,0:T(8,128)(2,1)S(1)}, bf16[32,1152]{1,0:T(8,128)(2,1)S(1)}, u32[]{:S(2)}, u32[]{:S(2)}) collective-permute-start(bf16[32,1152]{1,0:T(8,128)(2,1)S(1)} %get-tuple-element.45), channel_id=1, source_target_pairs={{0,16},{8,24},{16,0},{24,8},{1,17},{9,25},{17,1},{25,9},{2,18},{10... | collective-permute-start | bytes 221192 | tf_op jit(solution)/shard_map/ppermute | solution.py:30
  174.5 4.8 %shard_map.85 = bf16[1152,1152]{1,0:T(8,128)(2,1)} custom-call(bf16[128,1152]{1,0:T(8,128)(2,1)S(1)} %fusion.7.p0.refs_0_, bf16[128,1152]{1,0:T(8,128)(2,1)S(1)} %collective-permute-done.14.p1.refs_1_, bf16[128,1152]{1,0:T(8,128)(2,1)S(1)} %collective-permute-done.15.p2.refs_2_, bf16[128,1152]{1,0:T(8,128)(2,1)S(1)} %collective-permute-done.16.p3.refs_3_, ...), custom_call_target="tpu_custom_call" | custom-call | flops 2717908992 | bytes 4718592 | tf_op jit(solution)/shard_map/pallas_call | solution.py:53
  (74 shorter events, 31.1 us)
Async XLA Ops:
  15.2 11.4 %collective-permute-start.4 = (bf16[4,32,1152]{2,1,0:T(8,128)(2,1)S(1)}, bf16[4,32,1152]{2,1,0:T(8,128)(2,1)S(1)}, u32[]{:S(2)}, u32[]{:S(2)}) collective-permute-start(bf16[4,32,1152]{2,1,0:T(8,128)(2,1)S(1)} %pad_maximum_fusion.1.refs_0_), channel_id=1, source_target_pairs={{0,4},{2,6},{4,0},{6,2},{1,5},{3,7},{5,1},{7,3},{8,12},{10,14},{12... | collective-permute-start | bytes 884744 | tf_op jit(solution)/shard_map/ppermute | solution.py:30
  16.3 14.8 %collective-permute-start.5 = (bf16[4,32,1152]{2,1,0:T(8,128)(2,1)S(1)}, bf16[4,32,1152]{2,1,0:T(8,128)(2,1)}, u32[]{:S(2)}, u32[]{:S(2)}) collective-permute-start(bf16[4,32,1152]{2,1,0:T(8,128)(2,1)S(1)} %pad_maximum_fusion.1.refs_0_), channel_id=1, source_target_pairs={{0,6},{2,0},{4,2},{6,4},{1,7},{3,1},{5,3},{7,5},{8,14},{10,8},{12,... | collective-permute-start | bytes 884744 | tf_op jit(solution)/shard_map/ppermute | solution.py:30
  33.2 26.7 %collective-permute-start.31 = (bf16[32,1152]{1,0:T(8,128)(2,1)}, bf16[32,1152]{1,0:T(8,128)(2,1)}, u32[]{:S(2)}, u32[]{:S(2)}) collective-permute-start(bf16[32,1152]{1,0:T(8,128)(2,1)} %param.5), channel_id=1, source_target_pairs={{0,24},{8,0},{16,8},{24,16},{1,25},{9,1},{17,9},{25,17},{2,26},{10... | collective-permute-start | bytes 221192 | tf_op jit(solution)/shard_map/ppermute | solution.py:30
  33.4 28.9 %collective-permute-start.30 = (bf16[32,1152]{1,0:T(8,128)(2,1)}, bf16[32,1152]{1,0:T(8,128)(2,1)}, u32[]{:S(2)}, u32[]{:S(2)}) collective-permute-start(bf16[32,1152]{1,0:T(8,128)(2,1)} %param.5), channel_id=1, source_target_pairs={{0,16},{8,24},{16,0},{24,8},{1,17},{9,25},{17,1},{25,9},{2,18},{10... | collective-permute-start | bytes 221192 | tf_op jit(solution)/shard_map/ppermute | solution.py:30
  40.3 16.7 %collective-permute-start.12 = (bf16[128,1152]{1,0:T(8,128)(2,1)S(1)}, bf16[128,1152]{1,0:T(8,128)(2,1)S(1)}, u32[]{:S(2)}, u32[]{:S(2)}) collective-permute-start(bf16[128,1152]{1,0:T(8,128)(2,1)S(1)} %get-tuple-element.34), channel_id=1, source_target_pairs={{0,96},{32,0},{64,32},{96,64},{1,97},{33,1},{65,33},{97,65},{2,98}... | collective-permute-start | bytes 884744 | tf_op jit(solution)/shard_map/ppermute | solution.py:30
  41.1 17.7 %collective-permute-start.11 = (bf16[128,1152]{1,0:T(8,128)(2,1)S(1)}, bf16[128,1152]{1,0:T(8,128)(2,1)S(1)}, u32[]{:S(2)}, u32[]{:S(2)}) collective-permute-start(bf16[128,1152]{1,0:T(8,128)(2,1)S(1)} %get-tuple-element.33), channel_id=1, source_target_pairs={{0,64},{32,96},{64,0},{96,32},{1,65},{33,97},{65,1},{97,33},{2,66}... | collective-permute-start | bytes 884744 | tf_op jit(solution)/shard_map/ppermute | solution.py:30
  42.0 16.8 %collective-permute-start.10 = (bf16[128,1152]{1,0:T(8,128)(2,1)S(1)}, bf16[128,1152]{1,0:T(8,128)(2,1)S(1)}, u32[]{:S(2)}, u32[]{:S(2)}) collective-permute-start(bf16[128,1152]{1,0:T(8,128)(2,1)S(1)} %get-tuple-element.32), channel_id=1, source_target_pairs={{0,32},{32,64},{64,96},{96,0},{1,33},{33,65},{65,97},{97,1},{2,34}... | collective-permute-start | bytes 884744 | tf_op jit(solution)/shard_map/ppermute | solution.py:30
  58.8 15.3 %collective-permute-start.9 = (bf16[128,1152]{1,0:T(8,128)(2,1)S(1)}, bf16[128,1152]{1,0:T(8,128)(2,1)S(1)}, u32[]{:S(2)}, u32[]{:S(2)}) collective-permute-start(bf16[128,1152]{1,0:T(8,128)(2,1)S(1)} %get-tuple-element.30), channel_id=1, source_target_pairs={{0,96},{32,0},{64,32},{96,64},{1,97},{33,1},{65,33},{97,65},{2,98}... | collective-permute-start | bytes 884744 | tf_op jit(solution)/shard_map/ppermute | solution.py:30
  58.8 15.2 %collective-permute-start.8 = (bf16[128,1152]{1,0:T(8,128)(2,1)S(1)}, bf16[128,1152]{1,0:T(8,128)(2,1)S(1)}, u32[]{:S(2)}, u32[]{:S(2)}) collective-permute-start(bf16[128,1152]{1,0:T(8,128)(2,1)S(1)} %get-tuple-element.29), channel_id=1, source_target_pairs={{0,64},{32,96},{64,0},{96,32},{1,65},{33,97},{65,1},{97,33},{2,66}... | collective-permute-start | bytes 884744 | tf_op jit(solution)/shard_map/ppermute | solution.py:30
  59.9 14.7 %collective-permute-start.7 = (bf16[128,1152]{1,0:T(8,128)(2,1)S(1)}, bf16[128,1152]{1,0:T(8,128)(2,1)S(1)}, u32[]{:S(2)}, u32[]{:S(2)}) collective-permute-start(bf16[128,1152]{1,0:T(8,128)(2,1)S(1)} %get-tuple-element.28), channel_id=1, source_target_pairs={{0,32},{32,64},{64,96},{96,0},{1,33},{33,65},{65,97},{97,1},{2,34}... | collective-permute-start | bytes 884744 | tf_op jit(solution)/shard_map/ppermute | solution.py:30
  62.2 12.4 %collective-permute-start.13 = (bf16[128,1152]{1,0:T(8,128)(2,1)S(1)}, bf16[128,1152]{1,0:T(8,128)(2,1)S(1)}, u32[]{:S(2)}, u32[]{:S(2)}) collective-permute-start(bf16[128,1152]{1,0:T(8,128)(2,1)S(1)} %add_convert_fusion), channel_id=1, source_target_pairs={{0,128},{128,0},{1,129},{129,1},{2,130},{130,2},{3,131},{131,3},{4... | collective-permute-start | bytes 884744 | tf_op jit(solution)/shard_map/ppermute | solution.py:34
  69.0 16.6 %collective-permute-start.32 = (bf16[4,32,1152]{2,1,0:T(8,128)(2,1)S(1)}, bf16[4,32,1152]{2,1,0:T(8,128)(2,1)S(1)}, u32[]{:S(2)}, u32[]{:S(2)}) collective-permute-start(bf16[4,32,1152]{2,1,0:T(8,128)(2,1)S(1)} %pad_maximum_fusion.3.refs_0_), channel_id=1, source_target_pairs={{0,2},{2,4},{4,6},{6,0},{1,3},{3,5},{5,7},{7,1},{8,10},{10,12},{12... | collective-permute-start | bytes 884744 | tf_op jit(solution)/shard_map/ppermute | solution.py:30
  75.1 14.1 %collective-permute-start.14 = (bf16[128,1152]{1,0:T(8,128)(2,1)S(1)}, bf16[128,1152]{1,0:T(8,128)(2,1)S(1)}, u32[]{:S(2)}, u32[]{:S(2)}) collective-permute-start(bf16[128,1152]{1,0:T(8,128)(2,1)S(1)} %fusion.7.p0.refs_0_), channel_id=1, source_target_pairs={{0,96},{32,0},{64,32},{96,64},{1,97},{33,1},{65,33},{97,65},{2,98}... | collective-permute-start | bytes 884744 | tf_op jit(solution)/shard_map/ppermute | solution.py:30
  75.7 15.0 %collective-permute-start.18 = (bf16[128,1152]{1,0:T(8,128)(2,1)S(1)}, bf16[128,1152]{1,0:T(8,128)(2,1)S(1)}, u32[]{:S(2)}, u32[]{:S(2)}) collective-permute-start(bf16[128,1152]{1,0:T(8,128)(2,1)S(1)} %fusion.7.p0.refs_0_), channel_id=1, source_target_pairs={{0,128},{128,0},{1,129},{129,1},{2,130},{130,2},{3,131},{131,3},{4... | collective-permute-start | bytes 884744 | tf_op jit(solution)/shard_map/ppermute | solution.py:34
  81.3 11.2 %collective-permute-start.15 = (bf16[128,1152]{1,0:T(8,128)(2,1)S(1)}, bf16[128,1152]{1,0:T(8,128)(2,1)S(1)}, u32[]{:S(2)}, u32[]{:S(2)}) collective-permute-start(bf16[128,1152]{1,0:T(8,128)(2,1)S(1)} %fusion.7.p0.refs_0_), channel_id=1, source_target_pairs={{0,64},{32,96},{64,0},{96,32},{1,65},{33,97},{65,1},{97,33},{2,66}... | collective-permute-start | bytes 884744 | tf_op jit(solution)/shard_map/ppermute | solution.py:30
  84.8 14.2 %collective-permute-start.16 = (bf16[128,1152]{1,0:T(8,128)(2,1)S(1)}, bf16[128,1152]{1,0:T(8,128)(2,1)S(1)}, u32[]{:S(2)}, u32[]{:S(2)}) collective-permute-start(bf16[128,1152]{1,0:T(8,128)(2,1)S(1)} %fusion.7.p0.refs_0_), channel_id=1, source_target_pairs={{0,32},{32,64},{64,96},{96,0},{1,33},{33,65},{65,97},{97,1},{2,34}... | collective-permute-start | bytes 884744 | tf_op jit(solution)/shard_map/ppermute | solution.py:30
  85.6 18.9 %collective-permute-start.33 = (bf16[4,32,1152]{2,1,0:T(8,128)(2,1)S(1)}, bf16[4,32,1152]{2,1,0:T(8,128)(2,1)S(1)}, u32[]{:S(2)}, u32[]{:S(2)}) collective-permute-start(bf16[4,32,1152]{2,1,0:T(8,128)(2,1)S(1)} %pad_maximum_fusion.3.refs_0_), channel_id=1, source_target_pairs={{0,4},{2,6},{4,0},{6,2},{1,5},{3,7},{5,1},{7,3},{8,12},{10,14},{12... | collective-permute-start | bytes 884744 | tf_op jit(solution)/shard_map/ppermute | solution.py:30
  89.2 15.4 %collective-permute-start.34 = (bf16[4,32,1152]{2,1,0:T(8,128)(2,1)S(1)}, bf16[4,32,1152]{2,1,0:T(8,128)(2,1)S(1)}, u32[]{:S(2)}, u32[]{:S(2)}) collective-permute-start(bf16[4,32,1152]{2,1,0:T(8,128)(2,1)S(1)} %pad_maximum_fusion.3.refs_0_), channel_id=1, source_target_pairs={{0,6},{2,0},{4,2},{6,4},{1,7},{3,1},{5,3},{7,5},{8,14},{10,8},{12,... | collective-permute-start | bytes 884744 | tf_op jit(solution)/shard_map/ppermute | solution.py:30
  90.7 16.4 %collective-permute-start.19 = (bf16[128,1152]{1,0:T(8,128)(2,1)S(1)}, bf16[128,1152]{1,0:T(8,128)(2,1)S(1)}, u32[]{:S(2)}, u32[]{:S(2)}) collective-permute-start(bf16[128,1152]{1,0:T(8,128)(2,1)S(1)} %collective-permute-done.18.p0.refs_4_), channel_id=1, source_target_pairs={{0,96},{32,0},{64,32},{96,64},{1,97},{33,1},{65,33},{97,65},{2,98}... | collective-permute-start | bytes 884744 | tf_op jit(solution)/shard_map/ppermute | solution.py:30
  92.5 14.6 %collective-permute-start.20 = (bf16[128,1152]{1,0:T(8,128)(2,1)S(1)}, bf16[128,1152]{1,0:T(8,128)(2,1)S(1)}, u32[]{:S(2)}, u32[]{:S(2)}) collective-permute-start(bf16[128,1152]{1,0:T(8,128)(2,1)S(1)} %collective-permute-done.18.p0.refs_4_), channel_id=1, source_target_pairs={{0,64},{32,96},{64,0},{96,32},{1,65},{33,97},{65,1},{97,33},{2,66}... | collective-permute-start | bytes 884744 | tf_op jit(solution)/shard_map/ppermute | solution.py:30
  99.0 10.9 %collective-permute-start.21 = (bf16[128,1152]{1,0:T(8,128)(2,1)S(1)}, bf16[128,1152]{1,0:T(8,128)(2,1)S(1)}, u32[]{:S(2)}, u32[]{:S(2)}) collective-permute-start(bf16[128,1152]{1,0:T(8,128)(2,1)S(1)} %collective-permute-done.18.p0.refs_4_), channel_id=1, source_target_pairs={{0,32},{32,64},{64,96},{96,0},{1,33},{33,65},{65,97},{97,1},{2,34}... | collective-permute-start | bytes 884744 | tf_op jit(solution)/shard_map/ppermute | solution.py:30
  104.5 20.0 %collective-permute-start.17 = (bf16[4,2,32,1152]{3,2,1,0:T(8,128)(2,1)S(1)}, bf16[4,2,32,1152]{3,2,1,0:T(8,128)(2,1)S(1)}, u32[]{:S(2)}, u32[]{:S(2)}) collective-permute-start(bf16[4,2,32,1152]{3,2,1,0:T(8,128)(2,1)S(1)} %get-tuple-element.36), channel_id=1, source_target_pairs={{0,1},{1,0},{2,3},{3,2},{4,5},{5,4},{6,7},{7,6},{8,9},{9,8},{10,11... | collective-permute-start | bytes 1769480 | tf_op jit(solution)/shard_map/ppermute | solution.py:34
  104.6 19.6 %collective-permute-start.36 = (bf16[128,1152]{1,0:T(8,128)(2,1)S(1)}, bf16[128,1152]{1,0:T(8,128)(2,1)S(1)}, u32[]{:S(2)}, u32[]{:S(2)}) collective-permute-start(bf16[128,1152]{1,0:T(8,128)(2,1)S(1)} %bitcast.34), channel_id=1, source_target_pairs={{0,128},{128,0},{1,129},{129,1},{2,130},{130,2},{3,131},{131,3},{4... | collective-permute-start | bytes 884744 | tf_op jit(solution)/shard_map/ppermute | solution.py:34
  107.1 67.4 %collective-permute-start.35 = (bf16[2,4,2,32,1152]{4,3,2,1,0:T(8,128)(2,1)S(1)}, bf16[2,4,2,32,1152]{4,3,2,1,0:T(8,128)(2,1)S(1)}, u32[]{:S(2)}, u32[]{:S(2)}) collective-permute-start(bf16[2,4,2,32,1152]{4,3,2,1,0:T(8,128)(2,1)S(1)} %shard_map.84.refs_8_), channel_id=1, source_target_pairs={{0,1},{1,0},{2,3},{3,2},{4,5},{5,4},{6,7},{7,6},{8,9},{9,8},{10,11... | collective-permute-start | bytes 3538952 | tf_op jit(solution)/shard_map/ppermute | solution.py:34
  112.8 14.8 %collective-permute-start.22 = (bf16[4,2,32,1152]{3,2,1,0:T(8,128)(2,1)S(1)}, bf16[4,2,32,1152]{3,2,1,0:T(8,128)(2,1)S(1)}, u32[]{:S(2)}, u32[]{:S(2)}) collective-permute-start(bf16[4,2,32,1152]{3,2,1,0:T(8,128)(2,1)S(1)} %get-tuple-element.38), channel_id=1, source_target_pairs={{0,1},{1,0},{2,3},{3,2},{4,5},{5,4},{6,7},{7,6},{8,9},{9,8},{10,11... | collective-permute-start | bytes 1769480 | tf_op jit(solution)/shard_map/ppermute | solution.py:34
  124.3 23.8 %collective-permute-start.37 = (bf16[2,128,1152]{2,1,0:T(8,128)(2,1)S(1)}, bf16[2,128,1152]{2,1,0:T(8,128)(2,1)S(1)}, u32[]{:S(2)}, u32[]{:S(2)}) collective-permute-start(bf16[2,128,1152]{2,1,0:T(8,128)(2,1)S(1)} %pad_maximum_fusion.refs_0_), channel_id=1, source_target_pairs={{0,96},{32,0},{64,32},{96,64},{1,97},{33,1},{65,33},{97,65},{2,98}... | collective-permute-start | bytes 1769480 | tf_op jit(solution)/shard_map/ppermute | solution.py:30
  124.4 24.7 %collective-permute-start.38 = (bf16[2,128,1152]{2,1,0:T(8,128)(2,1)S(1)}, bf16[2,128,1152]{2,1,0:T(8,128)(2,1)S(1)}, u32[]{:S(2)}, u32[]{:S(2)}) collective-permute-start(bf16[2,128,1152]{2,1,0:T(8,128)(2,1)S(1)} %pad_maximum_fusion.refs_0_), channel_id=1, source_target_pairs={{0,64},{32,96},{64,0},{96,32},{1,65},{33,97},{65,1},{97,33},{2,66}... | collective-permute-start | bytes 1769480 | tf_op jit(solution)/shard_map/ppermute | solution.py:30
  124.5 26.9 %collective-permute-start.39 = (bf16[2,128,1152]{2,1,0:T(8,128)(2,1)S(1)}, bf16[2,128,1152]{2,1,0:T(8,128)(2,1)S(1)}, u32[]{:S(2)}, u32[]{:S(2)}) collective-permute-start(bf16[2,128,1152]{2,1,0:T(8,128)(2,1)S(1)} %pad_maximum_fusion.refs_0_), channel_id=1, source_target_pairs={{0,32},{32,64},{64,96},{96,0},{1,33},{33,65},{65,97},{97,1},{2,34}... | collective-permute-start | bytes 1769480 | tf_op jit(solution)/shard_map/ppermute | solution.py:30
  127.9 31.0 %collective-permute-start.23 = (bf16[2,2,32,1152]{3,2,1,0:T(8,128)(2,1)S(1)}, bf16[2,2,32,1152]{3,2,1,0:T(8,128)(2,1)S(1)}, u32[]{:S(2)}, u32[]{:S(2)}) collective-permute-start(bf16[2,2,32,1152]{3,2,1,0:T(8,128)(2,1)S(1)} %get-tuple-element.40), channel_id=1, source_target_pairs={{0,2},{2,4},{4,6},{6,0},{1,3},{3,5},{5,7},{7,1},{8,10},{10,12},{12... | collective-permute-start | bytes 884744 | tf_op jit(solution)/shard_map/ppermute | solution.py:30
  149.1 12.2 %collective-permute-start.25 = (bf16[2,2,32,1152]{3,2,1,0:T(8,128)(2,1)S(1)}, bf16[2,2,32,1152]{3,2,1,0:T(8,128)(2,1)S(1)}, u32[]{:S(2)}, u32[]{:S(2)}) collective-permute-start(bf16[2,2,32,1152]{3,2,1,0:T(8,128)(2,1)S(1)} %get-tuple-element.42), channel_id=1, source_target_pairs={{0,6},{2,0},{4,2},{6,4},{1,7},{3,1},{5,3},{7,5},{8,14},{10,8},{12,... | collective-permute-start | bytes 884744 | tf_op jit(solution)/shard_map/ppermute | solution.py:30
  162.0 17.3 %collective-permute-start.28 = (bf16[32,1152]{1,0:T(8,128)(2,1)S(1)}, bf16[32,1152]{1,0:T(8,128)(2,1)S(1)}, u32[]{:S(2)}, u32[]{:S(2)}) collective-permute-start(bf16[32,1152]{1,0:T(8,128)(2,1)S(1)} %get-tuple-element.46), channel_id=1, source_target_pairs={{0,24},{8,0},{16,8},{24,16},{1,25},{9,1},{17,9},{25,17},{2,26},{10... | collective-permute-start | bytes 221192 | tf_op jit(solution)/shard_map/ppermute | solution.py:30
  163.2 18.0 %collective-permute-start.27 = (bf16[32,1152]{1,0:T(8,128)(2,1)S(1)}, bf16[32,1152]{1,0:T(8,128)(2,1)S(1)}, u32[]{:S(2)}, u32[]{:S(2)}) collective-permute-start(bf16[32,1152]{1,0:T(8,128)(2,1)S(1)} %get-tuple-element.45), channel_id=1, source_target_pairs={{0,16},{8,24},{16,0},{24,8},{1,17},{9,25},{17,1},{25,9},{2,18},{10... | collective-permute-start | bytes 221192 | tf_op jit(solution)/shard_map/ppermute | solution.py:30
  (11 other events, 127.2 us)
where the time goes:
time: 182 us
  waiting for transfers between devices  79.9 us (44%)
  starting transfers between devices  67.5 us (37%)
  Pallas kernels  29.9 us (16%)
  other arithmetic  3.65 us (2%)
    ppermute x33, waiting for transfers between devices, shift(): lax.ppermute(value, axis, [(i, (i + step) % size) for i in range(size)])  67 us
    ppermute x33, starting transfers between devices, shift(): lax.ppermute(value, axis, [(i, (i + step) % size) for i in range(size)])  56.1 us
    pallas_call x11, Pallas kernels, call(): pl.pallas_call(kernel, out_shape=tuple((make(shape, dtype) for shape, dty...  29.9 us
    ppermute x7, waiting for transfers between devices, swap(): return lax.ppermute(value, axis, [(0, 1), (1, 0)])  12.9 us
    ppermute x7, starting transfers between devices, swap(): return lax.ppermute(value, axis, [(0, 1), (1, 0)])  11.4 us
  transfers between devices with their start and end apart: 40, of which 17 were waited for; matrix products, arithmetic and copies ran while one was open for 1% of the time, Pallas kernels for 15%

commit v1 on v0

--- a/solution.py
+++ b/solution.py
@@ -28,6 +28,11 @@
 def shift(value, axis, step):
     size = lax.axis_size(axis)
     return lax.ppermute(value, axis, [(i, (i + step) % size) for i in range(size)])
+
+
+def flip(value, axis, mask):
+    size = lax.axis_size(axis)
+    return lax.ppermute(value, axis, [(i, i ^ mask) for i in range(size)])
 
 
 def swap(value, axis):
@@ -68,27 +73,39 @@
     return lax.dot_general(left, right, (((1,), (1,)), ((), ())), preferred_element_type=F32)
 
 
-def col_place_kernel(where, *refs):
-    out = refs[-1]
-    zh, y, zl, x = (where[i] for i in range(4))
+def place(where, out, az, ax, block):
+    zh, y = where[0], where[1]
+    far = lax.rem(lax.div(az, 2) + zh, 2)
+    ay = lax.rem(az, 2) * 2 + lax.div(ax, 2)
+    out[far, lax.rem(ay + 4 - y, 4), lax.rem(ax, 2)] = block
+
+
+def shift_place_kernel(where, *refs):
     for kz in range(4):
         for kx in range(4):
-            az = lax.rem(zl + 4 - kz, 4)
-            ax = lax.rem(x + 4 - kx, 4)
-            far = lax.rem(lax.div(az, 2) + zh, 2)
-            ay = lax.rem(az, 2) * 2 + lax.div(ax, 2)
-            out[far, lax.rem(ay + 4 - y, 4), lax.rem(ax, 2)] = refs[kx][kz]
-
-
-def col_place(where, pieces):
-    rows, width = pieces[0].shape[1:]
-    return call(
-        col_place_kernel, [((2, 4, 2, rows, width), BF16)], pieces, where=where
-    )[0]
+            az = lax.rem(where[2] + 4 - kz, 4)
+            ax = lax.rem(where[3] + 4 - kx, 4)
+            place(where, refs[-1], az, ax, refs[kx][kz])
+
+
+def flip_place_kernel(where, near, far, out):
+    for kz in range(4):
+        for kx in range(4):
+            az = lax.bitwise_xor(where[2], kz)
+            ax = lax.bitwise_xor(where[3], kx)
+            place(where, out, az, ax, (near, far)[kx // 2][kx % 2, kz])
+
+
+def col_place(kernel, where, pieces):
+    rows, width = pieces[0].shape[-2:]
+    return call(kernel, [((2, 4, 2, rows, width), BF16)], pieces, where=where)[0]
 
 
 def shifts(value, axis):
-    return [value] + [shift(value, axis, k) for k in (1, 2, 3)]
+    got = [value]
+    for k in (1, 2, 3):
+        got.append(shift(value, axis, k))
+    return got
 
 
 def spread(value):
@@ -96,10 +113,17 @@
     return [own, three, two, one]
 
 
-def col_gather(where, own):
+def gather_shifts(where, own):
     line = jnp.stack(shifts(own, "zl"))
-    half = col_place(where, shifts(line, "x"))
-    return half, swap(half, "c")
+    return col_place(shift_place_kernel, where, shifts(line, "x"))
+
+
+def gather_flips(where, own):
+    pair = jnp.stack([own, flip(own, "zl", 1)])
+    line = jnp.concatenate([pair, flip(pair, "zl", 2)])
+    lines = jnp.stack([line, flip(line, "x", 1)])
+    rest = flip(lines, "x", 2)
+    return col_place(flip_place_kernel, where, [lines, rest])
 
 
 def own_act_kernel(half, weight, part, first):
@@ -181,27 +205,24 @@
     )
 
 
-def line_send_kernel(near, near_got, far, far_got, keep, one, two, three):
-    for plane, (own, got) in enumerate(((near, near_got), (far, far_got))):
-        for k, out in enumerate((keep, one, two, three)):
-            out[plane] = (own[k] + got[k].astype(F32)).astype(out.dtype)
-
-
-def line_sends(near, near_got, far, far_got):
-    shape = (2, *near.shape[1:])
-    return call(
-        line_send_kernel,
-        [(shape, F32)] + [(shape, BF16)] * 3,
-        [near, near_got, far, far_got],
-    )
-
-
-def line_kernel(where, kept, one, two, three, *outs_sums):
+def line_send_kernel(own, got, *outs):
+    for k, out in enumerate(outs):
+        out[...] = (own[k] + got[k].astype(F32)).astype(out.dtype)
+
+
+def line_sends(own, got):
+    shape = own.shape[1:]
+    return call(line_send_kernel, [(shape, F32)] + [(shape, BF16)] * 3, [own, got])
+
+
+def line_kernel(where, *refs):
     zh, zl = where[0], where[2]
-    outs, sums = outs_sums[:4], outs_sums[4]
-    sums[...] = (
-        kept[...] + one[...].astype(F32) + two[...].astype(F32) + three[...].astype(F32)
-    )
+    outs, sums = refs[8:12], refs[12]
+    for plane in range(2):
+        kept, one, two, three = refs[plane * 4 : plane * 4 + 4]
+        sums[plane] = (
+            kept[...] + one[...].astype(F32) + two[...].astype(F32) + three[...].astype(F32)
+        )
     for k, out in enumerate(outs):
         az = lax.rem(zl + k, 4)
         plane = lax.rem(lax.div(az, 2) + zh, 2)
@@ -209,7 +230,7 @@
 
 
 def line_sums(where, lines):
-    block, width = lines[0].shape[2:]
+    block, width = lines[0].shape[1:]
     return call(
         line_kernel,
         [((block, width), F32)] + [((block, width), BF16)] * 3,
@@ -243,18 +264,20 @@
         send(i).wait()
 
 
-def second_kernel(factor, *refs):
+def second_kernel(factor, where, *refs):
     pieces, (own, other, out, act, stage, sem) = refs[:4], refs[4:]
     rows = pieces[0].shape[1] // 2
     width = own.shape[-1]
-    for j, piece in enumerate(pieces):
+    y = where[1]
+    for i, piece in enumerate(pieces):
 
         @pl.loop(0, 4)
-        def _(i):
-            far, core = lax.div(i, 2), lax.rem(i, 2)
-            values = piece[far, pl.ds(core * rows, rows)].astype(F32)
-            start = (core * 8 + far * 4 + j) * rows
-            act[pl.ds(start, rows)] = gelu_value(values).astype(BF16)
+        def _(n):
+            low, core = lax.div(n, 2), lax.rem(n, 2)
+            ay = lax.bitwise_xor(y, i % 2 * 2 + low)
+            block = core * 8 + i // 2 * 4 + lax.rem(ay + 4 - y, 4)
+            values = piece[low, pl.ds(core * rows, rows)].astype(F32)
+            act[pl.ds(block * rows, rows)] = gelu_value(values).astype(BF16)
 
     half = 8 * rows
     lefts = [lambda cols, n=n: act[n * half : (n + 1) * half, cols] for n in range(2)]
@@ -262,7 +285,7 @@
     outer(lefts, rights, out, stage, sem, factor)
 
 
-def first_kernel(factor, *refs):
+def first_kernel(factor, where, *refs):
     pieces, (own, other, out, right, stage, sem) = refs[:8], refs[8:]
     rows = pieces[0].shape[0] // 2
     half = 8 * rows
@@ -279,7 +302,7 @@
     outer(lefts, rights, out, stage, sem, factor)
 
 
-def token_outer(kernel, pieces, halves, factor, swapped):
+def token_outer(kernel, where, pieces, halves, factor, swapped):
     width = pieces[0].shape[-1]
     tokens = sum(p.size for p in pieces) // width
     left, right = width, halves[0].shape[-1]
@@ -294,6 +317,7 @@
             pltpu.VMEM((left // CHUNK, CHUNK, right), BF16),
             pltpu.SemaphoreType.DMA((left // CHUNK,)),
         ],
+        where=where,
         flops=2 * tokens * left * right,
         hbm_out=True,
     )[0]
@@ -316,9 +340,13 @@
         ]
     ).reshape(token_rows, width)
 
-    grad_half, grad_other = col_gather(where, out_grad)
-    pre_far = swap(preact, "zh")
-    pre = spread(jnp.stack([preact, pre_far]))
+    grad_half = gather_shifts(where, out_grad)
+    grad_other = swap(grad_half, "c")
+
+    pre_near = jnp.stack([preact, flip(preact, "y", 1)])
+    pre = [pre_near, flip(pre_near, "y", 2)]
+    pre_far = swap(pre_near, "zh")
+    pre += [pre_far, flip(pre_far, "y", 2)]
 
     part, first = own_act(grad_half, second_weight)
 
@@ -339,18 +367,20 @@
 
     def plane_inputs(pieces):
         away, keep = token_products(where, pieces, first_weight)
-        return keep, swap(away, "c")
-
-    keep, *sends = line_sends(*plane_inputs(near), *plane_inputs(far))
-    lines = [keep] + [shift(s, "x", k) for k, s in zip((1, 2, 3), sends)]
+        got = swap(away, "c")
+        keep, *sends = line_sends(keep, got)
+        return [keep] + [shift(s, "x", k) for k, s in zip((1, 2, 3), sends)]
+
+    lines = plane_inputs(near) + plane_inputs(far)
     grad_inputs, *sends = line_sums(where, lines)
     got = [shift(s, "zl", k) for k, s in zip((1, 2, 3), sends)]
     grad_inputs = grad_inputs + sum(g.astype(F32) for g in got)
 
-    halves = col_gather(where, inputs)
-    grad_first = token_outer(first_kernel, near + far, halves, factor, True)
+    input_half = gather_flips(where, inputs)
+    halves = (input_half, swap(input_half, "c"))
+    grad_first = token_outer(first_kernel, where, near + far, halves, factor, True)
     grad_second = token_outer(
-        second_kernel, pre, (grad_half, grad_other), factor, False
+        second_kernel, where, pre, (grad_half, grad_other), factor, False
     )
     return (grad_inputs, grad_first, grad_second)
 

time: 182 us -> 188 us (1.033)
  the two profiles are of different devices: /device:TPU:26 before, /device:TPU:8 now
where the time goes in v1:
time: 188 us; the launch traced here: 186 us
  starting transfers between devices  106 us (56%)
  waiting for transfers between devices  44.9 us (24%)
  Pallas kernels  30.4 us (16%)
  other arithmetic  4.34 us (2%)
    ppermute x27, starting transfers between devices, shift(): lax.ppermute(value, axis, [(i, (i + step) % size) for i in range(size)])  82 us
    pallas_call x12, Pallas kernels, call(): pl.pallas_call(kernel, out_shape=tuple((make(shape, dtype) for shape, dty...  30.4 us
    ppermute x27, waiting for transfers between devices, shift(): lax.ppermute(value, axis, [(i, (i + step) % size) for i in range(size)])  24.3 us
    ppermute x7, waiting for transfers between devices, flip(): return lax.ppermute(value, axis, [(i, i ^ mask) for i in range(size)])  18.1 us
    ppermute x7, starting transfers between devices, swap(): return lax.ppermute(value, axis, [(0, 1), (1, 0)])  12.4 us
    ppermute x7, starting transfers between devices, flip(): return lax.ppermute(value, axis, [(i, i ^ mask) for i in range(size)])  11.4 us
  transfers between devices with their start and end apart: 41, of which 14 were waited for; matrix products, arithmetic and copies ran while one was open for 1% of the time, Pallas kernels for 15%

profile of v1, /device:TPU:8, one launch (start us, length us, event | category | flops | bytes accessed | tf_op | source)
XLA Modules:
  0.0 186.4 jit_solution(17746132646633977533)
XLA Ops:
  0.6 4.7 %collective-permute-start.2 = (bf16[32,1152]{1,0:T(8,128)(2,1)}, bf16[32,1152]{1,0:T(8,128)(2,1)S(1)}, u32[]{:S(2)}, u32[]{:S(2)}) collective-permute-start(bf16[32,1152]{1,0:T(8,128)(2,1)} %param.6), channel_id=1, source_target_pairs={{0,24},{8,0},{16,8},{24,16},{1,25},{9,1},{17,9},{25,17},{2,26},{10... | collective-permute-start | bytes 221192 | tf_op jit(solution)/shard_map/ppermute | solution.py:30
  6.0 2.3 %collective-permute-done.2 = bf16[32,1152]{1,0:T(8,128)(2,1)S(1)} collective-permute-done((bf16[32,1152]{1,0:T(8,128)(2,1)}, bf16[32,1152]{1,0:T(8,128)(2,1)S(1)}, u32[]{:S(2)}, u32[]{:S(2)}) %collective-permute-start.2) | collective-permute-done | bytes 73760 | tf_op jit(solution)/shard_map/ppermute | solution.py:30
  8.3 4.2 %collective-permute-done.1 = bf16[32,1152]{1,0:T(8,128)(2,1)S(1)} collective-permute-done((bf16[32,1152]{1,0:T(8,128)(2,1)}, bf16[32,1152]{1,0:T(8,128)(2,1)S(1)}, u32[]{:S(2)}, u32[]{:S(2)}) %collective-permute-start.1) | collective-permute-done | bytes 73760 | tf_op jit(solution)/shard_map/ppermute | solution.py:30
  15.0 2.7 %collective-permute-start.4 = (bf16[4,32,1152]{2,1,0:T(8,128)(2,1)S(1)}, bf16[4,32,1152]{2,1,0:T(8,128)(2,1)S(1)}, u32[]{:S(2)}, u32[]{:S(2)}) collective-permute-start(bf16[4,32,1152]{2,1,0:T(8,128)(2,1)S(1)} %pad_maximum_fusion.2.refs_0_), channel_id=1, source_target_pairs={{0,4},{2,6},{4,0},{6,2},{1,5},{3,7},{5,1},{7,3},{8,12},{10,14},{12... | collective-permute-start | bytes 884744 | tf_op jit(solution)/shard_map/ppermute | solution.py:30
  19.3 4.4 %collective-permute-done.3.refs_1_ = bf16[4,32,1152]{2,1,0:T(8,128)(2,1)S(1)} collective-permute-done((bf16[4,32,1152]{2,1,0:T(8,128)(2,1)S(1)}, bf16[4,32,1152]{2,1,0:T(8,128)(2,1)S(1)}, u32[]{:S(2)}, u32[]{:S(2)}) %collective-permute-start.3) | collective-permute-done | bytes 294944 | tf_op jit(solution)/shard_map/ppermute | solution.py:30
  23.7 7.3 %collective-permute-done.4.refs_2_ = bf16[4,32,1152]{2,1,0:T(8,128)(2,1)S(1)} collective-permute-done((bf16[4,32,1152]{2,1,0:T(8,128)(2,1)S(1)}, bf16[4,32,1152]{2,1,0:T(8,128)(2,1)S(1)}, u32[]{:S(2)}, u32[]{:S(2)}) %collective-permute-start.4) | collective-permute-done | bytes 294944 | tf_op jit(solution)/shard_map/ppermute | solution.py:30
  31.0 2.2 %shard_map.76.half.refs_5_ = bf16[2,4,2,32,1152]{4,3,2,1,0:T(8,128)(2,1)} custom-call(s32[5]{0:T(128)S(1)} %stack.67.where.refs_0_, bf16[4,32,1152]{2,1,0:T(8,128)(2,1)S(1)} %pad_maximum_fusion.2.refs_0_, bf16[4,32,1152]{2,1,0:T(8,128)(2,1)S(1)} %collective-permute-done.3.refs_1_, bf16[4,32,1152]{2,1,0:T(8,128)(2,1)S(1)} %collective-permute-done.4.refs_2_, ...), custom_call_target="tpu_custom_call" | custom-call | bytes 1179648 | tf_op jit(solution)/shard_map/pallas_call | solution.py:58
  34.2 3.9 %collective-permute-done.32 = bf16[32,1152]{1,0:T(8,128)(2,1)S(1)} collective-permute-done((bf16[32,1152]{1,0:T(8,128)(2,1)}, bf16[32,1152]{1,0:T(8,128)(2,1)S(1)}, u32[]{:S(2)}, u32[]{:S(2)}) %collective-permute-start.32) | collective-permute-done | bytes 73760 | tf_op jit(solution)/shard_map/ppermute | solution.py:35
  40.3 3.3 %shard_map.77 = (bf16[2,4,64,1152]{3,2,1,0:T(8,128)(2,1)S(1)}, f32[2,64,1152]{2,1,0:T(8,128)S(1)}) custom-call(bf16[2,4,2,32,1152]{4,3,2,1,0:T(8,128)(2,1)} %shard_map.76.half.refs_5_, bf16[1152,1152]{1,0:T(8,128)(2,1)S(1)} %copy-done), custom_call_target="tpu_custom_call" | custom-call | flops 1358954496 | bytes 3833856 | tf_op jit(solution)/shard_map/pallas_call | solution.py:58
  43.7 2.4 %shard_map.79 = (f32[128,1152]{1,0:T(8,128)S(1)}, bf16[128,1152]{1,0:T(8,128)(2,1)S(1)}, bf16[128,1152]{1,0:T(8,128)(2,1)S(1)}, bf16[128,1152]{1,0:T(8,128)(2,1)S(1)}) custom-call(bf16[2,4,2,32,1152]{4,3,2,1,0:T(8,128)(2,1)} %collective-permute-done.6.refs_0_.refs_6_, bf16[1152,1152]{1,0:T(8,128)(2,1)S(1)} %copy-done, ...), custom_call_target="tpu_custom_call" | custom-call | flops 679477248 | bytes 5308416 | tf_op jit(solution)/shard_map/pallas_call | solution.py:58
  46.6 2.6 %collective-permute-start.11 = (bf16[128,1152]{1,0:T(8,128)(2,1)S(1)}, bf16[128,1152]{1,0:T(8,128)(2,1)S(1)}, u32[]{:S(2)}, u32[]{:S(2)}) collective-permute-start(bf16[128,1152]{1,0:T(8,128)(2,1)S(1)} %get-tuple-element.37), channel_id=1, source_target_pairs={{0,64},{32,96},{64,0},{96,32},{1,65},{33,97},{65,1},{97,33},{2,66}... | collective-permute-start | bytes 884744 | tf_op jit(solution)/shard_map/ppermute | solution.py:30
  52.7 2.4 %shard_map.78 = (f32[128,1152]{1,0:T(8,128)S(1)}, bf16[128,1152]{1,0:T(8,128)(2,1)S(1)}, bf16[128,1152]{1,0:T(8,128)(2,1)S(1)}, bf16[128,1152]{1,0:T(8,128)(2,1)S(1)}) custom-call(bf16[2,4,2,32,1152]{4,3,2,1,0:T(8,128)(2,1)} %collective-permute-done.6.refs_0_.refs_6_, bf16[1152,1152]{1,0:T(8,128)(2,1)S(1)} %copy-done, ...), custom_call_target="tpu_custom_call" | custom-call | flops 679477248 | bytes 5308416 | tf_op jit(solution)/shard_map/pallas_call | solution.py:58
  55.3 10.4 %collective-permute-start.8 = (bf16[128,1152]{1,0:T(8,128)(2,1)S(1)}, bf16[128,1152]{1,0:T(8,128)(2,1)S(1)}, u32[]{:S(2)}, u32[]{:S(2)}) collective-permute-start(bf16[128,1152]{1,0:T(8,128)(2,1)S(1)} %get-tuple-element.33), channel_id=1, source_target_pairs={{0,64},{32,96},{64,0},{96,32},{1,65},{33,97},{65,1},{97,33},{2,66}... | collective-permute-start | bytes 884744 | tf_op jit(solution)/shard_map/ppermute | solution.py:30
  65.9 5.6 %collective-permute-start.13 = (bf16[128,1152]{1,0:T(8,128)(2,1)S(1)}, bf16[128,1152]{1,0:T(8,128)(2,1)S(1)}, u32[]{:S(2)}, u32[]{:S(2)}) collective-permute-start(bf16[128,1152]{1,0:T(8,128)(2,1)S(1)} %add_convert_fusion), channel_id=1, source_target_pairs={{0,128},{128,0},{1,129},{129,1},{2,130},{130,2},{3,131},{131,3},{4... | collective-permute-start | bytes 884744 | tf_op jit(solution)/shard_map/ppermute | solution.py:39
  73.7 2.9 %collective-permute-start.35 = (bf16[2,4,32,1152]{3,2,1,0:T(8,128)(2,1)S(1)}, bf16[2,4,32,1152]{3,2,1,0:T(8,128)(2,1)S(1)}, u32[]{:S(2)}, u32[]{:S(2)}) collective-permute-start(bf16[2,4,32,1152]{3,2,1,0:T(8,128)(2,1)S(1)} %pad_maximum_fusion.near), channel_id=1, source_target_pairs={{0,4},{2,6},{4,0},{6,2},{1,5},{3,7},{5,1},{7,3},{8,12},{10,14},{12... | collective-permute-start | bytes 1769480 | tf_op jit(solution)/shard_map/ppermute | solution.py:35
  78.3 5.6 %collective-permute-start.21 = (bf16[128,1152]{1,0:T(8,128)(2,1)S(1)}, bf16[128,1152]{1,0:T(8,128)(2,1)S(1)}, u32[]{:S(2)}, u32[]{:S(2)}) collective-permute-start(bf16[128,1152]{1,0:T(8,128)(2,1)S(1)} %fusion.7.p0.refs_1_), channel_id=1, source_target_pairs={{0,128},{128,0},{1,129},{129,1},{2,130},{130,2},{3,131},{131,3},{4... | collective-permute-start | bytes 884744 | tf_op jit(solution)/shard_map/ppermute | solution.py:39
  83.9 8.0 %collective-permute-start.14 = (bf16[128,1152]{1,0:T(8,128)(2,1)S(1)}, bf16[128,1152]{1,0:T(8,128)(2,1)S(1)}, u32[]{:S(2)}, u32[]{:S(2)}) collective-permute-start(bf16[128,1152]{1,0:T(8,128)(2,1)S(1)} %fusion.7.p0.refs_1_), channel_id=1, source_target_pairs={{0,96},{32,0},{64,32},{96,64},{1,97},{33,1},{65,33},{97,65},{2,98}... | collective-permute-start | bytes 884744 | tf_op jit(solution)/shard_map/ppermute | solution.py:30
  93.7 5.9 %collective-permute-start.22 = (bf16[128,1152]{1,0:T(8,128)(2,1)S(1)}, bf16[128,1152]{1,0:T(8,128)(2,1)S(1)}, u32[]{:S(2)}, u32[]{:S(2)}) collective-permute-start(bf16[128,1152]{1,0:T(8,128)(2,1)S(1)} %collective-permute-done.21.p0.refs_5_), channel_id=1, source_target_pairs={{0,96},{32,0},{64,32},{96,64},{1,97},{33,1},{65,33},{97,65},{2,98}... | collective-permute-start | bytes 884744 | tf_op jit(solution)/shard_map/ppermute | solution.py:30
  99.6 3.4 %collective-permute-start.23 = (bf16[128,1152]{1,0:T(8,128)(2,1)S(1)}, bf16[128,1152]{1,0:T(8,128)(2,1)S(1)}, u32[]{:S(2)}, u32[]{:S(2)}) collective-permute-start(bf16[128,1152]{1,0:T(8,128)(2,1)S(1)} %collective-permute-done.21.p0.refs_5_), channel_id=1, source_target_pairs={{0,64},{32,96},{64,0},{96,32},{1,65},{33,97},{65,1},{97,33},{2,66}... | collective-permute-start | bytes 884744 | tf_op jit(solution)/shard_map/ppermute | solution.py:30
  102.9 2.6 %collective-permute-done.15.p2.refs_3_ = bf16[128,1152]{1,0:T(8,128)(2,1)S(1)} collective-permute-done((bf16[128,1152]{1,0:T(8,128)(2,1)S(1)}, bf16[128,1152]{1,0:T(8,128)(2,1)S(1)}, u32[]{:S(2)}, u32[]{:S(2)}) %collective-permute-start.15) | collective-permute-done | bytes 294944 | tf_op jit(solution)/shard_map/ppermute | solution.py:30
  107.3 2.8 %shard_map.80 = (bf16[4,2,32,1152]{3,2,1,0:T(8,128)(2,1)S(1)}, f32[4,2,32,1152]{3,2,1,0:T(8,128)S(1)}) custom-call(s32[5]{0:T(128)S(1)} %stack.67.where.refs_0_, bf16[128,1152]{1,0:T(8,128)(2,1)S(1)} %fusion.7.p0.refs_1_, bf16[128,1152]{1,0:T(8,128)(2,1)S(1)} %collective-permute-done.14.p1.refs_2_, bf16[128,1152]{1,0:T(8,128)(2,1)S(1)} %collective-permute-done.15.p2.refs_3_, ...), custom_call_target="tpu_custom_call" | custom-call | flops 1358954496 | bytes 3833856 | tf_op jit(solution)/shard_map/pallas_call | solution.py:58
  112.9 2.8 %shard_map.82 = (bf16[4,2,32,1152]{3,2,1,0:T(8,128)(2,1)S(1)}, f32[4,2,32,1152]{3,2,1,0:T(8,128)S(1)}) custom-call(s32[5]{0:T(128)S(1)} %stack.67.where.refs_0_, bf16[128,1152]{1,0:T(8,128)(2,1)S(1)} %collective-permute-done.21.p0.refs_5_, bf16[128,1152]{1,0:T(8,128)(2,1)S(1)} %collective-permute-done.22.p1.refs_6_, ...), custom_call_target="tpu_custom_call" | custom-call | flops 1358954496 | bytes 3833856 | tf_op jit(solution)/shard_map/pallas_call | solution.py:58
  116.1 3.5 %collective-permute-start.38 = (bf16[2,128,1152]{2,1,0:T(8,128)(2,1)S(1)}, bf16[2,128,1152]{2,1,0:T(8,128)(2,1)S(1)}, u32[]{:S(2)}, u32[]{:S(2)}) collective-permute-start(bf16[2,128,1152]{2,1,0:T(8,128)(2,1)S(1)} %pad_maximum_fusion.1.refs_1_), channel_id=1, source_target_pairs={{0,64},{32,96},{64,0},{96,32},{1,65},{33,97},{65,1},{97,33},{2,66}... | collective-permute-start | bytes 1769480 | tf_op jit(solution)/shard_map/ppermute | solution.py:35
  121.2 5.9 %collective-permute-start.18 = (bf16[2,32,1152]{2,1,0:T(8,128)(2,1)S(1)}, bf16[2,32,1152]{2,1,0:T(8,128)(2,1)S(1)}, u32[]{:S(2)}, u32[]{:S(2)}) collective-permute-start(bf16[2,32,1152]{2,1,0:T(8,128)(2,1)S(1)} %get-tuple-element.42), channel_id=1, source_target_pairs={{0,2},{2,4},{4,6},{6,0},{1,3},{3,5},{5,7},{7,1},{8,10},{10,12},{12... | collective-permute-start | bytes 442376 | tf_op jit(solution)/shard_map/ppermute | solution.py:30
  127.1 2.3 %collective-permute-start.19 = (bf16[2,32,1152]{2,1,0:T(8,128)(2,1)S(1)}, bf16[2,32,1152]{2,1,0:T(8,128)(2,1)S(1)}, u32[]{:S(2)}, u32[]{:S(2)}) collective-permute-start(bf16[2,32,1152]{2,1,0:T(8,128)(2,1)S(1)} %get-tuple-element.43), channel_id=1, source_target_pairs={{0,4},{2,6},{4,0},{6,2},{1,5},{3,7},{5,1},{7,3},{8,12},{10,14},{12... | collective-permute-start | bytes 442376 | tf_op jit(solution)/shard_map/ppermute | solution.py:30
  129.5 4.3 %collective-permute-done.38.refs_2_ = bf16[2,128,1152]{2,1,0:T(8,128)(2,1)S(1)} collective-permute-done((bf16[2,128,1152]{2,1,0:T(8,128)(2,1)S(1)}, bf16[2,128,1152]{2,1,0:T(8,128)(2,1)S(1)}, u32[]{:S(2)}, u32[]{:S(2)}) %collective-permute-start.38) | collective-permute-done | bytes 589856 | tf_op jit(solution)/shard_map/ppermute | solution.py:35
  133.9 2.3 %collective-permute-start.20 = (bf16[2,32,1152]{2,1,0:T(8,128)(2,1)S(1)}, bf16[2,32,1152]{2,1,0:T(8,128)(2,1)S(1)}, u32[]{:S(2)}, u32[]{:S(2)}) collective-permute-start(bf16[2,32,1152]{2,1,0:T(8,128)(2,1)S(1)} %get-tuple-element.44), channel_id=1, source_target_pairs={{0,6},{2,0},{4,2},{6,4},{1,7},{3,1},{5,3},{7,5},{8,14},{10,8},{12,... | collective-permute-start | bytes 442376 | tf_op jit(solution)/shard_map/ppermute | solution.py:30
  136.1 9.9 %collective-permute-done.40.refs_4_ = bf16[2,128,1152]{2,1,0:T(8,128)(2,1)S(1)} collective-permute-done((bf16[2,128,1152]{2,1,0:T(8,128)(2,1)S(1)}, bf16[2,128,1152]{2,1,0:T(8,128)(2,1)S(1)}, u32[]{:S(2)}, u32[]{:S(2)}) %collective-permute-start.40) | collective-permute-done | bytes 589856 | tf_op jit(solution)/shard_map/ppermute | solution.py:35
  147.3 2.4 %collective-permute-start.27 = (bf16[2,32,1152]{2,1,0:T(8,128)(2,1)S(1)}, bf16[2,32,1152]{2,1,0:T(8,128)(2,1)S(1)}, u32[]{:S(2)}, u32[]{:S(2)}) collective-permute-start(bf16[2,32,1152]{2,1,0:T(8,128)(2,1)S(1)} %get-tuple-element.49), channel_id=1, source_target_pairs={{0,4},{2,6},{4,0},{6,2},{1,5},{3,7},{5,1},{7,3},{8,12},{10,14},{12... | collective-permute-start | bytes 442376 | tf_op jit(solution)/shard_map/ppermute | solution.py:30
  151.3 7.5 %shard_map.87 = bf16[1152,1152]{1,0:T(8,128)(2,1)} custom-call(s32[5]{0:T(128)S(1)} %stack.67.where.refs_0_, bf16[2,128,1152]{2,1,0:T(8,128)(2,1)S(1)} %pad_maximum_fusion.1.refs_1_, bf16[2,128,1152]{2,1,0:T(8,128)(2,1)S(1)} %collective-permute-done.38.refs_2_, bf16[2,128,1152]{2,1,0:T(8,128)(2,1)S(1)} %collective-permute-done.39.refs_3_, ...), custom_call_target="tpu_custom_call" | custom-call | flops 2717908992 | bytes 4718592 | tf_op jit(solution)/shard_map/pallas_call | solution.py:58
  161.1 18.1 %collective-permute-start.30 = (bf16[32,1152]{1,0:T(8,128)(2,1)S(1)}, bf16[32,1152]{1,0:T(8,128)(2,1)S(1)}, u32[]{:S(2)}, u32[]{:S(2)}) collective-permute-start(bf16[32,1152]{1,0:T(8,128)(2,1)S(1)} %get-tuple-element.53), channel_id=1, source_target_pairs={{0,16},{8,24},{16,0},{24,8},{1,17},{9,25},{17,1},{25,9},{2,18},{10... | collective-permute-start | bytes 221192 | tf_op jit(solution)/shard_map/ppermute | solution.py:30
  180.3 5.4 %shard_map.86 = bf16[1152,1152]{1,0:T(8,128)(2,1)} custom-call(s32[5]{0:T(128)S(1)} %stack.67.where.refs_0_, bf16[128,1152]{1,0:T(8,128)(2,1)S(1)} %fusion.7.p0.refs_1_, bf16[128,1152]{1,0:T(8,128)(2,1)S(1)} %collective-permute-done.14.p1.refs_2_, bf16[128,1152]{1,0:T(8,128)(2,1)S(1)} %collective-permute-done.15.p2.refs_3_, ...), custom_call_target="tpu_custom_call" | custom-call | flops 2717908992 | bytes 4718592 | tf_op jit(solution)/shard_map/pallas_call | solution.py:58
  (79 shorter events, 31.5 us)
Async XLA Ops:
  15.0 15.9 %collective-permute-start.4 = (bf16[4,32,1152]{2,1,0:T(8,128)(2,1)S(1)}, bf16[4,32,1152]{2,1,0:T(8,128)(2,1)S(1)}, u32[]{:S(2)}, u32[]{:S(2)}) collective-permute-start(bf16[4,32,1152]{2,1,0:T(8,128)(2,1)S(1)} %pad_maximum_fusion.2.refs_0_), channel_id=1, source_target_pairs={{0,4},{2,6},{4,0},{6,2},{1,5},{3,7},{5,1},{7,3},{8,12},{10,14},{12... | collective-permute-start | bytes 884744 | tf_op jit(solution)/shard_map/ppermute | solution.py:30
  17.8 13.2 %collective-permute-start.5 = (bf16[4,32,1152]{2,1,0:T(8,128)(2,1)S(1)}, bf16[4,32,1152]{2,1,0:T(8,128)(2,1)}, u32[]{:S(2)}, u32[]{:S(2)}) collective-permute-start(bf16[4,32,1152]{2,1,0:T(8,128)(2,1)S(1)} %pad_maximum_fusion.2.refs_0_), channel_id=1, source_target_pairs={{0,6},{2,0},{4,2},{6,4},{1,7},{3,1},{5,3},{7,5},{8,14},{10,8},{12,... | collective-permute-start | bytes 884744 | tf_op jit(solution)/shard_map/ppermute | solution.py:30
  33.1 10.5 %collective-permute-start.6 = (bf16[2,4,2,32,1152]{4,3,2,1,0:T(8,128)(2,1)}, bf16[2,4,2,32,1152]{4,3,2,1,0:T(8,128)(2,1)}, u32[]{:S(2)}, u32[]{:S(2)}) collective-permute-start(bf16[2,4,2,32,1152]{4,3,2,1,0:T(8,128)(2,1)} %shard_map.76.half.refs_5_), channel_id=1, source_target_pairs={{0,1},{1,0},{2,3},{3,2},{4,5},{5,4},{6,7},{7,6},{8,9},{9,8},{10,11... | collective-permute-start | bytes 3538952 | tf_op jit(solution)/shard_map/ppermute | solution.py:39
  38.9 12.1 %collective-permute-start.33 = (bf16[2,32,1152]{2,1,0:T(8,128)(2,1)S(1)}, bf16[2,32,1152]{2,1,0:T(8,128)(2,1)S(1)}, u32[]{:S(2)}, u32[]{:S(2)}) collective-permute-start(bf16[2,32,1152]{2,1,0:T(8,128)(2,1)S(1)} %pad_maximum_fusion.5), channel_id=1, source_target_pairs={{0,16},{8,24},{16,0},{24,8},{1,17},{9,25},{17,1},{25,9},{2,18},{10... | collective-permute-start | bytes 442376 | tf_op jit(solution)/shard_map/ppermute | solution.py:35
  46.6 19.1 %collective-permute-start.11 = (bf16[128,1152]{1,0:T(8,128)(2,1)S(1)}, bf16[128,1152]{1,0:T(8,128)(2,1)S(1)}, u32[]{:S(2)}, u32[]{:S(2)}) collective-permute-start(bf16[128,1152]{1,0:T(8,128)(2,1)S(1)} %get-tuple-element.37), channel_id=1, source_target_pairs={{0,64},{32,96},{64,0},{96,32},{1,65},{33,97},{65,1},{97,33},{2,66}... | collective-permute-start | bytes 884744 | tf_op jit(solution)/shard_map/ppermute | solution.py:30
  49.2 16.5 %collective-permute-start.10 = (bf16[128,1152]{1,0:T(8,128)(2,1)S(1)}, bf16[128,1152]{1,0:T(8,128)(2,1)S(1)}, u32[]{:S(2)}, u32[]{:S(2)}) collective-permute-start(bf16[128,1152]{1,0:T(8,128)(2,1)S(1)} %get-tuple-element.36), channel_id=1, source_target_pairs={{0,32},{32,64},{64,96},{96,0},{1,33},{33,65},{65,97},{97,1},{2,34}... | collective-permute-start | bytes 884744 | tf_op jit(solution)/shard_map/ppermute | solution.py:30
  51.1 20.4 %collective-permute-start.34 = (bf16[4,32,1152]{2,1,0:T(8,128)(2,1)S(1)}, bf16[4,32,1152]{2,1,0:T(8,128)(2,1)S(1)}, u32[]{:S(2)}, u32[]{:S(2)}) collective-permute-start(bf16[4,32,1152]{2,1,0:T(8,128)(2,1)S(1)} %get-tuple-element.56), channel_id=1, source_target_pairs={{0,2},{2,0},{4,6},{6,4},{1,3},{3,1},{5,7},{7,5},{8,10},{10,8},{12,... | collective-permute-start | bytes 884744 | tf_op jit(solution)/shard_map/ppermute | solution.py:35
  55.0 18.7 %collective-permute-start.9 = (bf16[128,1152]{1,0:T(8,128)(2,1)S(1)}, bf16[128,1152]{1,0:T(8,128)(2,1)S(1)}, u32[]{:S(2)}, u32[]{:S(2)}) collective-permute-start(bf16[128,1152]{1,0:T(8,128)(2,1)S(1)} %get-tuple-element.34), channel_id=1, source_target_pairs={{0,96},{32,0},{64,32},{96,64},{1,97},{33,1},{65,33},{97,65},{2,98}... | collective-permute-start | bytes 884744 | tf_op jit(solution)/shard_map/ppermute | solution.py:30
  55.3 21.4 %collective-permute-start.8 = (bf16[128,1152]{1,0:T(8,128)(2,1)S(1)}, bf16[128,1152]{1,0:T(8,128)(2,1)S(1)}, u32[]{:S(2)}, u32[]{:S(2)}) collective-permute-start(bf16[128,1152]{1,0:T(8,128)(2,1)S(1)} %get-tuple-element.33), channel_id=1, source_target_pairs={{0,64},{32,96},{64,0},{96,32},{1,65},{33,97},{65,1},{97,33},{2,66}... | collective-permute-start | bytes 884744 | tf_op jit(solution)/shard_map/ppermute | solution.py:30
  65.7 11.2 %collective-permute-start.7 = (bf16[128,1152]{1,0:T(8,128)(2,1)S(1)}, bf16[128,1152]{1,0:T(8,128)(2,1)S(1)}, u32[]{:S(2)}, u32[]{:S(2)}) collective-permute-start(bf16[128,1152]{1,0:T(8,128)(2,1)S(1)} %get-tuple-element.32), channel_id=1, source_target_pairs={{0,32},{32,64},{64,96},{96,0},{1,33},{33,65},{65,97},{97,1},{2,34}... | collective-permute-start | bytes 884744 | tf_op jit(solution)/shard_map/ppermute | solution.py:30
  65.9 12.0 %collective-permute-start.13 = (bf16[128,1152]{1,0:T(8,128)(2,1)S(1)}, bf16[128,1152]{1,0:T(8,128)(2,1)S(1)}, u32[]{:S(2)}, u32[]{:S(2)}) collective-permute-start(bf16[128,1152]{1,0:T(8,128)(2,1)S(1)} %add_convert_fusion), channel_id=1, source_target_pairs={{0,128},{128,0},{1,129},{129,1},{2,130},{130,2},{3,131},{131,3},{4... | collective-permute-start | bytes 884744 | tf_op jit(solution)/shard_map/ppermute | solution.py:39
  71.5 20.4 %collective-permute-start.37 = (bf16[128,1152]{1,0:T(8,128)(2,1)S(1)}, bf16[128,1152]{1,0:T(8,128)(2,1)S(1)}, u32[]{:S(2)}, u32[]{:S(2)}) collective-permute-start(bf16[128,1152]{1,0:T(8,128)(2,1)S(1)} %bitcast.35), channel_id=1, source_target_pairs={{0,32},{32,0},{64,96},{96,64},{1,33},{33,1},{65,97},{97,65},{2,34}... | collective-permute-start | bytes 884744 | tf_op jit(solution)/shard_map/ppermute | solution.py:35
  73.7 19.7 %collective-permute-start.35 = (bf16[2,4,32,1152]{3,2,1,0:T(8,128)(2,1)S(1)}, bf16[2,4,32,1152]{3,2,1,0:T(8,128)(2,1)S(1)}, u32[]{:S(2)}, u32[]{:S(2)}) collective-permute-start(bf16[2,4,32,1152]{3,2,1,0:T(8,128)(2,1)S(1)} %pad_maximum_fusion.near), channel_id=1, source_target_pairs={{0,4},{2,6},{4,0},{6,2},{1,5},{3,7},{5,1},{7,3},{8,12},{10,14},{12... | collective-permute-start | bytes 1769480 | tf_op jit(solution)/shard_map/ppermute | solution.py:35
  78.3 15.4 %collective-permute-start.21 = (bf16[128,1152]{1,0:T(8,128)(2,1)S(1)}, bf16[128,1152]{1,0:T(8,128)(2,1)S(1)}, u32[]{:S(2)}, u32[]{:S(2)}) collective-permute-start(bf16[128,1152]{1,0:T(8,128)(2,1)S(1)} %fusion.7.p0.refs_1_), channel_id=1, source_target_pairs={{0,128},{128,0},{1,129},{129,1},{2,130},{130,2},{3,131},{131,3},{4... | collective-permute-start | bytes 884744 | tf_op jit(solution)/shard_map/ppermute | solution.py:39
  83.9 15.7 %collective-permute-start.14 = (bf16[128,1152]{1,0:T(8,128)(2,1)S(1)}, bf16[128,1152]{1,0:T(8,128)(2,1)S(1)}, u32[]{:S(2)}, u32[]{:S(2)}) collective-permute-start(bf16[128,1152]{1,0:T(8,128)(2,1)S(1)} %fusion.7.p0.refs_1_), channel_id=1, source_target_pairs={{0,96},{32,0},{64,32},{96,64},{1,97},{33,1},{65,33},{97,65},{2,98}... | collective-permute-start | bytes 884744 | tf_op jit(solution)/shard_map/ppermute | solution.py:30
  91.9 13.6 %collective-permute-start.15 = (bf16[128,1152]{1,0:T(8,128)(2,1)S(1)}, bf16[128,1152]{1,0:T(8,128)(2,1)S(1)}, u32[]{:S(2)}, u32[]{:S(2)}) collective-permute-start(bf16[128,1152]{1,0:T(8,128)(2,1)S(1)} %fusion.7.p0.refs_1_), channel_id=1, source_target_pairs={{0,64},{32,96},{64,0},{96,32},{1,65},{33,97},{65,1},{97,33},{2,66}... | collective-permute-start | bytes 884744 | tf_op jit(solution)/shard_map/ppermute | solution.py:30
  91.9 15.4 %collective-permute-start.16 = (bf16[128,1152]{1,0:T(8,128)(2,1)S(1)}, bf16[128,1152]{1,0:T(8,128)(2,1)S(1)}, u32[]{:S(2)}, u32[]{:S(2)}) collective-permute-start(bf16[128,1152]{1,0:T(8,128)(2,1)S(1)} %fusion.7.p0.refs_1_), channel_id=1, source_target_pairs={{0,32},{32,64},{64,96},{96,0},{1,33},{33,65},{65,97},{97,1},{2,34}... | collective-permute-start | bytes 884744 | tf_op jit(solution)/shard_map/ppermute | solution.py:30
  93.4 27.6 %collective-permute-start.39 = (bf16[2,128,1152]{2,1,0:T(8,128)(2,1)S(1)}, bf16[2,128,1152]{2,1,0:T(8,128)(2,1)S(1)}, u32[]{:S(2)}, u32[]{:S(2)}) collective-permute-start(bf16[2,128,1152]{2,1,0:T(8,128)(2,1)S(1)} %pad_maximum_fusion.1.refs_1_), channel_id=1, source_target_pairs={{0,128},{128,0},{1,129},{129,1},{2,130},{130,2},{3,131},{131,3},{4... | collective-permute-start | bytes 1769480 | tf_op jit(solution)/shard_map/ppermute | solution.py:39
  93.7 16.4 %collective-permute-start.22 = (bf16[128,1152]{1,0:T(8,128)(2,1)S(1)}, bf16[128,1152]{1,0:T(8,128)(2,1)S(1)}, u32[]{:S(2)}, u32[]{:S(2)}) collective-permute-start(bf16[128,1152]{1,0:T(8,128)(2,1)S(1)} %collective-permute-done.21.p0.refs_5_), channel_id=1, source_target_pairs={{0,96},{32,0},{64,32},{96,64},{1,97},{33,1},{65,33},{97,65},{2,98}... | collective-permute-start | bytes 884744 | tf_op jit(solution)/shard_map/ppermute | solution.py:30
  99.6 13.2 %collective-permute-start.23 = (bf16[128,1152]{1,0:T(8,128)(2,1)S(1)}, bf16[128,1152]{1,0:T(8,128)(2,1)S(1)}, u32[]{:S(2)}, u32[]{:S(2)}) collective-permute-start(bf16[128,1152]{1,0:T(8,128)(2,1)S(1)} %collective-permute-done.21.p0.refs_5_), channel_id=1, source_target_pairs={{0,64},{32,96},{64,0},{96,32},{1,65},{33,97},{65,1},{97,33},{2,66}... | collective-permute-start | bytes 884744 | tf_op jit(solution)/shard_map/ppermute | solution.py:30
  107.3 73.0 %collective-permute-start.36 = (bf16[2,4,2,32,1152]{4,3,2,1,0:T(8,128)(2,1)S(1)}, bf16[2,4,2,32,1152]{4,3,2,1,0:T(8,128)(2,1)S(1)}, u32[]{:S(2)}, u32[]{:S(2)}) collective-permute-start(bf16[2,4,2,32,1152]{4,3,2,1,0:T(8,128)(2,1)S(1)} %shard_map.85.refs_9_), channel_id=1, source_target_pairs={{0,1},{1,0},{2,3},{3,2},{4,5},{5,4},{6,7},{7,6},{8,9},{9,8},{10,11... | collective-permute-start | bytes 3538952 | tf_op jit(solution)/shard_map/ppermute | solution.py:39
  110.1 10.9 %collective-permute-start.17 = (bf16[4,2,32,1152]{3,2,1,0:T(8,128)(2,1)S(1)}, bf16[4,2,32,1152]{3,2,1,0:T(8,128)(2,1)S(1)}, u32[]{:S(2)}, u32[]{:S(2)}) collective-permute-start(bf16[4,2,32,1152]{3,2,1,0:T(8,128)(2,1)S(1)} %get-tuple-element.40), channel_id=1, source_target_pairs={{0,1},{1,0},{2,3},{3,2},{4,5},{5,4},{6,7},{7,6},{8,9},{9,8},{10,11... | collective-permute-start | bytes 1769480 | tf_op jit(solution)/shard_map/ppermute | solution.py:39
  115.7 11.4 %collective-permute-start.25 = (bf16[4,2,32,1152]{3,2,1,0:T(8,128)(2,1)S(1)}, bf16[4,2,32,1152]{3,2,1,0:T(8,128)(2,1)S(1)}, u32[]{:S(2)}, u32[]{:S(2)}) collective-permute-start(bf16[4,2,32,1152]{3,2,1,0:T(8,128)(2,1)S(1)} %get-tuple-element.46), channel_id=1, source_target_pairs={{0,1},{1,0},{2,3},{3,2},{4,5},{5,4},{6,7},{7,6},{8,9},{9,8},{10,11... | collective-permute-start | bytes 1769480 | tf_op jit(solution)/shard_map/ppermute | solution.py:39
  116.1 17.8 %collective-permute-start.38 = (bf16[2,128,1152]{2,1,0:T(8,128)(2,1)S(1)}, bf16[2,128,1152]{2,1,0:T(8,128)(2,1)S(1)}, u32[]{:S(2)}, u32[]{:S(2)}) collective-permute-start(bf16[2,128,1152]{2,1,0:T(8,128)(2,1)S(1)} %pad_maximum_fusion.1.refs_1_), channel_id=1, source_target_pairs={{0,64},{32,96},{64,0},{96,32},{1,65},{33,97},{65,1},{97,33},{2,66}... | collective-permute-start | bytes 1769480 | tf_op jit(solution)/shard_map/ppermute | solution.py:35
  121.0 25.0 %collective-permute-start.40 = (bf16[2,128,1152]{2,1,0:T(8,128)(2,1)S(1)}, bf16[2,128,1152]{2,1,0:T(8,128)(2,1)S(1)}, u32[]{:S(2)}, u32[]{:S(2)}) collective-permute-start(bf16[2,128,1152]{2,1,0:T(8,128)(2,1)S(1)} %collective-permute-done.39.refs_3_), channel_id=1, source_target_pairs={{0,64},{32,96},{64,0},{96,32},{1,65},{33,97},{65,1},{97,33},{2,66}... | collective-permute-start | bytes 1769480 | tf_op jit(solution)/shard_map/ppermute | solution.py:35
  121.2 26.1 %collective-permute-start.18 = (bf16[2,32,1152]{2,1,0:T(8,128)(2,1)S(1)}, bf16[2,32,1152]{2,1,0:T(8,128)(2,1)S(1)}, u32[]{:S(2)}, u32[]{:S(2)}) collective-permute-start(bf16[2,32,1152]{2,1,0:T(8,128)(2,1)S(1)} %get-tuple-element.42), channel_id=1, source_target_pairs={{0,2},{2,4},{4,6},{6,0},{1,3},{3,5},{5,7},{7,1},{8,10},{10,12},{12... | collective-permute-start | bytes 442376 | tf_op jit(solution)/shard_map/ppermute | solution.py:30
  127.1 22.6 %collective-permute-start.19 = (bf16[2,32,1152]{2,1,0:T(8,128)(2,1)S(1)}, bf16[2,32,1152]{2,1,0:T(8,128)(2,1)S(1)}, u32[]{:S(2)}, u32[]{:S(2)}) collective-permute-start(bf16[2,32,1152]{2,1,0:T(8,128)(2,1)S(1)} %get-tuple-element.43), channel_id=1, source_target_pairs={{0,4},{2,6},{4,0},{6,2},{1,5},{3,7},{5,1},{7,3},{8,12},{10,14},{12... | collective-permute-start | bytes 442376 | tf_op jit(solution)/shard_map/ppermute | solution.py:30
  133.9 24.9 %collective-permute-start.20 = (bf16[2,32,1152]{2,1,0:T(8,128)(2,1)S(1)}, bf16[2,32,1152]{2,1,0:T(8,128)(2,1)S(1)}, u32[]{:S(2)}, u32[]{:S(2)}) collective-permute-start(bf16[2,32,1152]{2,1,0:T(8,128)(2,1)S(1)} %get-tuple-element.44), channel_id=1, source_target_pairs={{0,6},{2,0},{4,2},{6,4},{1,7},{3,1},{5,3},{7,5},{8,14},{10,8},{12,... | collective-permute-start | bytes 442376 | tf_op jit(solution)/shard_map/ppermute | solution.py:30
  146.1 12.7 %collective-permute-start.26 = (bf16[2,32,1152]{2,1,0:T(8,128)(2,1)S(1)}, bf16[2,32,1152]{2,1,0:T(8,128)(2,1)S(1)}, u32[]{:S(2)}, u32[]{:S(2)}) collective-permute-start(bf16[2,32,1152]{2,1,0:T(8,128)(2,1)S(1)} %get-tuple-element.48), channel_id=1, source_target_pairs={{0,2},{2,4},{4,6},{6,0},{1,3},{3,5},{5,7},{7,1},{8,10},{10,12},{12... | collective-permute-start | bytes 442376 | tf_op jit(solution)/shard_map/ppermute | solution.py:30
  147.3 11.5 %collective-permute-start.27 = (bf16[2,32,1152]{2,1,0:T(8,128)(2,1)S(1)}, bf16[2,32,1152]{2,1,0:T(8,128)(2,1)S(1)}, u32[]{:S(2)}, u32[]{:S(2)}) collective-permute-start(bf16[2,32,1152]{2,1,0:T(8,128)(2,1)S(1)} %get-tuple-element.49), channel_id=1, source_target_pairs={{0,4},{2,6},{4,0},{6,2},{1,5},{3,7},{5,1},{7,3},{8,12},{10,14},{12... | collective-permute-start | bytes 442376 | tf_op jit(solution)/shard_map/ppermute | solution.py:30
  159.5 26.2 %collective-permute-start.31 = (bf16[32,1152]{1,0:T(8,128)(2,1)S(1)}, bf16[32,1152]{1,0:T(8,128)(2,1)S(1)}, u32[]{:S(2)}, u32[]{:S(2)}) collective-permute-start(bf16[32,1152]{1,0:T(8,128)(2,1)S(1)} %get-tuple-element.54), channel_id=1, source_target_pairs={{0,24},{8,0},{16,8},{24,16},{1,25},{9,1},{17,9},{25,17},{2,26},{10... | collective-permute-start | bytes 221192 | tf_op jit(solution)/shard_map/ppermute | solution.py:30
  161.1 24.6 %collective-permute-start.30 = (bf16[32,1152]{1,0:T(8,128)(2,1)S(1)}, bf16[32,1152]{1,0:T(8,128)(2,1)S(1)}, u32[]{:S(2)}, u32[]{:S(2)}) collective-permute-start(bf16[32,1152]{1,0:T(8,128)(2,1)S(1)} %get-tuple-element.53), channel_id=1, source_target_pairs={{0,16},{8,24},{16,0},{24,8},{1,17},{9,25},{17,1},{25,9},{2,18},{10... | collective-permute-start | bytes 221192 | tf_op jit(solution)/shard_map/ppermute | solution.py:30
  (12 other events, 111.7 us)

commit v2 on v1

--- a/solution.py
+++ b/solution.py
@@ -243,49 +243,102 @@
 CHUNK = 384
 
 
-def outer(lefts, rights, out, stage, sem, factor):
+def outer(lefts, rights, columns_total, emit):
     dims = (((0,), (0,)), ((), ()))
 
-    def send(i):
-        start = pl.multiple_of(i * CHUNK, CHUNK)
-        return pltpu.make_async_copy(stage.at[i], out.at[pl.ds(start, CHUNK)], sem.at[i])
-
-    @pl.loop(0, out.shape[0] // CHUNK)
+    @pl.loop(0, columns_total // CHUNK)
     def _(i):
         columns = pl.ds(pl.multiple_of(i * CHUNK, CHUNK), CHUNK)
         total = sum(
             lax.dot_general(left(columns), right(), dims, preferred_element_type=F32)
             for left, right in zip(lefts, rights)
         )
+        emit(i, columns, total)
+
+
+def store_out(out, stage, sem, factor):
+    def send(i):
+        rows = pl.ds(pl.multiple_of(i * CHUNK, CHUNK), CHUNK)
+        return pltpu.make_async_copy(stage.at[i], out.at[rows], sem.at[i])
+
+    def emit(i, total):
         stage[i] = (total * factor).astype(BF16)
         send(i).start()
 
-    for i in range(out.shape[0] // CHUNK):
-        send(i).wait()
-
-
-def second_kernel(factor, where, *refs):
-    pieces, (own, other, out, act, stage, sem) = refs[:4], refs[4:]
+    def finish():
+        for i in range(out.shape[0] // CHUNK):
+            send(i).wait()
+
+    return emit, finish
+
+
+def stage_scratch(rows, width):
+    return [
+        pltpu.VMEM((rows // CHUNK, CHUNK, width), BF16),
+        pltpu.SemaphoreType.DMA((rows // CHUNK,)),
+    ]
+
+
+def second_kernel(plane, factor, where, *refs):
+    pieces, (own, other), refs = refs[:2], refs[2:4], refs[4:]
     rows = pieces[0].shape[1] // 2
     width = own.shape[-1]
+    act = refs[2] if plane else refs[1]
     y = where[1]
-    for i, piece in enumerate(pieces):
+    for high, piece in enumerate(pieces):
 
         @pl.loop(0, 4)
         def _(n):
             low, core = lax.div(n, 2), lax.rem(n, 2)
-            ay = lax.bitwise_xor(y, i % 2 * 2 + low)
-            block = core * 8 + i // 2 * 4 + lax.rem(ay + 4 - y, 4)
+            ay = lax.bitwise_xor(y, high * 2 + low)
+            block = core * 4 + lax.rem(ay + 4 - y, 4)
             values = piece[low, pl.ds(core * rows, rows)].astype(F32)
             act[pl.ds(block * rows, rows)] = gelu_value(values).astype(BF16)
 
-    half = 8 * rows
+    half = 4 * rows
     lefts = [lambda cols, n=n: act[n * half : (n + 1) * half, cols] for n in range(2)]
-    rights = [lambda h=h: h[...].reshape(-1, width) for h in (own, other)]
-    outer(lefts, rights, out, stage, sem, factor)
-
-
-def first_kernel(factor, where, *refs):
+    rights = [lambda h=h: h[plane].reshape(-1, width) for h in (own, other)]
+    if plane:
+        so_far, out, _, stage, sem = refs
+        emit, finish = store_out(out, stage, sem, factor)
+        outer(
+            lefts, rights, act.shape[1], lambda i, cols, t: emit(i, t + so_far[cols])
+        )
+        finish()
+    else:
+        total = refs[0]
+
+        def keep(i, cols, value):
+            total[cols] = value
+
+        outer(lefts, rights, act.shape[1], keep)
+
+
+def second_product(where, near, far, halves, factor):
+    rows, width = near[0].shape[1:]
+    out_width = halves[0].shape[-1]
+    flops = 8 * rows * width * out_width
+    act = pltpu.VMEM((4 * rows, width), BF16)
+    (total,) = call(
+        lambda *refs: second_kernel(0, factor, *refs),
+        [((width, out_width), F32)],
+        [*near, *halves],
+        scratch=[act],
+        where=where,
+        flops=flops,
+    )
+    return call(
+        lambda *refs: second_kernel(1, factor, *refs),
+        [((width, out_width), BF16)],
+        [*far, *halves, total],
+        scratch=[act, *stage_scratch(width, out_width)],
+        where=where,
+        flops=flops,
+        hbm_out=True,
+    )[0]
+
+
+def first_kernel(factor, *refs):
     pieces, (own, other, out, right, stage, sem) = refs[:8], refs[8:]
     rows = pieces[0].shape[0] // 2
     half = 8 * rows
@@ -299,26 +352,20 @@
         lambda cols, h=h: h[:, :, :, :, cols].reshape(-1, CHUNK) for h in (own, other)
     ]
     rights = [lambda n=n: right[n * half : (n + 1) * half] for n in range(2)]
-    outer(lefts, rights, out, stage, sem, factor)
-
-
-def token_outer(kernel, where, pieces, halves, factor, swapped):
-    width = pieces[0].shape[-1]
-    tokens = sum(p.size for p in pieces) // width
-    left, right = width, halves[0].shape[-1]
-    if swapped:
-        left, right = right, left
-    return call(
-        lambda *refs: kernel(factor, *refs),
-        [((left, right), BF16)],
+    emit, finish = store_out(out, stage, sem, factor)
+    outer(lefts, rights, out.shape[0], lambda i, cols, t: emit(i, t))
+    finish()
+
+
+def first_product(pieces, halves, factor):
+    rows, width = pieces[0].shape
+    out_rows = halves[0].shape[-1]
+    return call(
+        lambda *refs: first_kernel(factor, *refs),
+        [((out_rows, width), BF16)],
         [*pieces, *halves],
-        scratch=[
-            pltpu.VMEM((tokens, width), BF16),
-            pltpu.VMEM((left // CHUNK, CHUNK, right), BF16),
-            pltpu.SemaphoreType.DMA((left // CHUNK,)),
-        ],
-        where=where,
-        flops=2 * tokens * left * right,
+        scratch=[pltpu.VMEM((8 * rows, width), BF16), *stage_scratch(out_rows, width)],
+        flops=16 * rows * width * out_rows,
         hbm_out=True,
     )[0]
 
@@ -378,9 +425,9 @@
 
     input_half = gather_flips(where, inputs)
     halves = (input_half, swap(input_half, "c"))
-    grad_first = token_outer(first_kernel, where, near + far, halves, factor, True)
-    grad_second = token_outer(
-        second_kernel, where, pre, (grad_half, grad_other), factor, False
+    grad_first = first_product(near + far, halves, factor)
+    grad_second = second_product(
+        where, pre[:2], pre[2:], (grad_half, grad_other), factor
     )
     return (grad_inputs, grad_first, grad_second)
 

time: 188 us -> 184 us (0.979)
  waiting for transfers between devices: 44.9 us -> 51.2 us
  Pallas kernels: 30.4 us -> 24.5 us
  starting transfers between devices: 106 us -> 102 us
    ppermute x27, starting transfers between devices: 82 us -> 76 us  [shift(): lax.ppermute(value, axis, [(i, (i + step) % size) for i in range(size)])]
    pallas_call x12 -> x13, Pallas kernels: 30.4 us -> 24.5 us  [call(): pl.pallas_call(kernel, out_shape=tuple((make(shape, dtype) for shape, dty...]
    ppermute x27, waiting for transfers between devices: 24.3 us -> 30 us  [shift(): lax.ppermute(value, axis, [(i, (i + step) % size) for i in range(size)])]
  transfers between devices with their start and end apart: 41 -> 41, of which waited for: 14 -> 14; matrix products, arithmetic and copies ran while one was open for 1% -> 0% of each run, Pallas kernels for 15% -> 13%
where the time goes in v2:
time: 184 us; the launch traced here: 183 us
  starting transfers between devices  102 us (55%)
  waiting for transfers between devices  51.2 us (28%)
  Pallas kernels  24.5 us (13%)
  other arithmetic  2.46 us (1%)
  local copies, waits for them, and re-layouts  1.85 us (1%)
    ppermute x27, starting transfers between devices, shift(): lax.ppermute(value, axis, [(i, (i + step) % size) for i in range(size)])  76 us
    ppermute x27, waiting for transfers between devices, shift(): lax.ppermute(value, axis, [(i, (i + step) % size) for i in range(size)])  30 us
    pallas_call x13, Pallas kernels, call(): pl.pallas_call(kernel, out_shape=tuple((make(shape, dtype) for shape, dty...  24.5 us
    ppermute x7, waiting for transfers between devices, flip(): return lax.ppermute(value, axis, [(i, i ^ mask) for i in range(size)])  17.7 us
    ppermute x7, starting transfers between devices, swap(): return lax.ppermute(value, axis, [(0, 1), (1, 0)])  14.3 us
    ppermute x7, starting transfers between devices, flip(): return lax.ppermute(value, axis, [(i, i ^ mask) for i in range(size)])  11.5 us
  transfers between devices with their start and end apart: 41, of which 14 were waited for; matrix products, arithmetic and copies ran while one was open for 0% of the time, Pallas kernels for 13%

profile of v2, /device:TPU:8, one launch (start us, length us, event | category | flops | bytes accessed | tf_op | source)
XLA Modules:
  0.0 182.8 jit_solution(15734158764361652246)
XLA Ops:
  2.6 3.3 %collective-permute-start.1 = (bf16[32,1152]{1,0:T(8,128)(2,1)}, bf16[32,1152]{1,0:T(8,128)(2,1)S(1)}, u32[]{:S(2)}, u32[]{:S(2)}) collective-permute-start(bf16[32,1152]{1,0:T(8,128)(2,1)} %param.6), channel_id=1, source_target_pairs={{0,16},{8,24},{16,0},{24,8},{1,17},{9,25},{17,1},{25,9},{2,18},{10... | collective-permute-start | bytes 221192 | tf_op jit(solution)/shard_map/ppermute | solution.py:30
  8.5 2.5 %collective-permute-done.1 = bf16[32,1152]{1,0:T(8,128)(2,1)S(1)} collective-permute-done((bf16[32,1152]{1,0:T(8,128)(2,1)}, bf16[32,1152]{1,0:T(8,128)(2,1)S(1)}, u32[]{:S(2)}, u32[]{:S(2)}) %collective-permute-start.1) | collective-permute-done | bytes 73760 | tf_op jit(solution)/shard_map/ppermute | solution.py:30
  14.0 2.7 %collective-permute-start.4 = (bf16[4,32,1152]{2,1,0:T(8,128)(2,1)S(1)}, bf16[4,32,1152]{2,1,0:T(8,128)(2,1)S(1)}, u32[]{:S(2)}, u32[]{:S(2)}) collective-permute-start(bf16[4,32,1152]{2,1,0:T(8,128)(2,1)S(1)} %pad_maximum_fusion.2.refs_0_), channel_id=1, source_target_pairs={{0,4},{2,6},{4,0},{6,2},{1,5},{3,7},{5,1},{7,3},{8,12},{10,14},{12... | collective-permute-start | bytes 884744 | tf_op jit(solution)/shard_map/ppermute | solution.py:30
  18.2 4.4 %collective-permute-done.3.refs_1_ = bf16[4,32,1152]{2,1,0:T(8,128)(2,1)S(1)} collective-permute-done((bf16[4,32,1152]{2,1,0:T(8,128)(2,1)S(1)}, bf16[4,32,1152]{2,1,0:T(8,128)(2,1)S(1)}, u32[]{:S(2)}, u32[]{:S(2)}) %collective-permute-start.3) | collective-permute-done | bytes 294944 | tf_op jit(solution)/shard_map/ppermute | solution.py:30
  22.6 6.8 %collective-permute-done.4.refs_2_ = bf16[4,32,1152]{2,1,0:T(8,128)(2,1)S(1)} collective-permute-done((bf16[4,32,1152]{2,1,0:T(8,128)(2,1)S(1)}, bf16[4,32,1152]{2,1,0:T(8,128)(2,1)S(1)}, u32[]{:S(2)}, u32[]{:S(2)}) %collective-permute-start.4) | collective-permute-done | bytes 294944 | tf_op jit(solution)/shard_map/ppermute | solution.py:30
  30.3 2.2 %collective-permute-start.32 = (bf16[32,1152]{1,0:T(8,128)(2,1)S(1)}, bf16[32,1152]{1,0:T(8,128)(2,1)S(1)}, u32[]{:S(2)}, u32[]{:S(2)}) collective-permute-start(bf16[32,1152]{1,0:T(8,128)(2,1)S(1)} %copy-done.3), channel_id=1, source_target_pairs={{0,8},{8,0},{16,24},{24,16},{1,9},{9,1},{17,25},{25,17},{2,10},{10... | collective-permute-start | bytes 221192 | tf_op jit(solution)/shard_map/ppermute | solution.py:35
  32.5 2.8 %collective-permute-done.32 = bf16[32,1152]{1,0:T(8,128)(2,1)S(1)} collective-permute-done((bf16[32,1152]{1,0:T(8,128)(2,1)S(1)}, bf16[32,1152]{1,0:T(8,128)(2,1)S(1)}, u32[]{:S(2)}, u32[]{:S(2)}) %collective-permute-start.32) | collective-permute-done | bytes 73760 | tf_op jit(solution)/shard_map/ppermute | solution.py:35
  44.0 2.4 %collective-permute-start.12 = (bf16[128,1152]{1,0:T(8,128)(2,1)S(1)}, bf16[128,1152]{1,0:T(8,128)(2,1)S(1)}, u32[]{:S(2)}, u32[]{:S(2)}) collective-permute-start(bf16[128,1152]{1,0:T(8,128)(2,1)S(1)} %get-tuple-element.38), channel_id=1, source_target_pairs={{0,96},{32,0},{64,32},{96,64},{1,97},{33,1},{65,33},{97,65},{2,98}... | collective-permute-start | bytes 884744 | tf_op jit(solution)/shard_map/ppermute | solution.py:30
  49.2 6.6 %collective-permute-done.10 = bf16[128,1152]{1,0:T(8,128)(2,1)S(1)} collective-permute-done((bf16[128,1152]{1,0:T(8,128)(2,1)S(1)}, bf16[128,1152]{1,0:T(8,128)(2,1)S(1)}, u32[]{:S(2)}, u32[]{:S(2)}) %collective-permute-start.10) | collective-permute-done | bytes 294944 | tf_op jit(solution)/shard_map/ppermute | solution.py:30
  55.9 5.0 %collective-permute-start.9 = (bf16[128,1152]{1,0:T(8,128)(2,1)S(1)}, bf16[128,1152]{1,0:T(8,128)(2,1)S(1)}, u32[]{:S(2)}, u32[]{:S(2)}) collective-permute-start(bf16[128,1152]{1,0:T(8,128)(2,1)S(1)} %get-tuple-element.34), channel_id=1, source_target_pairs={{0,96},{32,0},{64,32},{96,64},{1,97},{33,1},{65,33},{97,65},{2,98}... | collective-permute-start | bytes 884744 | tf_op jit(solution)/shard_map/ppermute | solution.py:30
  61.0 5.5 %collective-permute-start.13 = (bf16[128,1152]{1,0:T(8,128)(2,1)S(1)}, bf16[128,1152]{1,0:T(8,128)(2,1)S(1)}, u32[]{:S(2)}, u32[]{:S(2)}) collective-permute-start(bf16[128,1152]{1,0:T(8,128)(2,1)S(1)} %add_convert_fusion), channel_id=1, source_target_pairs={{0,128},{128,0},{1,129},{129,1},{2,130},{130,2},{3,131},{131,3},{4... | collective-permute-start | bytes 884744 | tf_op jit(solution)/shard_map/ppermute | solution.py:39
  66.8 2.7 %collective-permute-start.35 = (bf16[2,4,32,1152]{3,2,1,0:T(8,128)(2,1)S(1)}, bf16[2,4,32,1152]{3,2,1,0:T(8,128)(2,1)S(1)}, u32[]{:S(2)}, u32[]{:S(2)}) collective-permute-start(bf16[2,4,32,1152]{3,2,1,0:T(8,128)(2,1)S(1)} %pad_maximum_fusion.near), channel_id=1, source_target_pairs={{0,4},{2,6},{4,0},{6,2},{1,5},{3,7},{5,1},{7,3},{8,12},{10,14},{12... | collective-permute-start | bytes 1769480 | tf_op jit(solution)/shard_map/ppermute | solution.py:35
  72.6 5.6 %collective-permute-start.21 = (bf16[128,1152]{1,0:T(8,128)(2,1)S(1)}, bf16[128,1152]{1,0:T(8,128)(2,1)S(1)}, u32[]{:S(2)}, u32[]{:S(2)}) collective-permute-start(bf16[128,1152]{1,0:T(8,128)(2,1)S(1)} %fusion.7.p0.refs_0_), channel_id=1, source_target_pairs={{0,128},{128,0},{1,129},{129,1},{2,130},{130,2},{3,131},{131,3},{4... | collective-permute-start | bytes 884744 | tf_op jit(solution)/shard_map/ppermute | solution.py:39
  79.3 2.2 %collective-permute-start.15 = (bf16[128,1152]{1,0:T(8,128)(2,1)S(1)}, bf16[128,1152]{1,0:T(8,128)(2,1)S(1)}, u32[]{:S(2)}, u32[]{:S(2)}) collective-permute-start(bf16[128,1152]{1,0:T(8,128)(2,1)S(1)} %fusion.7.p0.refs_0_), channel_id=1, source_target_pairs={{0,64},{32,96},{64,0},{96,32},{1,65},{33,97},{65,1},{97,33},{2,66}... | collective-permute-start | bytes 884744 | tf_op jit(solution)/shard_map/ppermute | solution.py:30
  81.5 2.1 %collective-permute-start.16 = (bf16[128,1152]{1,0:T(8,128)(2,1)S(1)}, bf16[128,1152]{1,0:T(8,128)(2,1)S(1)}, u32[]{:S(2)}, u32[]{:S(2)}) collective-permute-start(bf16[128,1152]{1,0:T(8,128)(2,1)S(1)} %fusion.7.p0.refs_0_), channel_id=1, source_target_pairs={{0,32},{32,64},{64,96},{96,0},{1,33},{33,65},{65,97},{97,1},{2,34}... | collective-permute-start | bytes 884744 | tf_op jit(solution)/shard_map/ppermute | solution.py:30
  83.7 2.3 %collective-permute-start.38 = (bf16[2,128,1152]{2,1,0:T(8,128)(2,1)S(1)}, bf16[2,128,1152]{2,1,0:T(8,128)(2,1)S(1)}, u32[]{:S(2)}, u32[]{:S(2)}) collective-permute-start(bf16[2,128,1152]{2,1,0:T(8,128)(2,1)S(1)} %pad_maximum_fusion.1.refs_1_), channel_id=1, source_target_pairs={{0,128},{128,0},{1,129},{129,1},{2,130},{130,2},{3,131},{131,3},{4... | collective-permute-start | bytes 1769480 | tf_op jit(solution)/shard_map/ppermute | solution.py:39
  86.0 2.4 %collective-permute-done.21.p0.refs_4_ = bf16[128,1152]{1,0:T(8,128)(2,1)S(1)} collective-permute-done((bf16[128,1152]{1,0:T(8,128)(2,1)S(1)}, bf16[128,1152]{1,0:T(8,128)(2,1)S(1)}, u32[]{:S(2)}, u32[]{:S(2)}) %collective-permute-start.21) | collective-permute-done | bytes 294944 | tf_op jit(solution)/shard_map/ppermute | solution.py:39
  89.0 7.3 %collective-permute-start.23 = (bf16[128,1152]{1,0:T(8,128)(2,1)S(1)}, bf16[128,1152]{1,0:T(8,128)(2,1)S(1)}, u32[]{:S(2)}, u32[]{:S(2)}) collective-permute-start(bf16[128,1152]{1,0:T(8,128)(2,1)S(1)} %collective-permute-done.21.p0.refs_4_), channel_id=1, source_target_pairs={{0,64},{32,96},{64,0},{96,32},{1,65},{33,97},{65,1},{97,33},{2,66}... | collective-permute-start | bytes 884744 | tf_op jit(solution)/shard_map/ppermute | solution.py:30
  97.1 2.9 %shard_map.80 = (bf16[4,2,32,1152]{3,2,1,0:T(8,128)(2,1)S(1)}, f32[4,2,32,1152]{3,2,1,0:T(8,128)S(1)}) custom-call(s32[5]{0:T(128)S(1)} %stack.67.where.refs_0_, bf16[128,1152]{1,0:T(8,128)(2,1)S(1)} %fusion.7.p0.refs_0_, bf16[128,1152]{1,0:T(8,128)(2,1)S(1)} %collective-permute-done.14.p1.refs_1_, bf16[128,1152]{1,0:T(8,128)(2,1)S(1)} %collective-permute-done.15.p2.refs_2_, ...), custom_call_target="tpu_custom_call" | custom-call | flops 1358954496 | bytes 3833856 | tf_op jit(solution)/shard_map/pallas_call | solution.py:58
  100.6 5.2 %collective-permute-done.23.p2.refs_6_ = bf16[128,1152]{1,0:T(8,128)(2,1)S(1)} collective-permute-done((bf16[128,1152]{1,0:T(8,128)(2,1)S(1)}, bf16[128,1152]{1,0:T(8,128)(2,1)S(1)}, u32[]{:S(2)}, u32[]{:S(2)}) %collective-permute-start.23) | collective-permute-done | bytes 294944 | tf_op jit(solution)/shard_map/ppermute | solution.py:30
  106.7 2.9 %shard_map.82 = (bf16[4,2,32,1152]{3,2,1,0:T(8,128)(2,1)S(1)}, f32[4,2,32,1152]{3,2,1,0:T(8,128)S(1)}) custom-call(s32[5]{0:T(128)S(1)} %stack.67.where.refs_0_, bf16[128,1152]{1,0:T(8,128)(2,1)S(1)} %collective-permute-done.21.p0.refs_4_, bf16[128,1152]{1,0:T(8,128)(2,1)S(1)} %collective-permute-done.22.p1.refs_5_, ...), custom_call_target="tpu_custom_call" | custom-call | flops 1358954496 | bytes 3833856 | tf_op jit(solution)/shard_map/pallas_call | solution.py:58
  109.7 3.0 %collective-permute-start.40 = (bf16[2,128,1152]{2,1,0:T(8,128)(2,1)S(1)}, bf16[2,128,1152]{2,1,0:T(8,128)(2,1)S(1)}, u32[]{:S(2)}, u32[]{:S(2)}) collective-permute-start(bf16[2,128,1152]{2,1,0:T(8,128)(2,1)S(1)} %pad_maximum_fusion.1.refs_1_), channel_id=1, source_target_pairs={{0,64},{32,96},{64,0},{96,32},{1,65},{33,97},{65,1},{97,33},{2,66}... | collective-permute-start | bytes 1769480 | tf_op jit(solution)/shard_map/ppermute | solution.py:35
  113.6 8.6 %collective-permute-start.18 = (bf16[2,32,1152]{2,1,0:T(8,128)(2,1)S(1)}, bf16[2,32,1152]{2,1,0:T(8,128)(2,1)S(1)}, u32[]{:S(2)}, u32[]{:S(2)}) collective-permute-start(bf16[2,32,1152]{2,1,0:T(8,128)(2,1)S(1)} %get-tuple-element.42), channel_id=1, source_target_pairs={{0,2},{2,4},{4,6},{6,0},{1,3},{3,5},{5,7},{7,1},{8,10},{10,12},{12... | collective-permute-start | bytes 442376 | tf_op jit(solution)/shard_map/ppermute | solution.py:30
  122.4 5.3 %collective-permute-done.40.refs_2_ = bf16[2,128,1152]{2,1,0:T(8,128)(2,1)S(1)} collective-permute-done((bf16[2,128,1152]{2,1,0:T(8,128)(2,1)S(1)}, bf16[2,128,1152]{2,1,0:T(8,128)(2,1)S(1)}, u32[]{:S(2)}, u32[]{:S(2)}) %collective-permute-start.40) | collective-permute-done | bytes 589856 | tf_op jit(solution)/shard_map/ppermute | solution.py:35
  127.7 2.3 %collective-permute-start.20 = (bf16[2,32,1152]{2,1,0:T(8,128)(2,1)S(1)}, bf16[2,32,1152]{2,1,0:T(8,128)(2,1)S(1)}, u32[]{:S(2)}, u32[]{:S(2)}) collective-permute-start(bf16[2,32,1152]{2,1,0:T(8,128)(2,1)S(1)} %get-tuple-element.44), channel_id=1, source_target_pairs={{0,6},{2,0},{4,2},{6,4},{1,7},{3,1},{5,3},{7,5},{8,14},{10,8},{12,... | collective-permute-start | bytes 442376 | tf_op jit(solution)/shard_map/ppermute | solution.py:30
  130.0 9.6 %collective-permute-done.39.refs_2_ = bf16[2,128,1152]{2,1,0:T(8,128)(2,1)S(1)} collective-permute-done((bf16[2,128,1152]{2,1,0:T(8,128)(2,1)S(1)}, bf16[2,128,1152]{2,1,0:T(8,128)(2,1)S(1)}, u32[]{:S(2)}, u32[]{:S(2)}) %collective-permute-start.39) | collective-permute-done | bytes 589856 | tf_op jit(solution)/shard_map/ppermute | solution.py:35
  139.5 3.1 %collective-permute-start.26 = (bf16[2,32,1152]{2,1,0:T(8,128)(2,1)S(1)}, bf16[2,32,1152]{2,1,0:T(8,128)(2,1)S(1)}, u32[]{:S(2)}, u32[]{:S(2)}) collective-permute-start(bf16[2,32,1152]{2,1,0:T(8,128)(2,1)S(1)} %get-tuple-element.48), channel_id=1, source_target_pairs={{0,2},{2,4},{4,6},{6,0},{1,3},{3,5},{5,7},{7,1},{8,10},{10,12},{12... | collective-permute-start | bytes 442376 | tf_op jit(solution)/shard_map/ppermute | solution.py:30
  145.3 3.3 %shard_map.87.refs_5_ = f32[1152,1152]{1,0:T(8,128)S(1)} custom-call(s32[5]{0:T(128)S(1)} %stack.67.where.refs_0_, bf16[2,128,1152]{2,1,0:T(8,128)(2,1)S(1)} %pad_maximum_fusion.1.refs_1_, bf16[2,128,1152]{2,1,0:T(8,128)(2,1)S(1)} %collective-permute-done.40.refs_2_, bf16[2,4,2,32,1152]{4,3,2,1,0:T(8,128)(2,1)S(1)} %shard_map.76.half.refs_3_, ...), custom_call_target="tpu_custom_call" | custom-call | flops 1358954496 | bytes 3538944 | tf_op jit(solution)/shard_map/pallas_call | solution.py:58
  148.6 4.3 %shard_map.88 = bf16[1152,1152]{1,0:T(8,128)(2,1)} custom-call(s32[5]{0:T(128)S(1)} %stack.67.where.refs_0_, bf16[2,128,1152]{2,1,0:T(8,128)(2,1)S(1)} %collective-permute-done.38.refs_1_, bf16[2,128,1152]{2,1,0:T(8,128)(2,1)S(1)} %collective-permute-done.39.refs_2_, bf16[2,4,2,32,1152]{4,3,2,1,0:T(8,128)(2,1)S(1)} %shard_map.76.half.refs_3_, ...), custom_call_target="tpu_custom_call" | custom-call | flops 1358954496 | bytes 6193152 | tf_op jit(solution)/shard_map/pallas_call | solution.py:58
  153.6 20.1 %collective-permute-start.29 = (bf16[32,1152]{1,0:T(8,128)(2,1)S(1)}, bf16[32,1152]{1,0:T(8,128)(2,1)S(1)}, u32[]{:S(2)}, u32[]{:S(2)}) collective-permute-start(bf16[32,1152]{1,0:T(8,128)(2,1)S(1)} %get-tuple-element.52), channel_id=1, source_target_pairs={{0,8},{8,16},{16,24},{24,0},{1,9},{9,17},{17,25},{25,1},{2,10},{10... | collective-permute-start | bytes 221192 | tf_op jit(solution)/shard_map/ppermute | solution.py:30
  174.4 2.8 %collective-permute-start.31 = (bf16[32,1152]{1,0:T(8,128)(2,1)S(1)}, bf16[32,1152]{1,0:T(8,128)(2,1)S(1)}, u32[]{:S(2)}, u32[]{:S(2)}) collective-permute-start(bf16[32,1152]{1,0:T(8,128)(2,1)S(1)} %get-tuple-element.54), channel_id=1, source_target_pairs={{0,24},{8,0},{16,8},{24,16},{1,25},{9,1},{17,9},{25,17},{2,26},{10... | collective-permute-start | bytes 221192 | tf_op jit(solution)/shard_map/ppermute | solution.py:30
  177.2 4.8 %shard_map.86 = bf16[1152,1152]{1,0:T(8,128)(2,1)} custom-call(bf16[128,1152]{1,0:T(8,128)(2,1)S(1)} %fusion.7.p0.refs_0_, bf16[128,1152]{1,0:T(8,128)(2,1)S(1)} %collective-permute-done.14.p1.refs_1_, bf16[128,1152]{1,0:T(8,128)(2,1)S(1)} %collective-permute-done.15.p2.refs_2_, bf16[128,1152]{1,0:T(8,128)(2,1)S(1)} %collective-permute-done.16.p3.refs_3_, ...), custom_call_target="tpu_custom_call" | custom-call | flops 2717908992 | bytes 4718592 | tf_op jit(solution)/shard_map/pallas_call | solution.py:58
  (84 shorter events, 34.9 us)
Async XLA Ops:
  14.0 15.4 %collective-permute-start.4 = (bf16[4,32,1152]{2,1,0:T(8,128)(2,1)S(1)}, bf16[4,32,1152]{2,1,0:T(8,128)(2,1)S(1)}, u32[]{:S(2)}, u32[]{:S(2)}) collective-permute-start(bf16[4,32,1152]{2,1,0:T(8,128)(2,1)S(1)} %pad_maximum_fusion.2.refs_0_), channel_id=1, source_target_pairs={{0,4},{2,6},{4,0},{6,2},{1,5},{3,7},{5,1},{7,3},{8,12},{10,14},{12... | collective-permute-start | bytes 884744 | tf_op jit(solution)/shard_map/ppermute | solution.py:30
  16.7 12.7 %collective-permute-start.5 = (bf16[4,32,1152]{2,1,0:T(8,128)(2,1)S(1)}, bf16[4,32,1152]{2,1,0:T(8,128)(2,1)S(1)}, u32[]{:S(2)}, u32[]{:S(2)}) collective-permute-start(bf16[4,32,1152]{2,1,0:T(8,128)(2,1)S(1)} %pad_maximum_fusion.2.refs_0_), channel_id=1, source_target_pairs={{0,6},{2,0},{4,2},{6,4},{1,7},{3,1},{5,3},{7,5},{8,14},{10,8},{12,... | collective-permute-start | bytes 884744 | tf_op jit(solution)/shard_map/ppermute | solution.py:30
  35.3 11.1 %collective-permute-start.33 = (bf16[2,32,1152]{2,1,0:T(8,128)(2,1)S(1)}, bf16[2,32,1152]{2,1,0:T(8,128)(2,1)S(1)}, u32[]{:S(2)}, u32[]{:S(2)}) collective-permute-start(bf16[2,32,1152]{2,1,0:T(8,128)(2,1)S(1)} %pad_maximum_fusion.5), channel_id=1, source_target_pairs={{0,16},{8,24},{16,0},{24,8},{1,17},{9,25},{17,1},{25,9},{2,18},{10... | collective-permute-start | bytes 442376 | tf_op jit(solution)/shard_map/ppermute | solution.py:35
  41.4 14.4 %collective-permute-start.10 = (bf16[128,1152]{1,0:T(8,128)(2,1)S(1)}, bf16[128,1152]{1,0:T(8,128)(2,1)S(1)}, u32[]{:S(2)}, u32[]{:S(2)}) collective-permute-start(bf16[128,1152]{1,0:T(8,128)(2,1)S(1)} %get-tuple-element.36), channel_id=1, source_target_pairs={{0,32},{32,64},{64,96},{96,0},{1,33},{33,65},{65,97},{97,1},{2,34}... | collective-permute-start | bytes 884744 | tf_op jit(solution)/shard_map/ppermute | solution.py:30
  43.0 12.8 %collective-permute-start.11 = (bf16[128,1152]{1,0:T(8,128)(2,1)S(1)}, bf16[128,1152]{1,0:T(8,128)(2,1)S(1)}, u32[]{:S(2)}, u32[]{:S(2)}) collective-permute-start(bf16[128,1152]{1,0:T(8,128)(2,1)S(1)} %get-tuple-element.37), channel_id=1, source_target_pairs={{0,64},{32,96},{64,0},{96,32},{1,65},{33,97},{65,1},{97,33},{2,66}... | collective-permute-start | bytes 884744 | tf_op jit(solution)/shard_map/ppermute | solution.py:30
  44.0 16.9 %collective-permute-start.12 = (bf16[128,1152]{1,0:T(8,128)(2,1)S(1)}, bf16[128,1152]{1,0:T(8,128)(2,1)S(1)}, u32[]{:S(2)}, u32[]{:S(2)}) collective-permute-start(bf16[128,1152]{1,0:T(8,128)(2,1)S(1)} %get-tuple-element.38), channel_id=1, source_target_pairs={{0,96},{32,0},{64,32},{96,64},{1,97},{33,1},{65,33},{97,65},{2,98}... | collective-permute-start | bytes 884744 | tf_op jit(solution)/shard_map/ppermute | solution.py:30
  46.5 20.1 %collective-permute-start.34 = (bf16[4,32,1152]{2,1,0:T(8,128)(2,1)S(1)}, bf16[4,32,1152]{2,1,0:T(8,128)(2,1)S(1)}, u32[]{:S(2)}, u32[]{:S(2)}) collective-permute-start(bf16[4,32,1152]{2,1,0:T(8,128)(2,1)S(1)} %get-tuple-element.56), channel_id=1, source_target_pairs={{0,2},{2,0},{4,6},{6,4},{1,3},{3,1},{5,7},{7,5},{8,10},{10,8},{12,... | collective-permute-start | bytes 884744 | tf_op jit(solution)/shard_map/ppermute | solution.py:35
  48.9 17.9 %collective-permute-start.7 = (bf16[128,1152]{1,0:T(8,128)(2,1)S(1)}, bf16[128,1152]{1,0:T(8,128)(2,1)S(1)}, u32[]{:S(2)}, u32[]{:S(2)}) collective-permute-start(bf16[128,1152]{1,0:T(8,128)(2,1)S(1)} %get-tuple-element.32), channel_id=1, source_target_pairs={{0,32},{32,64},{64,96},{96,0},{1,33},{33,65},{65,97},{97,1},{2,34}... | collective-permute-start | bytes 884744 | tf_op jit(solution)/shard_map/ppermute | solution.py:30
  55.8 13.7 %collective-permute-start.8 = (bf16[128,1152]{1,0:T(8,128)(2,1)S(1)}, bf16[128,1152]{1,0:T(8,128)(2,1)S(1)}, u32[]{:S(2)}, u32[]{:S(2)}) collective-permute-start(bf16[128,1152]{1,0:T(8,128)(2,1)S(1)} %get-tuple-element.33), channel_id=1, source_target_pairs={{0,64},{32,96},{64,0},{96,32},{1,65},{33,97},{65,1},{97,33},{2,66}... | collective-permute-start | bytes 884744 | tf_op jit(solution)/shard_map/ppermute | solution.py:30
  55.9 15.1 %collective-permute-start.9 = (bf16[128,1152]{1,0:T(8,128)(2,1)S(1)}, bf16[128,1152]{1,0:T(8,128)(2,1)S(1)}, u32[]{:S(2)}, u32[]{:S(2)}) collective-permute-start(bf16[128,1152]{1,0:T(8,128)(2,1)S(1)} %get-tuple-element.34), channel_id=1, source_target_pairs={{0,96},{32,0},{64,32},{96,64},{1,97},{33,1},{65,33},{97,65},{2,98}... | collective-permute-start | bytes 884744 | tf_op jit(solution)/shard_map/ppermute | solution.py:30
  61.0 11.1 %collective-permute-start.13 = (bf16[128,1152]{1,0:T(8,128)(2,1)S(1)}, bf16[128,1152]{1,0:T(8,128)(2,1)S(1)}, u32[]{:S(2)}, u32[]{:S(2)}) collective-permute-start(bf16[128,1152]{1,0:T(8,128)(2,1)S(1)} %add_convert_fusion), channel_id=1, source_target_pairs={{0,128},{128,0},{1,129},{129,1},{2,130},{130,2},{3,131},{131,3},{4... | collective-permute-start | bytes 884744 | tf_op jit(solution)/shard_map/ppermute | solution.py:39
  66.6 14.9 %collective-permute-start.37 = (bf16[128,1152]{1,0:T(8,128)(2,1)S(1)}, bf16[128,1152]{1,0:T(8,128)(2,1)S(1)}, u32[]{:S(2)}, u32[]{:S(2)}) collective-permute-start(bf16[128,1152]{1,0:T(8,128)(2,1)S(1)} %bitcast.35), channel_id=1, source_target_pairs={{0,32},{32,0},{64,96},{96,64},{1,33},{33,1},{65,97},{97,65},{2,34}... | collective-permute-start | bytes 884744 | tf_op jit(solution)/shard_map/ppermute | solution.py:35
  66.8 16.9 %collective-permute-start.35 = (bf16[2,4,32,1152]{3,2,1,0:T(8,128)(2,1)S(1)}, bf16[2,4,32,1152]{3,2,1,0:T(8,128)(2,1)S(1)}, u32[]{:S(2)}, u32[]{:S(2)}) collective-permute-start(bf16[2,4,32,1152]{3,2,1,0:T(8,128)(2,1)S(1)} %pad_maximum_fusion.near), channel_id=1, source_target_pairs={{0,4},{2,6},{4,0},{6,2},{1,5},{3,7},{5,1},{7,3},{8,12},{10,14},{12... | collective-permute-start | bytes 1769480 | tf_op jit(solution)/shard_map/ppermute | solution.py:35
  72.6 15.8 %collective-permute-start.21 = (bf16[128,1152]{1,0:T(8,128)(2,1)S(1)}, bf16[128,1152]{1,0:T(8,128)(2,1)S(1)}, u32[]{:S(2)}, u32[]{:S(2)}) collective-permute-start(bf16[128,1152]{1,0:T(8,128)(2,1)S(1)} %fusion.7.p0.refs_0_), channel_id=1, source_target_pairs={{0,128},{128,0},{1,129},{129,1},{2,130},{130,2},{3,131},{131,3},{4... | collective-permute-start | bytes 884744 | tf_op jit(solution)/shard_map/ppermute | solution.py:39
  78.1 10.9 %collective-permute-start.14 = (bf16[128,1152]{1,0:T(8,128)(2,1)S(1)}, bf16[128,1152]{1,0:T(8,128)(2,1)S(1)}, u32[]{:S(2)}, u32[]{:S(2)}) collective-permute-start(bf16[128,1152]{1,0:T(8,128)(2,1)S(1)} %fusion.7.p0.refs_0_), channel_id=1, source_target_pairs={{0,96},{32,0},{64,32},{96,64},{1,97},{33,1},{65,33},{97,65},{2,98}... | collective-permute-start | bytes 884744 | tf_op jit(solution)/shard_map/ppermute | solution.py:30
  79.3 17.0 %collective-permute-start.15 = (bf16[128,1152]{1,0:T(8,128)(2,1)S(1)}, bf16[128,1152]{1,0:T(8,128)(2,1)S(1)}, u32[]{:S(2)}, u32[]{:S(2)}) collective-permute-start(bf16[128,1152]{1,0:T(8,128)(2,1)S(1)} %fusion.7.p0.refs_0_), channel_id=1, source_target_pairs={{0,64},{32,96},{64,0},{96,32},{1,65},{33,97},{65,1},{97,33},{2,66}... | collective-permute-start | bytes 884744 | tf_op jit(solution)/shard_map/ppermute | solution.py:30
  81.5 15.5 %collective-permute-start.16 = (bf16[128,1152]{1,0:T(8,128)(2,1)S(1)}, bf16[128,1152]{1,0:T(8,128)(2,1)S(1)}, u32[]{:S(2)}, u32[]{:S(2)}) collective-permute-start(bf16[128,1152]{1,0:T(8,128)(2,1)S(1)} %fusion.7.p0.refs_0_), channel_id=1, source_target_pairs={{0,32},{32,64},{64,96},{96,0},{1,33},{33,65},{65,97},{97,1},{2,34}... | collective-permute-start | bytes 884744 | tf_op jit(solution)/shard_map/ppermute | solution.py:30
  83.7 28.9 %collective-permute-start.38 = (bf16[2,128,1152]{2,1,0:T(8,128)(2,1)S(1)}, bf16[2,128,1152]{2,1,0:T(8,128)(2,1)S(1)}, u32[]{:S(2)}, u32[]{:S(2)}) collective-permute-start(bf16[2,128,1152]{2,1,0:T(8,128)(2,1)S(1)} %pad_maximum_fusion.1.refs_1_), channel_id=1, source_target_pairs={{0,128},{128,0},{1,129},{129,1},{2,130},{130,2},{3,131},{131,3},{4... | collective-permute-start | bytes 1769480 | tf_op jit(solution)/shard_map/ppermute | solution.py:39
  88.4 11.6 %collective-permute-start.22 = (bf16[128,1152]{1,0:T(8,128)(2,1)S(1)}, bf16[128,1152]{1,0:T(8,128)(2,1)S(1)}, u32[]{:S(2)}, u32[]{:S(2)}) collective-permute-start(bf16[128,1152]{1,0:T(8,128)(2,1)S(1)} %collective-permute-done.21.p0.refs_4_), channel_id=1, source_target_pairs={{0,96},{32,0},{64,32},{96,64},{1,97},{33,1},{65,33},{97,65},{2,98}... | collective-permute-start | bytes 884744 | tf_op jit(solution)/shard_map/ppermute | solution.py:30
  89.0 16.7 %collective-permute-start.23 = (bf16[128,1152]{1,0:T(8,128)(2,1)S(1)}, bf16[128,1152]{1,0:T(8,128)(2,1)S(1)}, u32[]{:S(2)}, u32[]{:S(2)}) collective-permute-start(bf16[128,1152]{1,0:T(8,128)(2,1)S(1)} %collective-permute-done.21.p0.refs_4_), channel_id=1, source_target_pairs={{0,64},{32,96},{64,0},{96,32},{1,65},{33,97},{65,1},{97,33},{2,66}... | collective-permute-start | bytes 884744 | tf_op jit(solution)/shard_map/ppermute | solution.py:30
  96.3 10.4 %collective-permute-start.24 = (bf16[128,1152]{1,0:T(8,128)(2,1)S(1)}, bf16[128,1152]{1,0:T(8,128)(2,1)S(1)}, u32[]{:S(2)}, u32[]{:S(2)}) collective-permute-start(bf16[128,1152]{1,0:T(8,128)(2,1)S(1)} %collective-permute-done.21.p0.refs_4_), channel_id=1, source_target_pairs={{0,32},{32,64},{64,96},{96,0},{1,33},{33,65},{65,97},{97,1},{2,34}... | collective-permute-start | bytes 884744 | tf_op jit(solution)/shard_map/ppermute | solution.py:30
  97.0 80.2 %collective-permute-start.36 = (bf16[2,4,2,32,1152]{4,3,2,1,0:T(8,128)(2,1)S(1)}, bf16[2,4,2,32,1152]{4,3,2,1,0:T(8,128)(2,1)S(1)}, u32[]{:S(2)}, u32[]{:S(2)}) collective-permute-start(bf16[2,4,2,32,1152]{4,3,2,1,0:T(8,128)(2,1)S(1)} %shard_map.85.refs_8_), channel_id=1, source_target_pairs={{0,1},{1,0},{2,3},{3,2},{4,5},{5,4},{6,7},{7,6},{8,9},{9,8},{10,11... | collective-permute-start | bytes 3538952 | tf_op jit(solution)/shard_map/ppermute | solution.py:39
  100.0 13.5 %collective-permute-start.17 = (bf16[4,2,32,1152]{3,2,1,0:T(8,128)(2,1)S(1)}, bf16[4,2,32,1152]{3,2,1,0:T(8,128)(2,1)S(1)}, u32[]{:S(2)}, u32[]{:S(2)}) collective-permute-start(bf16[4,2,32,1152]{3,2,1,0:T(8,128)(2,1)S(1)} %get-tuple-element.40), channel_id=1, source_target_pairs={{0,1},{1,0},{2,3},{3,2},{4,5},{5,4},{6,7},{7,6},{8,9},{9,8},{10,11... | collective-permute-start | bytes 1769480 | tf_op jit(solution)/shard_map/ppermute | solution.py:39
  109.6 12.7 %collective-permute-start.25 = (bf16[4,2,32,1152]{3,2,1,0:T(8,128)(2,1)S(1)}, bf16[4,2,32,1152]{3,2,1,0:T(8,128)(2,1)S(1)}, u32[]{:S(2)}, u32[]{:S(2)}) collective-permute-start(bf16[4,2,32,1152]{3,2,1,0:T(8,128)(2,1)S(1)} %get-tuple-element.46), channel_id=1, source_target_pairs={{0,1},{1,0},{2,3},{3,2},{4,5},{5,4},{6,7},{7,6},{8,9},{9,8},{10,11... | collective-permute-start | bytes 1769480 | tf_op jit(solution)/shard_map/ppermute | solution.py:39
  109.7 18.0 %collective-permute-start.40 = (bf16[2,128,1152]{2,1,0:T(8,128)(2,1)S(1)}, bf16[2,128,1152]{2,1,0:T(8,128)(2,1)S(1)}, u32[]{:S(2)}, u32[]{:S(2)}) collective-permute-start(bf16[2,128,1152]{2,1,0:T(8,128)(2,1)S(1)} %pad_maximum_fusion.1.refs_1_), channel_id=1, source_target_pairs={{0,64},{32,96},{64,0},{96,32},{1,65},{33,97},{65,1},{97,33},{2,66}... | collective-permute-start | bytes 1769480 | tf_op jit(solution)/shard_map/ppermute | solution.py:35
  112.6 26.9 %collective-permute-start.39 = (bf16[2,128,1152]{2,1,0:T(8,128)(2,1)S(1)}, bf16[2,128,1152]{2,1,0:T(8,128)(2,1)S(1)}, u32[]{:S(2)}, u32[]{:S(2)}) collective-permute-start(bf16[2,128,1152]{2,1,0:T(8,128)(2,1)S(1)} %collective-permute-done.38.refs_1_), channel_id=1, source_target_pairs={{0,64},{32,96},{64,0},{96,32},{1,65},{33,97},{65,1},{97,33},{2,66}... | collective-permute-start | bytes 1769480 | tf_op jit(solution)/shard_map/ppermute | solution.py:35
  113.6 29.0 %collective-permute-start.18 = (bf16[2,32,1152]{2,1,0:T(8,128)(2,1)S(1)}, bf16[2,32,1152]{2,1,0:T(8,128)(2,1)S(1)}, u32[]{:S(2)}, u32[]{:S(2)}) collective-permute-start(bf16[2,32,1152]{2,1,0:T(8,128)(2,1)S(1)} %get-tuple-element.42), channel_id=1, source_target_pairs={{0,2},{2,4},{4,6},{6,0},{1,3},{3,5},{5,7},{7,1},{8,10},{10,12},{12... | collective-permute-start | bytes 442376 | tf_op jit(solution)/shard_map/ppermute | solution.py:30
  122.2 21.0 %collective-permute-start.19 = (bf16[2,32,1152]{2,1,0:T(8,128)(2,1)S(1)}, bf16[2,32,1152]{2,1,0:T(8,128)(2,1)S(1)}, u32[]{:S(2)}, u32[]{:S(2)}) collective-permute-start(bf16[2,32,1152]{2,1,0:T(8,128)(2,1)S(1)} %get-tuple-element.43), channel_id=1, source_target_pairs={{0,4},{2,6},{4,0},{6,2},{1,5},{3,7},{5,1},{7,3},{8,12},{10,14},{12... | collective-permute-start | bytes 442376 | tf_op jit(solution)/shard_map/ppermute | solution.py:30
  127.7 25.2 %collective-permute-start.20 = (bf16[2,32,1152]{2,1,0:T(8,128)(2,1)S(1)}, bf16[2,32,1152]{2,1,0:T(8,128)(2,1)S(1)}, u32[]{:S(2)}, u32[]{:S(2)}) collective-permute-start(bf16[2,32,1152]{2,1,0:T(8,128)(2,1)S(1)} %get-tuple-element.44), channel_id=1, source_target_pairs={{0,6},{2,0},{4,2},{6,4},{1,7},{3,1},{5,3},{7,5},{8,14},{10,8},{12,... | collective-permute-start | bytes 442376 | tf_op jit(solution)/shard_map/ppermute | solution.py:30
  139.5 13.3 %collective-permute-start.26 = (bf16[2,32,1152]{2,1,0:T(8,128)(2,1)S(1)}, bf16[2,32,1152]{2,1,0:T(8,128)(2,1)S(1)}, u32[]{:S(2)}, u32[]{:S(2)}) collective-permute-start(bf16[2,32,1152]{2,1,0:T(8,128)(2,1)S(1)} %get-tuple-element.48), channel_id=1, source_target_pairs={{0,2},{2,4},{4,6},{6,0},{1,3},{3,5},{5,7},{7,1},{8,10},{10,12},{12... | collective-permute-start | bytes 442376 | tf_op jit(solution)/shard_map/ppermute | solution.py:30
  142.6 10.2 %collective-permute-start.27 = (bf16[2,32,1152]{2,1,0:T(8,128)(2,1)S(1)}, bf16[2,32,1152]{2,1,0:T(8,128)(2,1)S(1)}, u32[]{:S(2)}, u32[]{:S(2)}) collective-permute-start(bf16[2,32,1152]{2,1,0:T(8,128)(2,1)S(1)} %get-tuple-element.49), channel_id=1, source_target_pairs={{0,4},{2,6},{4,0},{6,2},{1,5},{3,7},{5,1},{7,3},{8,12},{10,14},{12... | collective-permute-start | bytes 442376 | tf_op jit(solution)/shard_map/ppermute | solution.py:30
  153.6 28.4 %collective-permute-start.29 = (bf16[32,1152]{1,0:T(8,128)(2,1)S(1)}, bf16[32,1152]{1,0:T(8,128)(2,1)S(1)}, u32[]{:S(2)}, u32[]{:S(2)}) collective-permute-start(bf16[32,1152]{1,0:T(8,128)(2,1)S(1)} %get-tuple-element.52), channel_id=1, source_target_pairs={{0,8},{8,16},{16,24},{24,0},{1,9},{9,17},{17,25},{25,1},{2,10},{10... | collective-permute-start | bytes 221192 | tf_op jit(solution)/shard_map/ppermute | solution.py:30
  (14 other events, 122.0 us)

commit v3 on v2

--- a/solution.py
+++ b/solution.py
@@ -73,32 +73,16 @@
     return lax.dot_general(left, right, (((1,), (1,)), ((), ())), preferred_element_type=F32)
 
 
-def place(where, out, az, ax, block):
-    zh, y = where[0], where[1]
-    far = lax.rem(lax.div(az, 2) + zh, 2)
-    ay = lax.rem(az, 2) * 2 + lax.div(ax, 2)
-    out[far, lax.rem(ay + 4 - y, 4), lax.rem(ax, 2)] = block
-
-
-def shift_place_kernel(where, *refs):
+def place_kernel(where, *refs):
+    out = refs[-1]
+    zh, y, zl, x = (where[i] for i in range(4))
     for kz in range(4):
         for kx in range(4):
-            az = lax.rem(where[2] + 4 - kz, 4)
-            ax = lax.rem(where[3] + 4 - kx, 4)
-            place(where, refs[-1], az, ax, refs[kx][kz])
-
-
-def flip_place_kernel(where, near, far, out):
-    for kz in range(4):
-        for kx in range(4):
-            az = lax.bitwise_xor(where[2], kz)
-            ax = lax.bitwise_xor(where[3], kx)
-            place(where, out, az, ax, (near, far)[kx // 2][kx % 2, kz])
-
-
-def col_place(kernel, where, pieces):
-    rows, width = pieces[0].shape[-2:]
-    return call(kernel, [((2, 4, 2, rows, width), BF16)], pieces, where=where)[0]
+            az = lax.rem(zl + 4 - kz, 4)
+            ax = lax.rem(x + 4 - kx, 4)
+            far = lax.rem(lax.div(az, 2) + zh, 2)
+            ay = lax.rem(az, 2) * 2 + lax.div(ax, 2)
+            out[far, lax.rem(ay + 4 - y, 4), lax.rem(ax, 2)] = refs[kx][kz]
 
 
 def shifts(value, axis):
@@ -113,17 +97,12 @@
     return [own, three, two, one]
 
 
-def gather_shifts(where, own):
+def core_gather(where, own):
     line = jnp.stack(shifts(own, "zl"))
-    return col_place(shift_place_kernel, where, shifts(line, "x"))
-
-
-def gather_flips(where, own):
-    pair = jnp.stack([own, flip(own, "zl", 1)])
-    line = jnp.concatenate([pair, flip(pair, "zl", 2)])
-    lines = jnp.stack([line, flip(line, "x", 1)])
-    rest = flip(lines, "x", 2)
-    return col_place(flip_place_kernel, where, [lines, rest])
+    pieces = shifts(line, "x")
+    rows, width = own.shape
+    out = ((2, 4, 2, rows, width), BF16)
+    return call(place_kernel, [out], pieces, where=where)[0]
 
 
 def own_act_kernel(half, weight, part, first):
@@ -387,7 +366,7 @@
         ]
     ).reshape(token_rows, width)
 
-    grad_half = gather_shifts(where, out_grad)
+    grad_half = core_gather(where, out_grad)
     grad_other = swap(grad_half, "c")
 
     pre_near = jnp.stack([preact, flip(preact, "y", 1)])
@@ -423,7 +402,7 @@
     got = [shift(s, "zl", k) for k, s in zip((1, 2, 3), sends)]
     grad_inputs = grad_inputs + sum(g.astype(F32) for g in got)
 
-    input_half = gather_flips(where, inputs)
+    input_half = core_gather(where, inputs)
     halves = (input_half, swap(input_half, "c"))
     grad_first = first_product(near + far, halves, factor)
     grad_second = second_product(

time: 184 us -> 181 us (0.984)
    ppermute x7 -> x3, starting transfers between devices: 11.5 us -> 3.96 us  [flip(): return lax.ppermute(value, axis, [(i, i ^ mask) for i in range(size)])]
    ppermute x27 -> x33, starting transfers between devices: 76 us -> 81.1 us  [shift(): lax.ppermute(value, axis, [(i, (i + step) % size) for i in range(size)])]
    ppermute x7 -> x3, waiting for transfers between devices: 17.7 us -> 13.1 us  [flip(): return lax.ppermute(value, axis, [(i, i ^ mask) for i in range(size)])]
    ppermute x7, waiting for transfers between devices: 3.54 us -> 7.44 us  [swap(): return lax.ppermute(value, axis, [(0, 1), (1, 0)])]
    ppermute x7, starting transfers between devices: 14.3 us -> 16.9 us  [swap(): return lax.ppermute(value, axis, [(0, 1), (1, 0)])]
    ppermute x27 -> x33, waiting for transfers between devices: 30 us -> 29 us  [shift(): lax.ppermute(value, axis, [(i, (i + step) % size) for i in range(size)])]
  transfers between devices with their start and end apart: 41 -> 43, of which waited for: 14 -> 16; matrix products, arithmetic and copies ran while one was open for 0% -> 0% of each run, Pallas kernels for 13% -> 13%
where the time goes in v3:
time: 181 us
  starting transfers between devices  102 us (56%)
  waiting for transfers between devices  49.5 us (27%)
  Pallas kernels  24.5 us (14%)
  other arithmetic  2.37 us (1%)
  local copies, waits for them, and re-layouts  1.85 us (1%)
    ppermute x33, starting transfers between devices, shift(): lax.ppermute(value, axis, [(i, (i + step) % size) for i in range(size)])  81.1 us
    ppermute x33, waiting for transfers between devices, shift(): lax.ppermute(value, axis, [(i, (i + step) % size) for i in range(size)])  29 us
    pallas_call x13, Pallas kernels, call(): pl.pallas_call(kernel, out_shape=tuple((make(shape, dtype) for shape, dty...  24.5 us
    ppermute x7, starting transfers between devices, swap(): return lax.ppermute(value, axis, [(0, 1), (1, 0)])  16.9 us
    ppermute x3, waiting for transfers between devices, flip(): return lax.ppermute(value, axis, [(i, i ^ mask) for i in range(size)])  13.1 us
    ppermute x7, waiting for transfers between devices, swap(): return lax.ppermute(value, axis, [(0, 1), (1, 0)])  7.44 us
    ppermute x3, starting transfers between devices, flip(): return lax.ppermute(value, axis, [(i, i ^ mask) for i in range(size)])  3.96 us
  transfers between devices with their start and end apart: 43, of which 16 were waited for; matrix products, arithmetic and copies ran while one was open for 0% of the time, Pallas kernels for 13%

profile of v3, /device:TPU:8, one launch (start us, length us, event | category | flops | bytes accessed | tf_op | source)
XLA Modules:
  0.0 181.1 jit_solution(6765538301768555296)
XLA Ops:
  2.6 3.3 %collective-permute-start.1 = (bf16[32,1152]{1,0:T(8,128)(2,1)}, bf16[32,1152]{1,0:T(8,128)(2,1)S(1)}, u32[]{:S(2)}, u32[]{:S(2)}) collective-permute-start(bf16[32,1152]{1,0:T(8,128)(2,1)} %param.6), channel_id=1, source_target_pairs={{0,16},{8,24},{16,0},{24,8},{1,17},{9,25},{17,1},{25,9},{2,18},{10... | collective-permute-start | bytes 221192 | tf_op jit(solution)/shard_map/ppermute | solution.py:30
  8.5 2.5 %collective-permute-done.1 = bf16[32,1152]{1,0:T(8,128)(2,1)S(1)} collective-permute-done((bf16[32,1152]{1,0:T(8,128)(2,1)}, bf16[32,1152]{1,0:T(8,128)(2,1)S(1)}, u32[]{:S(2)}, u32[]{:S(2)}) %collective-permute-start.1) | collective-permute-done | bytes 73760 | tf_op jit(solution)/shard_map/ppermute | solution.py:30
  14.0 2.7 %collective-permute-start.4 = (bf16[4,32,1152]{2,1,0:T(8,128)(2,1)S(1)}, bf16[4,32,1152]{2,1,0:T(8,128)(2,1)S(1)}, u32[]{:S(2)}, u32[]{:S(2)}) collective-permute-start(bf16[4,32,1152]{2,1,0:T(8,128)(2,1)S(1)} %pad_maximum_fusion.1.refs_0_), channel_id=1, source_target_pairs={{0,4},{2,6},{4,0},{6,2},{1,5},{3,7},{5,1},{7,3},{8,12},{10,14},{12... | collective-permute-start | bytes 884744 | tf_op jit(solution)/shard_map/ppermute | solution.py:30
  18.2 4.4 %collective-permute-done.3.refs_1_ = bf16[4,32,1152]{2,1,0:T(8,128)(2,1)S(1)} collective-permute-done((bf16[4,32,1152]{2,1,0:T(8,128)(2,1)S(1)}, bf16[4,32,1152]{2,1,0:T(8,128)(2,1)S(1)}, u32[]{:S(2)}, u32[]{:S(2)}) %collective-permute-start.3) | collective-permute-done | bytes 294944 | tf_op jit(solution)/shard_map/ppermute | solution.py:30
  22.6 6.8 %collective-permute-done.4.refs_2_ = bf16[4,32,1152]{2,1,0:T(8,128)(2,1)S(1)} collective-permute-done((bf16[4,32,1152]{2,1,0:T(8,128)(2,1)S(1)}, bf16[4,32,1152]{2,1,0:T(8,128)(2,1)S(1)}, u32[]{:S(2)}, u32[]{:S(2)}) %collective-permute-start.4) | collective-permute-done | bytes 294944 | tf_op jit(solution)/shard_map/ppermute | solution.py:30
  41.0 2.4 %collective-permute-start.12 = (bf16[128,1152]{1,0:T(8,128)(2,1)S(1)}, bf16[128,1152]{1,0:T(8,128)(2,1)S(1)}, u32[]{:S(2)}, u32[]{:S(2)}) collective-permute-start(bf16[128,1152]{1,0:T(8,128)(2,1)S(1)} %get-tuple-element.38), channel_id=1, source_target_pairs={{0,96},{32,0},{64,32},{96,64},{1,97},{33,1},{65,33},{97,65},{2,98}... | collective-permute-start | bytes 884744 | tf_op jit(solution)/shard_map/ppermute | solution.py:30
  44.5 3.9 %collective-permute-done.10 = bf16[128,1152]{1,0:T(8,128)(2,1)S(1)} collective-permute-done((bf16[128,1152]{1,0:T(8,128)(2,1)S(1)}, bf16[128,1152]{1,0:T(8,128)(2,1)S(1)}, u32[]{:S(2)}, u32[]{:S(2)}) %collective-permute-start.10) | collective-permute-done | bytes 294944 | tf_op jit(solution)/shard_map/ppermute | solution.py:30
  51.4 5.3 %collective-permute-start.7 = (bf16[128,1152]{1,0:T(8,128)(2,1)S(1)}, bf16[128,1152]{1,0:T(8,128)(2,1)S(1)}, u32[]{:S(2)}, u32[]{:S(2)}) collective-permute-start(bf16[128,1152]{1,0:T(8,128)(2,1)S(1)} %get-tuple-element.32), channel_id=1, source_target_pairs={{0,32},{32,64},{64,96},{96,0},{1,33},{33,65},{65,97},{97,1},{2,34}... | collective-permute-start | bytes 884744 | tf_op jit(solution)/shard_map/ppermute | solution.py:30
  59.3 5.5 %collective-permute-start.13 = (bf16[128,1152]{1,0:T(8,128)(2,1)S(1)}, bf16[128,1152]{1,0:T(8,128)(2,1)S(1)}, u32[]{:S(2)}, u32[]{:S(2)}) collective-permute-start(bf16[128,1152]{1,0:T(8,128)(2,1)S(1)} %add_convert_fusion), channel_id=1, source_target_pairs={{0,128},{128,0},{1,129},{129,1},{2,130},{130,2},{3,131},{131,3},{4... | collective-permute-start | bytes 884744 | tf_op jit(solution)/shard_map/ppermute | solution.py:39
  66.3 2.7 %collective-permute-start.35 = (bf16[4,32,1152]{2,1,0:T(8,128)(2,1)S(1)}, bf16[4,32,1152]{2,1,0:T(8,128)(2,1)S(1)}, u32[]{:S(2)}, u32[]{:S(2)}) collective-permute-start(bf16[4,32,1152]{2,1,0:T(8,128)(2,1)S(1)} %pad_maximum_fusion.3.refs_0_), channel_id=1, source_target_pairs={{0,2},{2,4},{4,6},{6,0},{1,3},{3,5},{5,7},{7,1},{8,10},{10,12},{12... | collective-permute-start | bytes 884744 | tf_op jit(solution)/shard_map/ppermute | solution.py:30
  69.0 2.4 %collective-permute-start.36 = (bf16[4,32,1152]{2,1,0:T(8,128)(2,1)S(1)}, bf16[4,32,1152]{2,1,0:T(8,128)(2,1)S(1)}, u32[]{:S(2)}, u32[]{:S(2)}) collective-permute-start(bf16[4,32,1152]{2,1,0:T(8,128)(2,1)S(1)} %pad_maximum_fusion.3.refs_0_), channel_id=1, source_target_pairs={{0,4},{2,6},{4,0},{6,2},{1,5},{3,7},{5,1},{7,3},{8,12},{10,14},{12... | collective-permute-start | bytes 884744 | tf_op jit(solution)/shard_map/ppermute | solution.py:30
  72.3 2.3 %collective-permute-start.37 = (bf16[4,32,1152]{2,1,0:T(8,128)(2,1)S(1)}, bf16[4,32,1152]{2,1,0:T(8,128)(2,1)S(1)}, u32[]{:S(2)}, u32[]{:S(2)}) collective-permute-start(bf16[4,32,1152]{2,1,0:T(8,128)(2,1)S(1)} %pad_maximum_fusion.3.refs_0_), channel_id=1, source_target_pairs={{0,6},{2,0},{4,2},{6,4},{1,7},{3,1},{5,3},{7,5},{8,14},{10,8},{12,... | collective-permute-start | bytes 884744 | tf_op jit(solution)/shard_map/ppermute | solution.py:30
  75.0 5.6 %collective-permute-start.21 = (bf16[128,1152]{1,0:T(8,128)(2,1)S(1)}, bf16[128,1152]{1,0:T(8,128)(2,1)S(1)}, u32[]{:S(2)}, u32[]{:S(2)}) collective-permute-start(bf16[128,1152]{1,0:T(8,128)(2,1)S(1)} %fusion.7.p0.refs_0_), channel_id=1, source_target_pairs={{0,128},{128,0},{1,129},{129,1},{2,130},{130,2},{3,131},{131,3},{4... | collective-permute-start | bytes 884744 | tf_op jit(solution)/shard_map/ppermute | solution.py:39
  80.6 2.5 %collective-permute-start.14 = (bf16[128,1152]{1,0:T(8,128)(2,1)S(1)}, bf16[128,1152]{1,0:T(8,128)(2,1)S(1)}, u32[]{:S(2)}, u32[]{:S(2)}) collective-permute-start(bf16[128,1152]{1,0:T(8,128)(2,1)S(1)} %fusion.7.p0.refs_0_), channel_id=1, source_target_pairs={{0,96},{32,0},{64,32},{96,64},{1,97},{33,1},{65,33},{97,65},{2,98}... | collective-permute-start | bytes 884744 | tf_op jit(solution)/shard_map/ppermute | solution.py:30
  85.0 2.3 %collective-permute-start.16 = (bf16[128,1152]{1,0:T(8,128)(2,1)S(1)}, bf16[128,1152]{1,0:T(8,128)(2,1)S(1)}, u32[]{:S(2)}, u32[]{:S(2)}) collective-permute-start(bf16[128,1152]{1,0:T(8,128)(2,1)S(1)} %fusion.7.p0.refs_0_), channel_id=1, source_target_pairs={{0,32},{32,64},{64,96},{96,0},{1,33},{33,65},{65,97},{97,1},{2,34}... | collective-permute-start | bytes 884744 | tf_op jit(solution)/shard_map/ppermute | solution.py:30
  87.4 5.4 %collective-permute-start.40 = (bf16[2,128,1152]{2,1,0:T(8,128)(2,1)S(1)}, bf16[2,128,1152]{2,1,0:T(8,128)(2,1)S(1)}, u32[]{:S(2)}, u32[]{:S(2)}) collective-permute-start(bf16[2,128,1152]{2,1,0:T(8,128)(2,1)S(1)} %pad_maximum_fusion.refs_1_), channel_id=1, source_target_pairs={{0,128},{128,0},{1,129},{129,1},{2,130},{130,2},{3,131},{131,3},{4... | collective-permute-start | bytes 1769480 | tf_op jit(solution)/shard_map/ppermute | solution.py:39
  92.8 5.9 %collective-permute-start.23 = (bf16[128,1152]{1,0:T(8,128)(2,1)S(1)}, bf16[128,1152]{1,0:T(8,128)(2,1)S(1)}, u32[]{:S(2)}, u32[]{:S(2)}) collective-permute-start(bf16[128,1152]{1,0:T(8,128)(2,1)S(1)} %collective-permute-done.21.p0.refs_4_), channel_id=1, source_target_pairs={{0,64},{32,96},{64,0},{96,32},{1,65},{33,97},{65,1},{97,33},{2,66}... | collective-permute-start | bytes 884744 | tf_op jit(solution)/shard_map/ppermute | solution.py:30
  100.6 2.9 %shard_map.80 = (bf16[4,2,32,1152]{3,2,1,0:T(8,128)(2,1)S(1)}, f32[4,2,32,1152]{3,2,1,0:T(8,128)S(1)}) custom-call(s32[5]{0:T(128)S(1)} %stack.64.where.refs_0_, bf16[128,1152]{1,0:T(8,128)(2,1)S(1)} %fusion.7.p0.refs_0_, bf16[128,1152]{1,0:T(8,128)(2,1)S(1)} %collective-permute-done.14.p1.refs_1_, bf16[128,1152]{1,0:T(8,128)(2,1)S(1)} %collective-permute-done.15.p2.refs_2_, ...), custom_call_target="tpu_custom_call" | custom-call | flops 1358954496 | bytes 3833856 | tf_op jit(solution)/shard_map/pallas_call | solution.py:58
  104.2 3.9 %collective-permute-done.23.p2.refs_6_ = bf16[128,1152]{1,0:T(8,128)(2,1)S(1)} collective-permute-done((bf16[128,1152]{1,0:T(8,128)(2,1)S(1)}, bf16[128,1152]{1,0:T(8,128)(2,1)S(1)}, u32[]{:S(2)}, u32[]{:S(2)}) %collective-permute-start.23) | collective-permute-done | bytes 294944 | tf_op jit(solution)/shard_map/ppermute | solution.py:30
  109.2 2.9 %shard_map.82 = (bf16[4,2,32,1152]{3,2,1,0:T(8,128)(2,1)S(1)}, f32[4,2,32,1152]{3,2,1,0:T(8,128)S(1)}) custom-call(s32[5]{0:T(128)S(1)} %stack.64.where.refs_0_, bf16[128,1152]{1,0:T(8,128)(2,1)S(1)} %collective-permute-done.21.p0.refs_4_, bf16[128,1152]{1,0:T(8,128)(2,1)S(1)} %collective-permute-done.22.p1.refs_5_, ...), custom_call_target="tpu_custom_call" | custom-call | flops 1358954496 | bytes 3833856 | tf_op jit(solution)/shard_map/pallas_call | solution.py:58
  112.2 2.5 %collective-permute-start.42 = (bf16[2,128,1152]{2,1,0:T(8,128)(2,1)S(1)}, bf16[2,128,1152]{2,1,0:T(8,128)(2,1)S(1)}, u32[]{:S(2)}, u32[]{:S(2)}) collective-permute-start(bf16[2,128,1152]{2,1,0:T(8,128)(2,1)S(1)} %pad_maximum_fusion.refs_1_), channel_id=1, source_target_pairs={{0,64},{32,96},{64,0},{96,32},{1,65},{33,97},{65,1},{97,33},{2,66}... | collective-permute-start | bytes 1769480 | tf_op jit(solution)/shard_map/ppermute | solution.py:35
  114.8 7.4 %collective-permute-done.40.refs_1_ = bf16[2,128,1152]{2,1,0:T(8,128)(2,1)S(1)} collective-permute-done((bf16[2,128,1152]{2,1,0:T(8,128)(2,1)S(1)}, bf16[2,128,1152]{2,1,0:T(8,128)(2,1)S(1)}, u32[]{:S(2)}, u32[]{:S(2)}) %collective-permute-start.40) | collective-permute-done | bytes 589856 | tf_op jit(solution)/shard_map/ppermute | solution.py:39
  122.3 3.3 %collective-permute-start.18 = (bf16[2,32,1152]{2,1,0:T(8,128)(2,1)S(1)}, bf16[2,32,1152]{2,1,0:T(8,128)(2,1)S(1)}, u32[]{:S(2)}, u32[]{:S(2)}) collective-permute-start(bf16[2,32,1152]{2,1,0:T(8,128)(2,1)S(1)} %get-tuple-element.42), channel_id=1, source_target_pairs={{0,2},{2,4},{4,6},{6,0},{1,3},{3,5},{5,7},{7,1},{8,10},{10,12},{12... | collective-permute-start | bytes 442376 | tf_op jit(solution)/shard_map/ppermute | solution.py:30
  125.6 2.3 %collective-permute-start.19 = (bf16[2,32,1152]{2,1,0:T(8,128)(2,1)S(1)}, bf16[2,32,1152]{2,1,0:T(8,128)(2,1)S(1)}, u32[]{:S(2)}, u32[]{:S(2)}) collective-permute-start(bf16[2,32,1152]{2,1,0:T(8,128)(2,1)S(1)} %get-tuple-element.43), channel_id=1, source_target_pairs={{0,4},{2,6},{4,0},{6,2},{1,5},{3,7},{5,1},{7,3},{8,12},{10,14},{12... | collective-permute-start | bytes 442376 | tf_op jit(solution)/shard_map/ppermute | solution.py:30
  131.0 11.1 %collective-permute-done.41.refs_2_ = bf16[2,128,1152]{2,1,0:T(8,128)(2,1)S(1)} collective-permute-done((bf16[2,128,1152]{2,1,0:T(8,128)(2,1)S(1)}, bf16[2,128,1152]{2,1,0:T(8,128)(2,1)S(1)}, u32[]{:S(2)}, u32[]{:S(2)}) %collective-permute-start.41) | collective-permute-done | bytes 589856 | tf_op jit(solution)/shard_map/ppermute | solution.py:35
  142.1 2.4 %collective-permute-start.27 = (bf16[2,32,1152]{2,1,0:T(8,128)(2,1)S(1)}, bf16[2,32,1152]{2,1,0:T(8,128)(2,1)S(1)}, u32[]{:S(2)}, u32[]{:S(2)}) collective-permute-start(bf16[2,32,1152]{2,1,0:T(8,128)(2,1)S(1)} %get-tuple-element.49), channel_id=1, source_target_pairs={{0,4},{2,6},{4,0},{6,2},{1,5},{3,7},{5,1},{7,3},{8,12},{10,14},{12... | collective-permute-start | bytes 442376 | tf_op jit(solution)/shard_map/ppermute | solution.py:30
  145.9 3.3 %shard_map.87.refs_5_ = f32[1152,1152]{1,0:T(8,128)S(1)} custom-call(s32[5]{0:T(128)S(1)} %stack.64.where.refs_0_, bf16[2,128,1152]{2,1,0:T(8,128)(2,1)S(1)} %pad_maximum_fusion.refs_1_, bf16[2,128,1152]{2,1,0:T(8,128)(2,1)S(1)} %collective-permute-done.42.refs_2_, bf16[2,4,2,32,1152]{4,3,2,1,0:T(8,128)(2,1)S(1)} %shard_map.76.half.refs_3_, ...), custom_call_target="tpu_custom_call" | custom-call | flops 1358954496 | bytes 3538944 | tf_op jit(solution)/shard_map/pallas_call | solution.py:58
  149.1 4.3 %shard_map.88 = bf16[1152,1152]{1,0:T(8,128)(2,1)} custom-call(s32[5]{0:T(128)S(1)} %stack.64.where.refs_0_, bf16[2,128,1152]{2,1,0:T(8,128)(2,1)S(1)} %collective-permute-done.40.refs_1_, bf16[2,128,1152]{2,1,0:T(8,128)(2,1)S(1)} %collective-permute-done.41.refs_2_, bf16[2,4,2,32,1152]{4,3,2,1,0:T(8,128)(2,1)S(1)} %shard_map.76.half.refs_3_, ...), custom_call_target="tpu_custom_call" | custom-call | flops 1358954496 | bytes 6193152 | tf_op jit(solution)/shard_map/pallas_call | solution.py:58
  154.2 13.5 %collective-permute-start.29 = (bf16[32,1152]{1,0:T(8,128)(2,1)S(1)}, bf16[32,1152]{1,0:T(8,128)(2,1)S(1)}, u32[]{:S(2)}, u32[]{:S(2)}) collective-permute-start(bf16[32,1152]{1,0:T(8,128)(2,1)S(1)} %get-tuple-element.52), channel_id=1, source_target_pairs={{0,8},{8,16},{16,24},{24,0},{1,9},{9,17},{17,25},{25,1},{2,10},{10... | collective-permute-start | bytes 221192 | tf_op jit(solution)/shard_map/ppermute | solution.py:30
  167.7 4.9 %collective-permute-start.30 = (bf16[32,1152]{1,0:T(8,128)(2,1)S(1)}, bf16[32,1152]{1,0:T(8,128)(2,1)S(1)}, u32[]{:S(2)}, u32[]{:S(2)}) collective-permute-start(bf16[32,1152]{1,0:T(8,128)(2,1)S(1)} %get-tuple-element.53), channel_id=1, source_target_pairs={{0,16},{8,24},{16,0},{24,8},{1,17},{9,25},{17,1},{25,9},{2,18},{10... | collective-permute-start | bytes 221192 | tf_op jit(solution)/shard_map/ppermute | solution.py:30
  172.7 2.8 %collective-permute-start.31 = (bf16[32,1152]{1,0:T(8,128)(2,1)S(1)}, bf16[32,1152]{1,0:T(8,128)(2,1)S(1)}, u32[]{:S(2)}, u32[]{:S(2)}) collective-permute-start(bf16[32,1152]{1,0:T(8,128)(2,1)S(1)} %get-tuple-element.54), channel_id=1, source_target_pairs={{0,24},{8,0},{16,8},{24,16},{1,25},{9,1},{17,9},{25,17},{2,26},{10... | collective-permute-start | bytes 221192 | tf_op jit(solution)/shard_map/ppermute | solution.py:30
  175.5 4.8 %shard_map.86 = bf16[1152,1152]{1,0:T(8,128)(2,1)} custom-call(bf16[128,1152]{1,0:T(8,128)(2,1)S(1)} %fusion.7.p0.refs_0_, bf16[128,1152]{1,0:T(8,128)(2,1)S(1)} %collective-permute-done.14.p1.refs_1_, bf16[128,1152]{1,0:T(8,128)(2,1)S(1)} %collective-permute-done.15.p2.refs_2_, bf16[128,1152]{1,0:T(8,128)(2,1)S(1)} %collective-permute-done.16.p3.refs_3_, ...), custom_call_target="tpu_custom_call" | custom-call | flops 2717908992 | bytes 4718592 | tf_op jit(solution)/shard_map/pallas_call | solution.py:58
  (84 shorter events, 41.9 us)
Async XLA Ops:
  14.0 15.4 %collective-permute-start.4 = (bf16[4,32,1152]{2,1,0:T(8,128)(2,1)S(1)}, bf16[4,32,1152]{2,1,0:T(8,128)(2,1)S(1)}, u32[]{:S(2)}, u32[]{:S(2)}) collective-permute-start(bf16[4,32,1152]{2,1,0:T(8,128)(2,1)S(1)} %pad_maximum_fusion.1.refs_0_), channel_id=1, source_target_pairs={{0,4},{2,6},{4,0},{6,2},{1,5},{3,7},{5,1},{7,3},{8,12},{10,14},{12... | collective-permute-start | bytes 884744 | tf_op jit(solution)/shard_map/ppermute | solution.py:30
  16.7 12.7 %collective-permute-start.5 = (bf16[4,32,1152]{2,1,0:T(8,128)(2,1)S(1)}, bf16[4,32,1152]{2,1,0:T(8,128)(2,1)S(1)}, u32[]{:S(2)}, u32[]{:S(2)}) collective-permute-start(bf16[4,32,1152]{2,1,0:T(8,128)(2,1)S(1)} %pad_maximum_fusion.1.refs_0_), channel_id=1, source_target_pairs={{0,6},{2,0},{4,2},{6,4},{1,7},{3,1},{5,3},{7,5},{8,14},{10,8},{12,... | collective-permute-start | bytes 884744 | tf_op jit(solution)/shard_map/ppermute | solution.py:30
  30.2 28.4 %collective-permute-start.32 = (bf16[32,1152]{1,0:T(8,128)(2,1)S(1)}, bf16[32,1152]{1,0:T(8,128)(2,1)S(1)}, u32[]{:S(2)}, u32[]{:S(2)}) collective-permute-start(bf16[32,1152]{1,0:T(8,128)(2,1)S(1)} %copy-done.3), channel_id=1, source_target_pairs={{0,8},{8,16},{16,24},{24,0},{1,9},{9,17},{17,25},{25,1},{2,10},{10... | collective-permute-start | bytes 221192 | tf_op jit(solution)/shard_map/ppermute | solution.py:30
  32.4 26.8 %collective-permute-start.33 = (bf16[32,1152]{1,0:T(8,128)(2,1)S(1)}, bf16[32,1152]{1,0:T(8,128)(2,1)S(1)}, u32[]{:S(2)}, u32[]{:S(2)}) collective-permute-start(bf16[32,1152]{1,0:T(8,128)(2,1)S(1)} %copy-done.3), channel_id=1, source_target_pairs={{0,16},{8,24},{16,0},{24,8},{1,17},{9,25},{17,1},{25,9},{2,18},{10... | collective-permute-start | bytes 221192 | tf_op jit(solution)/shard_map/ppermute | solution.py:30
  40.1 11.4 %collective-permute-start.11 = (bf16[128,1152]{1,0:T(8,128)(2,1)S(1)}, bf16[128,1152]{1,0:T(8,128)(2,1)S(1)}, u32[]{:S(2)}, u32[]{:S(2)}) collective-permute-start(bf16[128,1152]{1,0:T(8,128)(2,1)S(1)} %get-tuple-element.37), channel_id=1, source_target_pairs={{0,64},{32,96},{64,0},{96,32},{1,65},{33,97},{65,1},{97,33},{2,66}... | collective-permute-start | bytes 884744 | tf_op jit(solution)/shard_map/ppermute | solution.py:30
  41.0 15.7 %collective-permute-start.12 = (bf16[128,1152]{1,0:T(8,128)(2,1)S(1)}, bf16[128,1152]{1,0:T(8,128)(2,1)S(1)}, u32[]{:S(2)}, u32[]{:S(2)}) collective-permute-start(bf16[128,1152]{1,0:T(8,128)(2,1)S(1)} %get-tuple-element.38), channel_id=1, source_target_pairs={{0,96},{32,0},{64,32},{96,64},{1,97},{33,1},{65,33},{97,65},{2,98}... | collective-permute-start | bytes 884744 | tf_op jit(solution)/shard_map/ppermute | solution.py:30
  48.4 16.4 %collective-permute-start.34 = (bf16[32,1152]{1,0:T(8,128)(2,1)S(1)}, bf16[32,1152]{1,0:T(8,128)(2,1)S(1)}, u32[]{:S(2)}, u32[]{:S(2)}) collective-permute-start(bf16[32,1152]{1,0:T(8,128)(2,1)S(1)} %copy-done.3), channel_id=1, source_target_pairs={{0,24},{8,0},{16,8},{24,16},{1,25},{9,1},{17,9},{25,17},{2,26},{10... | collective-permute-start | bytes 221192 | tf_op jit(solution)/shard_map/ppermute | solution.py:30
  51.4 14.9 %collective-permute-start.7 = (bf16[128,1152]{1,0:T(8,128)(2,1)S(1)}, bf16[128,1152]{1,0:T(8,128)(2,1)S(1)}, u32[]{:S(2)}, u32[]{:S(2)}) collective-permute-start(bf16[128,1152]{1,0:T(8,128)(2,1)S(1)} %get-tuple-element.32), channel_id=1, source_target_pairs={{0,32},{32,64},{64,96},{96,0},{1,33},{33,65},{65,97},{97,1},{2,34}... | collective-permute-start | bytes 884744 | tf_op jit(solution)/shard_map/ppermute | solution.py:30
  56.7 12.3 %collective-permute-start.8 = (bf16[128,1152]{1,0:T(8,128)(2,1)S(1)}, bf16[128,1152]{1,0:T(8,128)(2,1)S(1)}, u32[]{:S(2)}, u32[]{:S(2)}) collective-permute-start(bf16[128,1152]{1,0:T(8,128)(2,1)S(1)} %get-tuple-element.33), channel_id=1, source_target_pairs={{0,64},{32,96},{64,0},{96,32},{1,65},{33,97},{65,1},{97,33},{2,66}... | collective-permute-start | bytes 884744 | tf_op jit(solution)/shard_map/ppermute | solution.py:30
  58.7 13.6 %collective-permute-start.9 = (bf16[128,1152]{1,0:T(8,128)(2,1)S(1)}, bf16[128,1152]{1,0:T(8,128)(2,1)S(1)}, u32[]{:S(2)}, u32[]{:S(2)}) collective-permute-start(bf16[128,1152]{1,0:T(8,128)(2,1)S(1)} %get-tuple-element.34), channel_id=1, source_target_pairs={{0,96},{32,0},{64,32},{96,64},{1,97},{33,1},{65,33},{97,65},{2,98}... | collective-permute-start | bytes 884744 | tf_op jit(solution)/shard_map/ppermute | solution.py:30
  59.3 15.3 %collective-permute-start.13 = (bf16[128,1152]{1,0:T(8,128)(2,1)S(1)}, bf16[128,1152]{1,0:T(8,128)(2,1)S(1)}, u32[]{:S(2)}, u32[]{:S(2)}) collective-permute-start(bf16[128,1152]{1,0:T(8,128)(2,1)S(1)} %add_convert_fusion), channel_id=1, source_target_pairs={{0,128},{128,0},{1,129},{129,1},{2,130},{130,2},{3,131},{131,3},{4... | collective-permute-start | bytes 884744 | tf_op jit(solution)/shard_map/ppermute | solution.py:39
  64.8 15.8 %collective-permute-start.39 = (bf16[128,1152]{1,0:T(8,128)(2,1)S(1)}, bf16[128,1152]{1,0:T(8,128)(2,1)S(1)}, u32[]{:S(2)}, u32[]{:S(2)}) collective-permute-start(bf16[128,1152]{1,0:T(8,128)(2,1)S(1)} %bitcast.34), channel_id=1, source_target_pairs={{0,32},{32,0},{64,96},{96,64},{1,33},{33,1},{65,97},{97,65},{2,34}... | collective-permute-start | bytes 884744 | tf_op jit(solution)/shard_map/ppermute | solution.py:35
  66.3 16.8 %collective-permute-start.35 = (bf16[4,32,1152]{2,1,0:T(8,128)(2,1)S(1)}, bf16[4,32,1152]{2,1,0:T(8,128)(2,1)S(1)}, u32[]{:S(2)}, u32[]{:S(2)}) collective-permute-start(bf16[4,32,1152]{2,1,0:T(8,128)(2,1)S(1)} %pad_maximum_fusion.3.refs_0_), channel_id=1, source_target_pairs={{0,2},{2,4},{4,6},{6,0},{1,3},{3,5},{5,7},{7,1},{8,10},{10,12},{12... | collective-permute-start | bytes 884744 | tf_op jit(solution)/shard_map/ppermute | solution.py:30
  69.0 16.0 %collective-permute-start.36 = (bf16[4,32,1152]{2,1,0:T(8,128)(2,1)S(1)}, bf16[4,32,1152]{2,1,0:T(8,128)(2,1)S(1)}, u32[]{:S(2)}, u32[]{:S(2)}) collective-permute-start(bf16[4,32,1152]{2,1,0:T(8,128)(2,1)S(1)} %pad_maximum_fusion.3.refs_0_), channel_id=1, source_target_pairs={{0,4},{2,6},{4,0},{6,2},{1,5},{3,7},{5,1},{7,3},{8,12},{10,14},{12... | collective-permute-start | bytes 884744 | tf_op jit(solution)/shard_map/ppermute | solution.py:30
  72.3 15.1 %collective-permute-start.37 = (bf16[4,32,1152]{2,1,0:T(8,128)(2,1)S(1)}, bf16[4,32,1152]{2,1,0:T(8,128)(2,1)S(1)}, u32[]{:S(2)}, u32[]{:S(2)}) collective-permute-start(bf16[4,32,1152]{2,1,0:T(8,128)(2,1)S(1)} %pad_maximum_fusion.3.refs_0_), channel_id=1, source_target_pairs={{0,6},{2,0},{4,2},{6,4},{1,7},{3,1},{5,3},{7,5},{8,14},{10,8},{12,... | collective-permute-start | bytes 884744 | tf_op jit(solution)/shard_map/ppermute | solution.py:30
  75.0 17.8 %collective-permute-start.21 = (bf16[128,1152]{1,0:T(8,128)(2,1)S(1)}, bf16[128,1152]{1,0:T(8,128)(2,1)S(1)}, u32[]{:S(2)}, u32[]{:S(2)}) collective-permute-start(bf16[128,1152]{1,0:T(8,128)(2,1)S(1)} %fusion.7.p0.refs_0_), channel_id=1, source_target_pairs={{0,128},{128,0},{1,129},{129,1},{2,130},{130,2},{3,131},{131,3},{4... | collective-permute-start | bytes 884744 | tf_op jit(solution)/shard_map/ppermute | solution.py:39
  80.6 12.2 %collective-permute-start.14 = (bf16[128,1152]{1,0:T(8,128)(2,1)S(1)}, bf16[128,1152]{1,0:T(8,128)(2,1)S(1)}, u32[]{:S(2)}, u32[]{:S(2)}) collective-permute-start(bf16[128,1152]{1,0:T(8,128)(2,1)S(1)} %fusion.7.p0.refs_0_), channel_id=1, source_target_pairs={{0,96},{32,0},{64,32},{96,64},{1,97},{33,1},{65,33},{97,65},{2,98}... | collective-permute-start | bytes 884744 | tf_op jit(solution)/shard_map/ppermute | solution.py:30
  83.1 16.2 %collective-permute-start.15 = (bf16[128,1152]{1,0:T(8,128)(2,1)S(1)}, bf16[128,1152]{1,0:T(8,128)(2,1)S(1)}, u32[]{:S(2)}, u32[]{:S(2)}) collective-permute-start(bf16[128,1152]{1,0:T(8,128)(2,1)S(1)} %fusion.7.p0.refs_0_), channel_id=1, source_target_pairs={{0,64},{32,96},{64,0},{96,32},{1,65},{33,97},{65,1},{97,33},{2,66}... | collective-permute-start | bytes 884744 | tf_op jit(solution)/shard_map/ppermute | solution.py:30
  85.0 15.5 %collective-permute-start.16 = (bf16[128,1152]{1,0:T(8,128)(2,1)S(1)}, bf16[128,1152]{1,0:T(8,128)(2,1)S(1)}, u32[]{:S(2)}, u32[]{:S(2)}) collective-permute-start(bf16[128,1152]{1,0:T(8,128)(2,1)S(1)} %fusion.7.p0.refs_0_), channel_id=1, source_target_pairs={{0,32},{32,64},{64,96},{96,0},{1,33},{33,65},{65,97},{97,1},{2,34}... | collective-permute-start | bytes 884744 | tf_op jit(solution)/shard_map/ppermute | solution.py:30
  87.4 34.8 %collective-permute-start.40 = (bf16[2,128,1152]{2,1,0:T(8,128)(2,1)S(1)}, bf16[2,128,1152]{2,1,0:T(8,128)(2,1)S(1)}, u32[]{:S(2)}, u32[]{:S(2)}) collective-permute-start(bf16[2,128,1152]{2,1,0:T(8,128)(2,1)S(1)} %pad_maximum_fusion.refs_1_), channel_id=1, source_target_pairs={{0,128},{128,0},{1,129},{129,1},{2,130},{130,2},{3,131},{131,3},{4... | collective-permute-start | bytes 1769480 | tf_op jit(solution)/shard_map/ppermute | solution.py:39
  92.8 15.4 %collective-permute-start.23 = (bf16[128,1152]{1,0:T(8,128)(2,1)S(1)}, bf16[128,1152]{1,0:T(8,128)(2,1)S(1)}, u32[]{:S(2)}, u32[]{:S(2)}) collective-permute-start(bf16[128,1152]{1,0:T(8,128)(2,1)S(1)} %collective-permute-done.21.p0.refs_4_), channel_id=1, source_target_pairs={{0,64},{32,96},{64,0},{96,32},{1,65},{33,97},{65,1},{97,33},{2,66}... | collective-permute-start | bytes 884744 | tf_op jit(solution)/shard_map/ppermute | solution.py:30
  100.5 74.9 %collective-permute-start.38 = (bf16[2,4,2,32,1152]{4,3,2,1,0:T(8,128)(2,1)S(1)}, bf16[2,4,2,32,1152]{4,3,2,1,0:T(8,128)(2,1)S(1)}, u32[]{:S(2)}, u32[]{:S(2)}) collective-permute-start(bf16[2,4,2,32,1152]{4,3,2,1,0:T(8,128)(2,1)S(1)} %shard_map.85.refs_8_), channel_id=1, source_target_pairs={{0,1},{1,0},{2,3},{3,2},{4,5},{5,4},{6,7},{7,6},{8,9},{9,8},{10,11... | collective-permute-start | bytes 3538952 | tf_op jit(solution)/shard_map/ppermute | solution.py:39
  104.0 18.1 %collective-permute-start.17 = (bf16[4,2,32,1152]{3,2,1,0:T(8,128)(2,1)S(1)}, bf16[4,2,32,1152]{3,2,1,0:T(8,128)(2,1)S(1)}, u32[]{:S(2)}, u32[]{:S(2)}) collective-permute-start(bf16[4,2,32,1152]{3,2,1,0:T(8,128)(2,1)S(1)} %get-tuple-element.40), channel_id=1, source_target_pairs={{0,1},{1,0},{2,3},{3,2},{4,5},{5,4},{6,7},{7,6},{8,9},{9,8},{10,11... | collective-permute-start | bytes 1769480 | tf_op jit(solution)/shard_map/ppermute | solution.py:39
  112.1 13.4 %collective-permute-start.25 = (bf16[4,2,32,1152]{3,2,1,0:T(8,128)(2,1)S(1)}, bf16[4,2,32,1152]{3,2,1,0:T(8,128)(2,1)S(1)}, u32[]{:S(2)}, u32[]{:S(2)}) collective-permute-start(bf16[4,2,32,1152]{3,2,1,0:T(8,128)(2,1)S(1)} %get-tuple-element.46), channel_id=1, source_target_pairs={{0,1},{1,0},{2,3},{3,2},{4,5},{5,4},{6,7},{7,6},{8,9},{9,8},{10,11... | collective-permute-start | bytes 1769480 | tf_op jit(solution)/shard_map/ppermute | solution.py:39
  112.2 17.8 %collective-permute-start.42 = (bf16[2,128,1152]{2,1,0:T(8,128)(2,1)S(1)}, bf16[2,128,1152]{2,1,0:T(8,128)(2,1)S(1)}, u32[]{:S(2)}, u32[]{:S(2)}) collective-permute-start(bf16[2,128,1152]{2,1,0:T(8,128)(2,1)S(1)} %pad_maximum_fusion.refs_1_), channel_id=1, source_target_pairs={{0,64},{32,96},{64,0},{96,32},{1,65},{33,97},{65,1},{97,33},{2,66}... | collective-permute-start | bytes 1769480 | tf_op jit(solution)/shard_map/ppermute | solution.py:35
  122.2 19.9 %collective-permute-start.41 = (bf16[2,128,1152]{2,1,0:T(8,128)(2,1)S(1)}, bf16[2,128,1152]{2,1,0:T(8,128)(2,1)S(1)}, u32[]{:S(2)}, u32[]{:S(2)}) collective-permute-start(bf16[2,128,1152]{2,1,0:T(8,128)(2,1)S(1)} %collective-permute-done.40.refs_1_), channel_id=1, source_target_pairs={{0,64},{32,96},{64,0},{96,32},{1,65},{33,97},{65,1},{97,33},{2,66}... | collective-permute-start | bytes 1769480 | tf_op jit(solution)/shard_map/ppermute | solution.py:35
  122.3 19.8 %collective-permute-start.18 = (bf16[2,32,1152]{2,1,0:T(8,128)(2,1)S(1)}, bf16[2,32,1152]{2,1,0:T(8,128)(2,1)S(1)}, u32[]{:S(2)}, u32[]{:S(2)}) collective-permute-start(bf16[2,32,1152]{2,1,0:T(8,128)(2,1)S(1)} %get-tuple-element.42), channel_id=1, source_target_pairs={{0,2},{2,4},{4,6},{6,0},{1,3},{3,5},{5,7},{7,1},{8,10},{10,12},{12... | collective-permute-start | bytes 442376 | tf_op jit(solution)/shard_map/ppermute | solution.py:30
  125.6 19.0 %collective-permute-start.19 = (bf16[2,32,1152]{2,1,0:T(8,128)(2,1)S(1)}, bf16[2,32,1152]{2,1,0:T(8,128)(2,1)S(1)}, u32[]{:S(2)}, u32[]{:S(2)}) collective-permute-start(bf16[2,32,1152]{2,1,0:T(8,128)(2,1)S(1)} %get-tuple-element.43), channel_id=1, source_target_pairs={{0,4},{2,6},{4,0},{6,2},{1,5},{3,7},{5,1},{7,3},{8,12},{10,14},{12... | collective-permute-start | bytes 442376 | tf_op jit(solution)/shard_map/ppermute | solution.py:30
  130.0 23.4 %collective-permute-start.20 = (bf16[2,32,1152]{2,1,0:T(8,128)(2,1)S(1)}, bf16[2,32,1152]{2,1,0:T(8,128)(2,1)S(1)}, u32[]{:S(2)}, u32[]{:S(2)}) collective-permute-start(bf16[2,32,1152]{2,1,0:T(8,128)(2,1)S(1)} %get-tuple-element.44), channel_id=1, source_target_pairs={{0,6},{2,0},{4,2},{6,4},{1,7},{3,1},{5,3},{7,5},{8,14},{10,8},{12,... | collective-permute-start | bytes 442376 | tf_op jit(solution)/shard_map/ppermute | solution.py:30
  142.1 11.3 %collective-permute-start.27 = (bf16[2,32,1152]{2,1,0:T(8,128)(2,1)S(1)}, bf16[2,32,1152]{2,1,0:T(8,128)(2,1)S(1)}, u32[]{:S(2)}, u32[]{:S(2)}) collective-permute-start(bf16[2,32,1152]{2,1,0:T(8,128)(2,1)S(1)} %get-tuple-element.49), channel_id=1, source_target_pairs={{0,4},{2,6},{4,0},{6,2},{1,5},{3,7},{5,1},{7,3},{8,12},{10,14},{12... | collective-permute-start | bytes 442376 | tf_op jit(solution)/shard_map/ppermute | solution.py:30
  154.2 26.2 %collective-permute-start.29 = (bf16[32,1152]{1,0:T(8,128)(2,1)S(1)}, bf16[32,1152]{1,0:T(8,128)(2,1)S(1)}, u32[]{:S(2)}, u32[]{:S(2)}) collective-permute-start(bf16[32,1152]{1,0:T(8,128)(2,1)S(1)} %get-tuple-element.52), channel_id=1, source_target_pairs={{0,8},{8,16},{16,24},{24,0},{1,9},{9,17},{17,25},{25,1},{2,10},{10... | collective-permute-start | bytes 221192 | tf_op jit(solution)/shard_map/ppermute | solution.py:30
  167.7 12.6 %collective-permute-start.30 = (bf16[32,1152]{1,0:T(8,128)(2,1)S(1)}, bf16[32,1152]{1,0:T(8,128)(2,1)S(1)}, u32[]{:S(2)}, u32[]{:S(2)}) collective-permute-start(bf16[32,1152]{1,0:T(8,128)(2,1)S(1)} %get-tuple-element.53), channel_id=1, source_target_pairs={{0,16},{8,24},{16,0},{24,8},{1,17},{9,25},{17,1},{25,9},{2,18},{10... | collective-permute-start | bytes 221192 | tf_op jit(solution)/shard_map/ppermute | solution.py:30
  (15 other events, 131.4 us)

commit v4 on v3

--- a/solution.py
+++ b/solution.py
@@ -75,14 +75,15 @@
 
 def place_kernel(where, *refs):
     out = refs[-1]
-    zh, y, zl, x = (where[i] for i in range(4))
-    for kz in range(4):
+    y, zl, x = (where[i] for i in range(1, 4))
+
+    @pl.loop(0, 4)
+    def _(kz):
+        az = lax.rem(zl + 4 - kz, 4)
         for kx in range(4):
-            az = lax.rem(zl + 4 - kz, 4)
             ax = lax.rem(x + 4 - kx, 4)
-            far = lax.rem(lax.div(az, 2) + zh, 2)
             ay = lax.rem(az, 2) * 2 + lax.div(ax, 2)
-            out[far, lax.rem(ay + 4 - y, 4), lax.rem(ax, 2)] = refs[kx][kz]
+            out[lax.div(az, 2), lax.rem(ay + 4 - y, 4), lax.rem(ax, 2)] = refs[kx][kz]
 
 
 def shifts(value, axis):
@@ -98,7 +99,8 @@
 
 
 def core_gather(where, own):
-    line = jnp.stack(shifts(own, "zl"))
+    pieces = shifts(own, "zl")
+    line = jnp.stack(pieces)
     pieces = shifts(line, "x")
     rows, width = own.shape
     out = ((2, 4, 2, rows, width), BF16)
@@ -146,6 +148,42 @@
     )
 
 
+ROWS = 16
+
+
+def row_sum_kernel(keep, one, two, three, total, send):
+    @pl.loop(0, keep.shape[0] // ROWS)
+    def _(i):
+        r = pl.ds(pl.multiple_of(i * ROWS, ROWS), ROWS)
+        value = (
+            keep[r] + one[r].astype(F32) + two[r].astype(F32) + three[r].astype(F32)
+        )
+        total[r] = value
+        send[r] = value.astype(BF16)
+
+
+def row_sum(keep, got):
+    return call(row_sum_kernel, [(keep.shape, F32), (keep.shape, BF16)], [keep, *got])
+
+
+def hidden_kernel(plane, where, total, got, near, far, out):
+    @pl.loop(0, total.shape[0] // ROWS)
+    def _(i):
+        r = pl.ds(pl.multiple_of(i * ROWS, ROWS), ROWS)
+        values = jnp.where(where[0] == plane, near[r].astype(F32), far[0, r].astype(F32))
+        grad_act = total[r] + got[r].astype(F32)
+        out[r] = (grad_act * gelu_slope(values)).astype(BF16)
+
+
+def hidden(plane, where, total, got, near, far):
+    return call(
+        lambda *refs: hidden_kernel(plane, *refs),
+        [(total.shape, BF16)],
+        [total, got, near, far],
+        where=where,
+    )[0]
+
+
 def token_kernel(where, p0, p1, p2, p3, weight, away, keep, rows):
     y, x = where[1], where[3]
     block = rows.shape[3]
@@ -154,9 +192,11 @@
         for low in range(2):
             ax = lax.rem(ay, 2) * 2 + low
             kx = lax.rem(ax + 4 - x, 4)
-            for core in range(2):
-                start = (core * 2 + low) * block
-                rows[core, kx, lax.div(ay, 2)] = piece[start : start + block]
+
+            @pl.loop(0, 2)
+            def _(core):
+                start = pl.multiple_of((core * 2 + low) * block, block)
+                rows[core, kx, lax.div(ay, 2)] = piece[pl.ds(start, block)]
 
     @pl.loop(0, 2)
     def _(core):
@@ -195,7 +235,7 @@
 
 
 def line_kernel(where, *refs):
-    zh, zl = where[0], where[2]
+    zl = where[2]
     outs, sums = refs[8:12], refs[12]
     for plane in range(2):
         kept, one, two, three = refs[plane * 4 : plane * 4 + 4]
@@ -204,8 +244,7 @@
         )
     for k, out in enumerate(outs):
         az = lax.rem(zl + k, 4)
-        plane = lax.rem(lax.div(az, 2) + zh, 2)
-        out[...] = sums[plane, lax.rem(az, 2)].astype(out.dtype)
+        out[...] = sums[lax.div(az, 2), lax.rem(az, 2)].astype(out.dtype)
 
 
 def line_sums(where, lines):
@@ -276,7 +315,8 @@
 
     half = 4 * rows
     lefts = [lambda cols, n=n: act[n * half : (n + 1) * half, cols] for n in range(2)]
-    rights = [lambda h=h: h[plane].reshape(-1, width) for h in (own, other)]
+    tokens = lax.rem(where[0] + plane, 2)
+    rights = [lambda h=h: h[tokens].reshape(-1, width) for h in (own, other)]
     if plane:
         so_far, out, _, stage, sem = refs
         emit, finish = store_out(out, stage, sem, factor)
@@ -374,22 +414,24 @@
     pre_far = swap(pre_near, "zh")
     pre += [pre_far, flip(pre_far, "y", 2)]
 
-    part, first = own_act(grad_half, second_weight)
+    part, lead = own_act(grad_half, second_weight)
 
     def plane_sum(far):
-        keep, *sends = other_act(far, grad_other, second_weight, part, first)
-        got = [shift(s, "y", k) for k, s in zip((1, 2, 3), sends)]
-        return keep + sum(g.astype(F32) for g in got)
-
-    far_sum = plane_sum(1).astype(BF16)
-    near_sum = plane_sum(0)
-    from_far = swap(far_sum, "zh")
-    grad_act = near_sum + from_far.astype(F32)
-    grad_own = (grad_act * gelu_slope(preact.astype(F32))).astype(BF16)
-
-    near = spread(grad_own)
-    own_far = swap(grad_own, "zh")
-    far = spread(own_far)
+        keep, *sends = other_act(far, grad_other, second_weight, part, lead)
+        got = []
+        for k, value in zip((1, 2, 3), sends):
+            got.append(shift(value, "y", k))
+        return row_sum(keep, got)
+
+    sums = [plane_sum(0), plane_sum(1)]
+
+    def exchange(plane):
+        total, send = sums[plane]
+        return total, swap(send, "zh")
+
+    first = hidden(0, where, *exchange(0), preact, pre_far)
+    second = hidden(1, where, *exchange(1), preact, pre_far)
+    near, far = spread(first), spread(second)
 
     def plane_inputs(pieces):
         away, keep = token_products(where, pieces, first_weight)

time: 181 us -> 195 us (1.077)
  waiting for transfers between devices: 49.5 us -> 92.6 us
  starting transfers between devices: 102 us -> 70.3 us
  Pallas kernels: 24.5 us -> 27 us
    ppermute x33, waiting for transfers between devices: 29 us -> 63.6 us  [shift(): lax.ppermute(value, axis, [(i, (i + step) % size) for i in range(size)])]
    ppermute x33, starting transfers between devices: 81.1 us -> 56.1 us  [shift(): lax.ppermute(value, axis, [(i, (i + step) % size) for i in range(size)])]
    ppermute x7, starting transfers between devices: 16.9 us -> 9.78 us  [swap(): return lax.ppermute(value, axis, [(0, 1), (1, 0)])]
    ppermute x3, waiting for transfers between devices: 13.1 us -> 19.9 us  [flip(): return lax.ppermute(value, axis, [(i, i ^ mask) for i in range(size)])]
    pallas_call x13 -> x17, Pallas kernels: 24.5 us -> 27 us  [call(): pl.pallas_call(kernel, out_shape=tuple((make(shape, dtype) for shape, dty...]
  transfers between devices with their start and end apart: 43 -> 43, of which waited for: 16 -> 15; matrix products, arithmetic and copies ran while one was open for 0% -> 0% of each run, Pallas kernels for 13% -> 14%
where the time goes in v4:
time: 195 us
  waiting for transfers between devices  92.6 us (47%)
  starting transfers between devices  70.3 us (36%)
  Pallas kernels  27 us (14%)
    ppermute x33, waiting for transfers between devices, shift(): lax.ppermute(value, axis, [(i, (i + step) % size) for i in range(size)])  63.6 us
    ppermute x33, starting transfers between devices, shift(): lax.ppermute(value, axis, [(i, (i + step) % size) for i in range(size)])  56.1 us
    pallas_call x17, Pallas kernels, call(): pl.pallas_call(kernel, out_shape=tuple((make(shape, dtype) for shape, dty...  27 us
    ppermute x3, waiting for transfers between devices, flip(): return lax.ppermute(value, axis, [(i, i ^ mask) for i in range(size)])  19.9 us
    ppermute x7, starting transfers between devices, swap(): return lax.ppermute(value, axis, [(0, 1), (1, 0)])  9.78 us
    ppermute x7, waiting for transfers between devices, swap(): return lax.ppermute(value, axis, [(0, 1), (1, 0)])  9.08 us
    ppermute x3, starting transfers between devices, flip(): return lax.ppermute(value, axis, [(i, i ^ mask) for i in range(size)])  4.45 us
  transfers between devices with their start and end apart: 43, of which 15 were waited for; matrix products, arithmetic and copies ran while one was open for 0% of the time, Pallas kernels for 14%

profile of v4, /device:TPU:8, one launch (start us, length us, event | category | flops | bytes accessed | tf_op | source)
XLA Modules:
  0.0 194.7 jit_solution(13234388819578752906)
XLA Ops:
  2.6 3.3 %collective-permute-start.1 = (bf16[32,1152]{1,0:T(8,128)(2,1)}, bf16[32,1152]{1,0:T(8,128)(2,1)S(1)}, u32[]{:S(2)}, u32[]{:S(2)}) collective-permute-start(bf16[32,1152]{1,0:T(8,128)(2,1)} %param.6), channel_id=1, source_target_pairs={{0,16},{8,24},{16,0},{24,8},{1,17},{9,25},{17,1},{25,9},{2,18},{10... | collective-permute-start | bytes 221192 | tf_op jit(solution)/shard_map/ppermute | solution.py:30
  8.5 2.5 %collective-permute-done.1 = bf16[32,1152]{1,0:T(8,128)(2,1)S(1)} collective-permute-done((bf16[32,1152]{1,0:T(8,128)(2,1)}, bf16[32,1152]{1,0:T(8,128)(2,1)S(1)}, u32[]{:S(2)}, u32[]{:S(2)}) %collective-permute-start.1) | collective-permute-done | bytes 73760 | tf_op jit(solution)/shard_map/ppermute | solution.py:30
  14.0 2.7 %collective-permute-start.4 = (bf16[4,32,1152]{2,1,0:T(8,128)(2,1)S(1)}, bf16[4,32,1152]{2,1,0:T(8,128)(2,1)S(1)}, u32[]{:S(2)}, u32[]{:S(2)}) collective-permute-start(bf16[4,32,1152]{2,1,0:T(8,128)(2,1)S(1)} %pad_maximum_fusion.1.refs_0_), channel_id=1, source_target_pairs={{0,4},{2,6},{4,0},{6,2},{1,5},{3,7},{5,1},{7,3},{8,12},{10,14},{12... | collective-permute-start | bytes 884744 | tf_op jit(solution)/shard_map/ppermute | solution.py:30
  18.2 4.4 %collective-permute-done.3.refs_1_ = bf16[4,32,1152]{2,1,0:T(8,128)(2,1)S(1)} collective-permute-done((bf16[4,32,1152]{2,1,0:T(8,128)(2,1)S(1)}, bf16[4,32,1152]{2,1,0:T(8,128)(2,1)S(1)}, u32[]{:S(2)}, u32[]{:S(2)}) %collective-permute-start.3) | collective-permute-done | bytes 294944 | tf_op jit(solution)/shard_map/ppermute | solution.py:30
  22.6 6.8 %collective-permute-done.4.refs_2_ = bf16[4,32,1152]{2,1,0:T(8,128)(2,1)S(1)} collective-permute-done((bf16[4,32,1152]{2,1,0:T(8,128)(2,1)S(1)}, bf16[4,32,1152]{2,1,0:T(8,128)(2,1)S(1)}, u32[]{:S(2)}, u32[]{:S(2)}) %collective-permute-start.4) | collective-permute-done | bytes 294944 | tf_op jit(solution)/shard_map/ppermute | solution.py:30
  38.1 2.4 %collective-permute-start.20 = (bf16[128,1152]{1,0:T(8,128)(2,1)S(1)}, bf16[128,1152]{1,0:T(8,128)(2,1)S(1)}, u32[]{:S(2)}, u32[]{:S(2)}) collective-permute-start(bf16[128,1152]{1,0:T(8,128)(2,1)S(1)} %get-tuple-element.48), channel_id=1, source_target_pairs={{0,32},{32,64},{64,96},{96,0},{1,33},{33,65},{65,97},{97,1},{2,34}... | collective-permute-start | bytes 884744 | tf_op jit(solution)/shard_map/ppermute | solution.py:30
  43.3 5.9 %collective-permute-start.12 = (bf16[2,128,1152]{2,1,0:T(8,128)(2,1)S(1)}, bf16[2,128,1152]{2,1,0:T(8,128)(2,1)S(1)}, u32[]{:S(2)}, u32[]{:S(2)}) collective-permute-start(bf16[2,128,1152]{2,1,0:T(8,128)(2,1)S(1)} %pad_maximum_fusion.refs_1_), channel_id=1, source_target_pairs={{0,128},{128,0},{1,129},{129,1},{2,130},{130,2},{3,131},{131,3},{4... | collective-permute-start | bytes 1769480 | tf_op jit(solution)/shard_map/ppermute | solution.py:39
  50.0 27.6 %collective-permute-done.35 = bf16[32,1152]{1,0:T(8,128)(2,1)S(1)} collective-permute-done((bf16[32,1152]{1,0:T(8,128)(2,1)S(1)}, bf16[32,1152]{1,0:T(8,128)(2,1)S(1)}, u32[]{:S(2)}, u32[]{:S(2)}) %collective-permute-start.35) | collective-permute-done | bytes 73760 | tf_op jit(solution)/shard_map/ppermute | solution.py:30
  77.6 2.1 %collective-permute-start.36 = (bf16[32,1152]{1,0:T(8,128)(2,1)S(1)}, bf16[32,1152]{1,0:T(8,128)(2,1)S(1)}, u32[]{:S(2)}, u32[]{:S(2)}) collective-permute-start(bf16[32,1152]{1,0:T(8,128)(2,1)S(1)} %copy-done.4), channel_id=1, source_target_pairs={{0,24},{8,0},{16,8},{24,16},{1,25},{9,1},{17,9},{25,17},{2,26},{10... | collective-permute-start | bytes 221192 | tf_op jit(solution)/shard_map/ppermute | solution.py:30
  81.3 3.5 %collective-permute-start.8 = (bf16[128,1152]{1,0:T(8,128)(2,1)S(1)}, bf16[128,1152]{1,0:T(8,128)(2,1)S(1)}, u32[]{:S(2)}, u32[]{:S(2)}) collective-permute-start(bf16[128,1152]{1,0:T(8,128)(2,1)S(1)} %get-tuple-element.37), channel_id=1, source_target_pairs={{0,64},{32,96},{64,0},{96,32},{1,65},{33,97},{65,1},{97,33},{2,66}... | collective-permute-start | bytes 884744 | tf_op jit(solution)/shard_map/ppermute | solution.py:30
  86.8 4.0 %collective-permute-done.7.one = bf16[128,1152]{1,0:T(8,128)(2,1)S(1)} collective-permute-done((bf16[128,1152]{1,0:T(8,128)(2,1)S(1)}, bf16[128,1152]{1,0:T(8,128)(2,1)S(1)}, u32[]{:S(2)}, u32[]{:S(2)}) %collective-permute-start.7) | collective-permute-done | bytes 294944 | tf_op jit(solution)/shard_map/ppermute | solution.py:30
  92.7 5.0 %collective-permute-done.9.three = bf16[128,1152]{1,0:T(8,128)(2,1)S(1)} collective-permute-done((bf16[128,1152]{1,0:T(8,128)(2,1)S(1)}, bf16[128,1152]{1,0:T(8,128)(2,1)S(1)}, u32[]{:S(2)}, u32[]{:S(2)}) %collective-permute-start.9) | collective-permute-done | bytes 294944 | tf_op jit(solution)/shard_map/ppermute | solution.py:30
  99.6 2.7 %collective-permute-start.38 = (bf16[4,32,1152]{2,1,0:T(8,128)(2,1)S(1)}, bf16[4,32,1152]{2,1,0:T(8,128)(2,1)S(1)}, u32[]{:S(2)}, u32[]{:S(2)}) collective-permute-start(bf16[4,32,1152]{2,1,0:T(8,128)(2,1)S(1)} %pad_maximum_fusion.3.refs_0_), channel_id=1, source_target_pairs={{0,4},{2,6},{4,0},{6,2},{1,5},{3,7},{5,1},{7,3},{8,12},{10,14},{12... | collective-permute-start | bytes 884744 | tf_op jit(solution)/shard_map/ppermute | solution.py:30
  104.7 2.4 %collective-permute-start.24 = (bf16[128,1152]{1,0:T(8,128)(2,1)S(1)}, bf16[128,1152]{1,0:T(8,128)(2,1)S(1)}, u32[]{:S(2)}, u32[]{:S(2)}) collective-permute-start(bf16[128,1152]{1,0:T(8,128)(2,1)S(1)} %shard_map.85.p0.refs_4_), channel_id=1, source_target_pairs={{0,96},{32,0},{64,32},{96,64},{1,97},{33,1},{65,33},{97,65},{2,98}... | collective-permute-start | bytes 884744 | tf_op jit(solution)/shard_map/ppermute | solution.py:30
  108.0 9.1 %collective-permute-done.10.refs_2_ = bf16[128,1152]{1,0:T(8,128)(2,1)S(1)} collective-permute-done((bf16[128,1152]{1,0:T(8,128)(2,1)S(1)}, bf16[128,1152]{1,0:T(8,128)(2,1)S(1)}, u32[]{:S(2)}, u32[]{:S(2)}) %collective-permute-start.10) | collective-permute-done | bytes 294944 | tf_op jit(solution)/shard_map/ppermute | solution.py:39
  118.0 2.1 %collective-permute-start.13 = (bf16[128,1152]{1,0:T(8,128)(2,1)S(1)}, bf16[128,1152]{1,0:T(8,128)(2,1)S(1)}, u32[]{:S(2)}, u32[]{:S(2)}) collective-permute-start(bf16[128,1152]{1,0:T(8,128)(2,1)S(1)} %shard_map.80.p0.refs_0_), channel_id=1, source_target_pairs={{0,96},{32,0},{64,32},{96,64},{1,97},{33,1},{65,33},{97,65},{2,98}... | collective-permute-start | bytes 884744 | tf_op jit(solution)/shard_map/ppermute | solution.py:30
  121.4 2.5 %collective-permute-start.15 = (bf16[128,1152]{1,0:T(8,128)(2,1)S(1)}, bf16[128,1152]{1,0:T(8,128)(2,1)S(1)}, u32[]{:S(2)}, u32[]{:S(2)}) collective-permute-start(bf16[128,1152]{1,0:T(8,128)(2,1)S(1)} %shard_map.80.p0.refs_0_), channel_id=1, source_target_pairs={{0,32},{32,64},{64,96},{96,0},{1,33},{33,65},{65,97},{97,1},{2,34}... | collective-permute-start | bytes 884744 | tf_op jit(solution)/shard_map/ppermute | solution.py:30
  124.8 2.1 %collective-permute-done.26.p3.refs_7_ = bf16[128,1152]{1,0:T(8,128)(2,1)S(1)} collective-permute-done((bf16[128,1152]{1,0:T(8,128)(2,1)S(1)}, bf16[128,1152]{1,0:T(8,128)(2,1)S(1)}, u32[]{:S(2)}, u32[]{:S(2)}) %collective-permute-start.26) | collective-permute-done | bytes 294944 | tf_op jit(solution)/shard_map/ppermute | solution.py:30
  126.9 2.9 %shard_map.86 = (bf16[4,2,32,1152]{3,2,1,0:T(8,128)(2,1)S(1)}, f32[4,2,32,1152]{3,2,1,0:T(8,128)S(1)}) custom-call(s32[5]{0:T(128)S(1)} %stack.64.where.refs_0_, bf16[128,1152]{1,0:T(8,128)(2,1)S(1)} %shard_map.85.p0.refs_4_, bf16[128,1152]{1,0:T(8,128)(2,1)S(1)} %collective-permute-done.24.p1.refs_5_, ...), custom_call_target="tpu_custom_call" | custom-call | flops 1358954496 | bytes 3833856 | tf_op jit(solution)/shard_map/pallas_call | solution.py:58
  130.2 4.2 %collective-permute-done.14.p2.refs_2_ = bf16[128,1152]{1,0:T(8,128)(2,1)S(1)} collective-permute-done((bf16[128,1152]{1,0:T(8,128)(2,1)S(1)}, bf16[128,1152]{1,0:T(8,128)(2,1)S(1)}, u32[]{:S(2)}, u32[]{:S(2)}) %collective-permute-start.14) | collective-permute-done | bytes 294944 | tf_op jit(solution)/shard_map/ppermute | solution.py:30
  134.3 4.3 %collective-permute-done.15.p3.refs_3_ = bf16[128,1152]{1,0:T(8,128)(2,1)S(1)} collective-permute-done((bf16[128,1152]{1,0:T(8,128)(2,1)S(1)}, bf16[128,1152]{1,0:T(8,128)(2,1)S(1)}, u32[]{:S(2)}, u32[]{:S(2)}) %collective-permute-start.15) | collective-permute-done | bytes 294944 | tf_op jit(solution)/shard_map/ppermute | solution.py:30
  138.6 2.9 %shard_map.81 = (bf16[4,2,32,1152]{3,2,1,0:T(8,128)(2,1)S(1)}, f32[4,2,32,1152]{3,2,1,0:T(8,128)S(1)}) custom-call(s32[5]{0:T(128)S(1)} %stack.64.where.refs_0_, bf16[128,1152]{1,0:T(8,128)(2,1)S(1)} %shard_map.80.p0.refs_0_, bf16[128,1152]{1,0:T(8,128)(2,1)S(1)} %collective-permute-done.13.p1.refs_1_, ...), custom_call_target="tpu_custom_call" | custom-call | flops 1358954496 | bytes 3833856 | tf_op jit(solution)/shard_map/pallas_call | solution.py:58
  142.7 2.6 %collective-permute-start.41 = (bf16[2,128,1152]{2,1,0:T(8,128)(2,1)S(1)}, bf16[2,128,1152]{2,1,0:T(8,128)(2,1)S(1)}, u32[]{:S(2)}, u32[]{:S(2)}) collective-permute-start(bf16[2,128,1152]{2,1,0:T(8,128)(2,1)S(1)} %collective-permute-done.12.refs_4_.refs_1_), channel_id=1, source_target_pairs={{0,64},{32,96},{64,0},{96,32},{1,65},{33,97},{65,1},{97,33},{2,66}... | collective-permute-start | bytes 1769480 | tf_op jit(solution)/shard_map/ppermute | solution.py:35
  146.8 2.4 %collective-permute-start.29 = (bf16[2,32,1152]{2,1,0:T(8,128)(2,1)S(1)}, bf16[2,32,1152]{2,1,0:T(8,128)(2,1)S(1)}, u32[]{:S(2)}, u32[]{:S(2)}) collective-permute-start(bf16[2,32,1152]{2,1,0:T(8,128)(2,1)S(1)} %get-tuple-element.57), channel_id=1, source_target_pairs={{0,4},{2,6},{4,0},{6,2},{1,5},{3,7},{5,1},{7,3},{8,12},{10,14},{12... | collective-permute-start | bytes 442376 | tf_op jit(solution)/shard_map/ppermute | solution.py:30
  149.4 10.1 %collective-permute-done.42.refs_2_ = bf16[2,128,1152]{2,1,0:T(8,128)(2,1)S(1)} collective-permute-done((bf16[2,128,1152]{2,1,0:T(8,128)(2,1)S(1)}, bf16[2,128,1152]{2,1,0:T(8,128)(2,1)S(1)}, u32[]{:S(2)}, u32[]{:S(2)}) %collective-permute-start.42) | collective-permute-done | bytes 589856 | tf_op jit(solution)/shard_map/ppermute | solution.py:35
  159.5 2.3 %collective-permute-start.30 = (bf16[2,32,1152]{2,1,0:T(8,128)(2,1)S(1)}, bf16[2,32,1152]{2,1,0:T(8,128)(2,1)S(1)}, u32[]{:S(2)}, u32[]{:S(2)}) collective-permute-start(bf16[2,32,1152]{2,1,0:T(8,128)(2,1)S(1)} %get-tuple-element.58), channel_id=1, source_target_pairs={{0,6},{2,0},{4,2},{6,4},{1,7},{3,1},{5,3},{7,5},{8,14},{10,8},{12,... | collective-permute-start | bytes 442376 | tf_op jit(solution)/shard_map/ppermute | solution.py:30
  161.7 9.8 %collective-permute-done.41.refs_2_ = bf16[2,128,1152]{2,1,0:T(8,128)(2,1)S(1)} collective-permute-done((bf16[2,128,1152]{2,1,0:T(8,128)(2,1)S(1)}, bf16[2,128,1152]{2,1,0:T(8,128)(2,1)S(1)}, u32[]{:S(2)}, u32[]{:S(2)}) %collective-permute-start.41) | collective-permute-done | bytes 589856 | tf_op jit(solution)/shard_map/ppermute | solution.py:35
  172.9 2.4 %collective-permute-start.18 = (bf16[2,32,1152]{2,1,0:T(8,128)(2,1)S(1)}, bf16[2,32,1152]{2,1,0:T(8,128)(2,1)S(1)}, u32[]{:S(2)}, u32[]{:S(2)}) collective-permute-start(bf16[2,32,1152]{2,1,0:T(8,128)(2,1)S(1)} %get-tuple-element.45), channel_id=1, source_target_pairs={{0,4},{2,6},{4,0},{6,2},{1,5},{3,7},{5,1},{7,3},{8,12},{10,14},{12... | collective-permute-start | bytes 442376 | tf_op jit(solution)/shard_map/ppermute | solution.py:30
  176.9 3.3 %shard_map.91.refs_5_ = f32[1152,1152]{1,0:T(8,128)S(1)} custom-call(s32[5]{0:T(128)S(1)} %stack.64.where.refs_0_, bf16[2,128,1152]{2,1,0:T(8,128)(2,1)S(1)} %pad_maximum_fusion.refs_1_, bf16[2,128,1152]{2,1,0:T(8,128)(2,1)S(1)} %collective-permute-done.42.refs_2_, bf16[2,4,2,32,1152]{4,3,2,1,0:T(8,128)(2,1)S(1)} %shard_map.76.half.refs_3_, ...), custom_call_target="tpu_custom_call" | custom-call | flops 1358954496 | bytes 3538944 | tf_op jit(solution)/shard_map/pallas_call | solution.py:58
  180.1 4.2 %shard_map.92 = bf16[1152,1152]{1,0:T(8,128)(2,1)} custom-call(s32[5]{0:T(128)S(1)} %stack.64.where.refs_0_, bf16[2,128,1152]{2,1,0:T(8,128)(2,1)S(1)} %collective-permute-done.12.refs_4_.refs_1_, bf16[2,128,1152]{2,1,0:T(8,128)(2,1)S(1)} %collective-permute-done.41.refs_2_, bf16[2,4,2,32,1152]{4,3,2,1,0:T(8,128)(2,1)S(1)} %shard_map.76.half.refs_3_, ...), custom_call_target="tpu_custom_call" | custom-call | flops 1358954496 | bytes 6193152 | tf_op jit(solution)/shard_map/pallas_call | solution.py:58
  186.0 3.1 %collective-permute-start.33 = (bf16[32,1152]{1,0:T(8,128)(2,1)S(1)}, bf16[32,1152]{1,0:T(8,128)(2,1)S(1)}, u32[]{:S(2)}, u32[]{:S(2)}) collective-permute-start(bf16[32,1152]{1,0:T(8,128)(2,1)S(1)} %get-tuple-element.62), channel_id=1, source_target_pairs={{0,24},{8,0},{16,8},{24,16},{1,25},{9,1},{17,9},{25,17},{2,26},{10... | collective-permute-start | bytes 221192 | tf_op jit(solution)/shard_map/ppermute | solution.py:30
  189.1 4.8 %shard_map.90 = bf16[1152,1152]{1,0:T(8,128)(2,1)} custom-call(bf16[128,1152]{1,0:T(8,128)(2,1)S(1)} %shard_map.80.p0.refs_0_, bf16[128,1152]{1,0:T(8,128)(2,1)S(1)} %collective-permute-done.13.p1.refs_1_, bf16[128,1152]{1,0:T(8,128)(2,1)S(1)} %collective-permute-done.14.p2.refs_2_, bf16[128,1152]{1,0:T(8,128)(2,1)S(1)} %collective-permute-done.15.p3.refs_3_, ...), custom_call_target="tpu_custom_call" | custom-call | flops 2717908992 | bytes 4718592 | tf_op jit(solution)/shard_map/pallas_call | solution.py:58
  (88 shorter events, 43.3 us)
Async XLA Ops:
  12.4 10.2 %collective-permute-start.3 = (bf16[4,32,1152]{2,1,0:T(8,128)(2,1)S(1)}, bf16[4,32,1152]{2,1,0:T(8,128)(2,1)S(1)}, u32[]{:S(2)}, u32[]{:S(2)}) collective-permute-start(bf16[4,32,1152]{2,1,0:T(8,128)(2,1)S(1)} %pad_maximum_fusion.1.refs_0_), channel_id=1, source_target_pairs={{0,2},{2,4},{4,6},{6,0},{1,3},{3,5},{5,7},{7,1},{8,10},{10,12},{12... | collective-permute-start | bytes 884744 | tf_op jit(solution)/shard_map/ppermute | solution.py:30
  14.0 15.4 %collective-permute-start.4 = (bf16[4,32,1152]{2,1,0:T(8,128)(2,1)S(1)}, bf16[4,32,1152]{2,1,0:T(8,128)(2,1)S(1)}, u32[]{:S(2)}, u32[]{:S(2)}) collective-permute-start(bf16[4,32,1152]{2,1,0:T(8,128)(2,1)S(1)} %pad_maximum_fusion.1.refs_0_), channel_id=1, source_target_pairs={{0,4},{2,6},{4,0},{6,2},{1,5},{3,7},{5,1},{7,3},{8,12},{10,14},{12... | collective-permute-start | bytes 884744 | tf_op jit(solution)/shard_map/ppermute | solution.py:30
  16.7 12.7 %collective-permute-start.5 = (bf16[4,32,1152]{2,1,0:T(8,128)(2,1)S(1)}, bf16[4,32,1152]{2,1,0:T(8,128)(2,1)S(1)}, u32[]{:S(2)}, u32[]{:S(2)}) collective-permute-start(bf16[4,32,1152]{2,1,0:T(8,128)(2,1)S(1)} %pad_maximum_fusion.1.refs_0_), channel_id=1, source_target_pairs={{0,6},{2,0},{4,2},{6,4},{1,7},{3,1},{5,3},{7,5},{8,14},{10,8},{12,... | collective-permute-start | bytes 884744 | tf_op jit(solution)/shard_map/ppermute | solution.py:30
  30.4 12.9 %collective-permute-start.11 = (bf16[128,1152]{1,0:T(8,128)(2,1)S(1)}, bf16[128,1152]{1,0:T(8,128)(2,1)S(1)}, u32[]{:S(2)}, u32[]{:S(2)}) collective-permute-start(bf16[128,1152]{1,0:T(8,128)(2,1)S(1)} %bitcast.33), channel_id=1, source_target_pairs={{0,32},{32,0},{64,96},{96,64},{1,33},{33,1},{65,97},{97,65},{2,34}... | collective-permute-start | bytes 884744 | tf_op jit(solution)/shard_map/ppermute | solution.py:35
  31.2 18.0 %collective-permute-start.34 = (bf16[32,1152]{1,0:T(8,128)(2,1)S(1)}, bf16[32,1152]{1,0:T(8,128)(2,1)S(1)}, u32[]{:S(2)}, u32[]{:S(2)}) collective-permute-start(bf16[32,1152]{1,0:T(8,128)(2,1)S(1)} %copy-done.4), channel_id=1, source_target_pairs={{0,8},{8,16},{16,24},{24,0},{1,9},{9,17},{17,25},{25,1},{2,10},{10... | collective-permute-start | bytes 221192 | tf_op jit(solution)/shard_map/ppermute | solution.py:30
  38.1 42.7 %collective-permute-start.20 = (bf16[128,1152]{1,0:T(8,128)(2,1)S(1)}, bf16[128,1152]{1,0:T(8,128)(2,1)S(1)}, u32[]{:S(2)}, u32[]{:S(2)}) collective-permute-start(bf16[128,1152]{1,0:T(8,128)(2,1)S(1)} %get-tuple-element.48), channel_id=1, source_target_pairs={{0,32},{32,64},{64,96},{96,0},{1,33},{33,65},{65,97},{97,1},{2,34}... | collective-permute-start | bytes 884744 | tf_op jit(solution)/shard_map/ppermute | solution.py:30
  40.4 40.9 %collective-permute-start.21 = (bf16[128,1152]{1,0:T(8,128)(2,1)S(1)}, bf16[128,1152]{1,0:T(8,128)(2,1)S(1)}, u32[]{:S(2)}, u32[]{:S(2)}) collective-permute-start(bf16[128,1152]{1,0:T(8,128)(2,1)S(1)} %get-tuple-element.49), channel_id=1, source_target_pairs={{0,64},{32,96},{64,0},{96,32},{1,65},{33,97},{65,1},{97,33},{2,66}... | collective-permute-start | bytes 884744 | tf_op jit(solution)/shard_map/ppermute | solution.py:30
  41.7 43.1 %collective-permute-start.22 = (bf16[128,1152]{1,0:T(8,128)(2,1)S(1)}, bf16[128,1152]{1,0:T(8,128)(2,1)S(1)}, u32[]{:S(2)}, u32[]{:S(2)}) collective-permute-start(bf16[128,1152]{1,0:T(8,128)(2,1)S(1)} %get-tuple-element.50), channel_id=1, source_target_pairs={{0,96},{32,0},{64,32},{96,64},{1,97},{33,1},{65,33},{97,65},{2,98}... | collective-permute-start | bytes 884744 | tf_op jit(solution)/shard_map/ppermute | solution.py:30
  43.3 58.9 %collective-permute-start.12 = (bf16[2,128,1152]{2,1,0:T(8,128)(2,1)S(1)}, bf16[2,128,1152]{2,1,0:T(8,128)(2,1)S(1)}, u32[]{:S(2)}, u32[]{:S(2)}) collective-permute-start(bf16[2,128,1152]{2,1,0:T(8,128)(2,1)S(1)} %pad_maximum_fusion.refs_1_), channel_id=1, source_target_pairs={{0,128},{128,0},{1,129},{129,1},{2,130},{130,2},{3,131},{131,3},{4... | collective-permute-start | bytes 1769480 | tf_op jit(solution)/shard_map/ppermute | solution.py:39
  49.2 28.4 %collective-permute-start.35 = (bf16[32,1152]{1,0:T(8,128)(2,1)S(1)}, bf16[32,1152]{1,0:T(8,128)(2,1)S(1)}, u32[]{:S(2)}, u32[]{:S(2)}) collective-permute-start(bf16[32,1152]{1,0:T(8,128)(2,1)S(1)} %copy-done.4), channel_id=1, source_target_pairs={{0,16},{8,24},{16,0},{24,8},{1,17},{9,25},{17,1},{25,9},{2,18},{10... | collective-permute-start | bytes 221192 | tf_op jit(solution)/shard_map/ppermute | solution.py:30
  80.8 10.0 %collective-permute-start.7 = (bf16[128,1152]{1,0:T(8,128)(2,1)S(1)}, bf16[128,1152]{1,0:T(8,128)(2,1)S(1)}, u32[]{:S(2)}, u32[]{:S(2)}) collective-permute-start(bf16[128,1152]{1,0:T(8,128)(2,1)S(1)} %get-tuple-element.36), channel_id=1, source_target_pairs={{0,32},{32,64},{64,96},{96,0},{1,33},{33,65},{65,97},{97,1},{2,34}... | collective-permute-start | bytes 884744 | tf_op jit(solution)/shard_map/ppermute | solution.py:30
  81.3 11.4 %collective-permute-start.8 = (bf16[128,1152]{1,0:T(8,128)(2,1)S(1)}, bf16[128,1152]{1,0:T(8,128)(2,1)S(1)}, u32[]{:S(2)}, u32[]{:S(2)}) collective-permute-start(bf16[128,1152]{1,0:T(8,128)(2,1)S(1)} %get-tuple-element.37), channel_id=1, source_target_pairs={{0,64},{32,96},{64,0},{96,32},{1,65},{33,97},{65,1},{97,33},{2,66}... | collective-permute-start | bytes 884744 | tf_op jit(solution)/shard_map/ppermute | solution.py:30
  84.8 12.9 %collective-permute-start.9 = (bf16[128,1152]{1,0:T(8,128)(2,1)S(1)}, bf16[128,1152]{1,0:T(8,128)(2,1)S(1)}, u32[]{:S(2)}, u32[]{:S(2)}) collective-permute-start(bf16[128,1152]{1,0:T(8,128)(2,1)S(1)} %get-tuple-element.38), channel_id=1, source_target_pairs={{0,96},{32,0},{64,32},{96,64},{1,97},{33,1},{65,33},{97,65},{2,98}... | collective-permute-start | bytes 884744 | tf_op jit(solution)/shard_map/ppermute | solution.py:30
  85.0 18.8 %collective-permute-start.23 = (bf16[128,1152]{1,0:T(8,128)(2,1)S(1)}, bf16[128,1152]{1,0:T(8,128)(2,1)S(1)}, u32[]{:S(2)}, u32[]{:S(2)}) collective-permute-start(bf16[128,1152]{1,0:T(8,128)(2,1)S(1)} %get-tuple-element.52), channel_id=1, source_target_pairs={{0,128},{128,0},{1,129},{129,1},{2,130},{130,2},{3,131},{131,3},{4... | collective-permute-start | bytes 884744 | tf_op jit(solution)/shard_map/ppermute | solution.py:39
  90.7 16.4 %collective-permute-start.37 = (bf16[4,32,1152]{2,1,0:T(8,128)(2,1)S(1)}, bf16[4,32,1152]{2,1,0:T(8,128)(2,1)S(1)}, u32[]{:S(2)}, u32[]{:S(2)}) collective-permute-start(bf16[4,32,1152]{2,1,0:T(8,128)(2,1)S(1)} %pad_maximum_fusion.3.refs_0_), channel_id=1, source_target_pairs={{0,2},{2,4},{4,6},{6,0},{1,3},{3,5},{5,7},{7,1},{8,10},{10,12},{12... | collective-permute-start | bytes 884744 | tf_op jit(solution)/shard_map/ppermute | solution.py:30
  97.9 19.1 %collective-permute-start.10 = (bf16[128,1152]{1,0:T(8,128)(2,1)S(1)}, bf16[128,1152]{1,0:T(8,128)(2,1)S(1)}, u32[]{:S(2)}, u32[]{:S(2)}) collective-permute-start(bf16[128,1152]{1,0:T(8,128)(2,1)S(1)} %get-tuple-element.40), channel_id=1, source_target_pairs={{0,128},{128,0},{1,129},{129,1},{2,130},{130,2},{3,131},{131,3},{4... | collective-permute-start | bytes 884744 | tf_op jit(solution)/shard_map/ppermute | solution.py:39
  99.6 18.4 %collective-permute-start.38 = (bf16[4,32,1152]{2,1,0:T(8,128)(2,1)S(1)}, bf16[4,32,1152]{2,1,0:T(8,128)(2,1)S(1)}, u32[]{:S(2)}, u32[]{:S(2)}) collective-permute-start(bf16[4,32,1152]{2,1,0:T(8,128)(2,1)S(1)} %pad_maximum_fusion.3.refs_0_), channel_id=1, source_target_pairs={{0,4},{2,6},{4,0},{6,2},{1,5},{3,7},{5,1},{7,3},{8,12},{10,14},{12... | collective-permute-start | bytes 884744 | tf_op jit(solution)/shard_map/ppermute | solution.py:30
  102.3 17.8 %collective-permute-start.39 = (bf16[4,32,1152]{2,1,0:T(8,128)(2,1)S(1)}, bf16[4,32,1152]{2,1,0:T(8,128)(2,1)S(1)}, u32[]{:S(2)}, u32[]{:S(2)}) collective-permute-start(bf16[4,32,1152]{2,1,0:T(8,128)(2,1)S(1)} %pad_maximum_fusion.3.refs_0_), channel_id=1, source_target_pairs={{0,6},{2,0},{4,2},{6,4},{1,7},{3,1},{5,3},{7,5},{8,14},{10,8},{12,... | collective-permute-start | bytes 884744 | tf_op jit(solution)/shard_map/ppermute | solution.py:30
  104.7 16.7 %collective-permute-start.24 = (bf16[128,1152]{1,0:T(8,128)(2,1)S(1)}, bf16[128,1152]{1,0:T(8,128)(2,1)S(1)}, u32[]{:S(2)}, u32[]{:S(2)}) collective-permute-start(bf16[128,1152]{1,0:T(8,128)(2,1)S(1)} %shard_map.85.p0.refs_4_), channel_id=1, source_target_pairs={{0,96},{32,0},{64,32},{96,64},{1,97},{33,1},{65,33},{97,65},{2,98}... | collective-permute-start | bytes 884744 | tf_op jit(solution)/shard_map/ppermute | solution.py:30
  107.1 17.6 %collective-permute-start.25 = (bf16[128,1152]{1,0:T(8,128)(2,1)S(1)}, bf16[128,1152]{1,0:T(8,128)(2,1)S(1)}, u32[]{:S(2)}, u32[]{:S(2)}) collective-permute-start(bf16[128,1152]{1,0:T(8,128)(2,1)S(1)} %shard_map.85.p0.refs_4_), channel_id=1, source_target_pairs={{0,64},{32,96},{64,0},{96,32},{1,65},{33,97},{65,1},{97,33},{2,66}... | collective-permute-start | bytes 884744 | tf_op jit(solution)/shard_map/ppermute | solution.py:30
  118.0 12.2 %collective-permute-start.13 = (bf16[128,1152]{1,0:T(8,128)(2,1)S(1)}, bf16[128,1152]{1,0:T(8,128)(2,1)S(1)}, u32[]{:S(2)}, u32[]{:S(2)}) collective-permute-start(bf16[128,1152]{1,0:T(8,128)(2,1)S(1)} %shard_map.80.p0.refs_0_), channel_id=1, source_target_pairs={{0,96},{32,0},{64,32},{96,64},{1,97},{33,1},{65,33},{97,65},{2,98}... | collective-permute-start | bytes 884744 | tf_op jit(solution)/shard_map/ppermute | solution.py:30
  120.1 14.2 %collective-permute-start.14 = (bf16[128,1152]{1,0:T(8,128)(2,1)S(1)}, bf16[128,1152]{1,0:T(8,128)(2,1)S(1)}, u32[]{:S(2)}, u32[]{:S(2)}) collective-permute-start(bf16[128,1152]{1,0:T(8,128)(2,1)S(1)} %shard_map.80.p0.refs_0_), channel_id=1, source_target_pairs={{0,64},{32,96},{64,0},{96,32},{1,65},{33,97},{65,1},{97,33},{2,66}... | collective-permute-start | bytes 884744 | tf_op jit(solution)/shard_map/ppermute | solution.py:30
  121.4 17.2 %collective-permute-start.15 = (bf16[128,1152]{1,0:T(8,128)(2,1)S(1)}, bf16[128,1152]{1,0:T(8,128)(2,1)S(1)}, u32[]{:S(2)}, u32[]{:S(2)}) collective-permute-start(bf16[128,1152]{1,0:T(8,128)(2,1)S(1)} %shard_map.80.p0.refs_0_), channel_id=1, source_target_pairs={{0,32},{32,64},{64,96},{96,0},{1,33},{33,65},{65,97},{97,1},{2,34}... | collective-permute-start | bytes 884744 | tf_op jit(solution)/shard_map/ppermute | solution.py:30
  124.7 64.4 %collective-permute-start.40 = (bf16[2,4,2,32,1152]{4,3,2,1,0:T(8,128)(2,1)S(1)}, bf16[2,4,2,32,1152]{4,3,2,1,0:T(8,128)(2,1)S(1)}, u32[]{:S(2)}, u32[]{:S(2)}) collective-permute-start(bf16[2,4,2,32,1152]{4,3,2,1,0:T(8,128)(2,1)S(1)} %shard_map.89.refs_8_), channel_id=1, source_target_pairs={{0,1},{1,0},{2,3},{3,2},{4,5},{5,4},{6,7},{7,6},{8,9},{9,8},{10,11... | collective-permute-start | bytes 3538952 | tf_op jit(solution)/shard_map/ppermute | solution.py:39
  129.8 15.4 %collective-permute-start.27 = (bf16[4,2,32,1152]{3,2,1,0:T(8,128)(2,1)S(1)}, bf16[4,2,32,1152]{3,2,1,0:T(8,128)(2,1)S(1)}, u32[]{:S(2)}, u32[]{:S(2)}) collective-permute-start(bf16[4,2,32,1152]{3,2,1,0:T(8,128)(2,1)S(1)} %get-tuple-element.54), channel_id=1, source_target_pairs={{0,1},{1,0},{2,3},{3,2},{4,5},{5,4},{6,7},{7,6},{8,9},{9,8},{10,11... | collective-permute-start | bytes 1769480 | tf_op jit(solution)/shard_map/ppermute | solution.py:39
  141.7 17.8 %collective-permute-start.42 = (bf16[2,128,1152]{2,1,0:T(8,128)(2,1)S(1)}, bf16[2,128,1152]{2,1,0:T(8,128)(2,1)S(1)}, u32[]{:S(2)}, u32[]{:S(2)}) collective-permute-start(bf16[2,128,1152]{2,1,0:T(8,128)(2,1)S(1)} %pad_maximum_fusion.refs_1_), channel_id=1, source_target_pairs={{0,64},{32,96},{64,0},{96,32},{1,65},{33,97},{65,1},{97,33},{2,66}... | collective-permute-start | bytes 1769480 | tf_op jit(solution)/shard_map/ppermute | solution.py:35
  142.7 28.8 %collective-permute-start.41 = (bf16[2,128,1152]{2,1,0:T(8,128)(2,1)S(1)}, bf16[2,128,1152]{2,1,0:T(8,128)(2,1)S(1)}, u32[]{:S(2)}, u32[]{:S(2)}) collective-permute-start(bf16[2,128,1152]{2,1,0:T(8,128)(2,1)S(1)} %collective-permute-done.12.refs_4_.refs_1_), channel_id=1, source_target_pairs={{0,64},{32,96},{64,0},{96,32},{1,65},{33,97},{65,1},{97,33},{2,66}... | collective-permute-start | bytes 1769480 | tf_op jit(solution)/shard_map/ppermute | solution.py:35
  145.4 27.5 %collective-permute-start.28 = (bf16[2,32,1152]{2,1,0:T(8,128)(2,1)S(1)}, bf16[2,32,1152]{2,1,0:T(8,128)(2,1)S(1)}, u32[]{:S(2)}, u32[]{:S(2)}) collective-permute-start(bf16[2,32,1152]{2,1,0:T(8,128)(2,1)S(1)} %get-tuple-element.56), channel_id=1, source_target_pairs={{0,2},{2,4},{4,6},{6,0},{1,3},{3,5},{5,7},{7,1},{8,10},{10,12},{12... | collective-permute-start | bytes 442376 | tf_op jit(solution)/shard_map/ppermute | solution.py:30
  146.8 28.5 %collective-permute-start.29 = (bf16[2,32,1152]{2,1,0:T(8,128)(2,1)S(1)}, bf16[2,32,1152]{2,1,0:T(8,128)(2,1)S(1)}, u32[]{:S(2)}, u32[]{:S(2)}) collective-permute-start(bf16[2,32,1152]{2,1,0:T(8,128)(2,1)S(1)} %get-tuple-element.57), channel_id=1, source_target_pairs={{0,4},{2,6},{4,0},{6,2},{1,5},{3,7},{5,1},{7,3},{8,12},{10,14},{12... | collective-permute-start | bytes 442376 | tf_op jit(solution)/shard_map/ppermute | solution.py:30
  159.5 24.9 %collective-permute-start.30 = (bf16[2,32,1152]{2,1,0:T(8,128)(2,1)S(1)}, bf16[2,32,1152]{2,1,0:T(8,128)(2,1)S(1)}, u32[]{:S(2)}, u32[]{:S(2)}) collective-permute-start(bf16[2,32,1152]{2,1,0:T(8,128)(2,1)S(1)} %get-tuple-element.58), channel_id=1, source_target_pairs={{0,6},{2,0},{4,2},{6,4},{1,7},{3,1},{5,3},{7,5},{8,14},{10,8},{12,... | collective-permute-start | bytes 442376 | tf_op jit(solution)/shard_map/ppermute | solution.py:30
  171.5 12.9 %collective-permute-start.17 = (bf16[2,32,1152]{2,1,0:T(8,128)(2,1)S(1)}, bf16[2,32,1152]{2,1,0:T(8,128)(2,1)S(1)}, u32[]{:S(2)}, u32[]{:S(2)}) collective-permute-start(bf16[2,32,1152]{2,1,0:T(8,128)(2,1)S(1)} %get-tuple-element.44), channel_id=1, source_target_pairs={{0,2},{2,4},{4,6},{6,0},{1,3},{3,5},{5,7},{7,1},{8,10},{10,12},{12... | collective-permute-start | bytes 442376 | tf_op jit(solution)/shard_map/ppermute | solution.py:30
  172.9 11.5 %collective-permute-start.18 = (bf16[2,32,1152]{2,1,0:T(8,128)(2,1)S(1)}, bf16[2,32,1152]{2,1,0:T(8,128)(2,1)S(1)}, u32[]{:S(2)}, u32[]{:S(2)}) collective-permute-start(bf16[2,32,1152]{2,1,0:T(8,128)(2,1)S(1)} %get-tuple-element.45), channel_id=1, source_target_pairs={{0,4},{2,6},{4,0},{6,2},{1,5},{3,7},{5,1},{7,3},{8,12},{10,14},{12... | collective-permute-start | bytes 442376 | tf_op jit(solution)/shard_map/ppermute | solution.py:30
  (16 other events, 153.3 us)
